TPU v7x, 32 devices: a whole 2x2x4 slice. The times are simulated.
32 devices in a mesh: heads: 8 (over z, x), ctx: 4 (over y, core).
Axes of the slice: x: 2, y: 2, z: 4, core: 2. Of those that a mesh axis runs over, the one named last changes fastest.
Arguments:
- queries: bfloat16 [4096, 4096], P(('ctx', 'heads')), may hold values from -500 to 500
- keys_in: bfloat16 [4096, 512], P(('ctx', 'heads')), may hold values from -7 to 7
- values_in: bfloat16 [4096, 512], P(('ctx', 'heads')), may hold values from -6 to 6
- cotangent: bfloat16 [4096, 4096], P(('ctx', 'heads')), may hold values from -6 to 6
- rand_blocks: int32 [32, 1], replicated, may hold values from 0 to 31, as said below
- glob_blocks: int32 [2], replicated, may hold values from 0 to 31
Outputs:
- attn_out: bfloat16 [4096, 4096], P(('ctx', 'heads'))
- grad_query: bfloat16 [4096, 4096], P(('ctx', 'heads'))
- grad_keys: bfloat16 [4096, 512], P(('ctx', 'heads'))
- grad_values: bfloat16 [4096, 512], P(('ctx', 'heads'))
Inputs may be any that keep to these rules, and one draw needn't show every extreme that they name: `rand_blocks`: of the 8 entries in the rows of one segment's query blocks (rows c*8 to (c+1)*8 - 1), exactly 2 name blocks of each segment (blocks s*8 to (s+1)*8 - 1).
All inputs are finite; a program needn't handle non-finite values.
Results may differ from a plain program's by a relative error of at most 0.0075.
Values may be sent and summed in bfloat16 or wider, within the bound.
No kernel may reach another device: no remote copies, remote signals or barrier semaphores. Data moves between devices by JAX's collectives and lax.ppermute only.
A program may use at most 128 MiB of HBM per device.

v0:
```python
import math

import jax
import jax.numpy as jnp
from jax import lax
from jax.sharding import PartitionSpec as P

HD = 128
H = 32
KVH = 4
BLK = 128
NG = 2
NR = 1


NEG_FILL = -1e30


def extended_2(value, sides, width):
    for axis, dim in sides:
        size, length = (lax.axis_size(axis), value.shape[dim])
        up = [(i, (i + 1) % size) for i in range(size - 1)]
        down = [(j, i) for i, j in up]
        last = lax.slice_in_dim(value, length - width, length, axis=dim)
        initial = lax.slice_in_dim(value, 0, width, axis=dim)
        before = lax.ppermute(last, axis, up)
        after = lax.ppermute(initial, axis, down)
        value = jnp.concatenate([before, value, after], axis=dim)
    return value


def broadcast(value, axis, root):
    mine = lax.axis_index(axis) == root
    return lax.psum(jnp.where(mine, value, jnp.zeros_like(value)), axis)


def shifted(value, axis, steps):
    count = lax.axis_size(axis)
    initial, last = (max(0, -steps), min(count, count - steps))
    return lax.ppermute(value, axis, [(source, source + steps) for source in range(initial, last)])


def shards(queries, keys_in, values_in, cotangent, rand_blocks, glob_blocks):
    ctx_count = lax.axis_size("ctx")
    ctx_rank = lax.axis_index("ctx")
    local_tokens = queries.shape[0]
    group_size = H // KVH
    scale_factor = 1.0 / math.sqrt(HD)
    per_step = 4
    key_slots = 3 + NG + NR
    width_pair = 2 * HD
    query_wide = jnp.transpose(queries.reshape(local_tokens, H, HD), (1, 0, 2))
    dout_wide = jnp.transpose(cotangent.reshape(local_tokens, H, HD), (1, 0, 2))
    keys_group = jnp.transpose(keys_in.reshape(local_tokens, KVH, HD), (1, 0, 2))
    values_group = jnp.transpose(values_in.reshape(local_tokens, KVH, HD), (1, 0, 2))
    pairs_group = jnp.concatenate([keys_group, values_group], axis=2)
    pairs_wide = jnp.repeat(pairs_group, group_size, axis=0)
    query_heads, pairs_heads, dout_heads = (
        lax.all_to_all(query_wide, "heads", split_axis=0, concat_axis=1, tiled=True),
        lax.all_to_all(pairs_wide, "heads", split_axis=0, concat_axis=1, tiled=True),
        lax.all_to_all(dout_wide, "heads", split_axis=0, concat_axis=1, tiled=True),
    )
    local_heads = query_heads.shape[0]
    seg_rows = query_heads.shape[1]
    block_local = seg_rows // BLK
    extended = extended_2(pairs_heads, (("ctx", 1),), BLK)
    pair_blocks = pairs_heads.reshape(local_heads, block_local, BLK, width_pair)
    glob_owner = glob_blocks // block_local
    glob_local = glob_blocks % block_local
    fetched = []
    for glob_slot in range(NG):
        glob_piece = lax.dynamic_index_in_dim(pair_blocks, glob_local[glob_slot], 1, keepdims=False)
        fetched.append(broadcast(glob_piece, "ctx", glob_owner[glob_slot]))
    global_pairs = jnp.stack(fetched, axis=1)
    request_count = block_local * NR
    capacity = request_count // ctx_count
    requests = rand_blocks.reshape(ctx_count, request_count)
    req_owner = requests // block_local
    req_local = requests % block_local
    positions = jnp.arange(request_count, dtype=jnp.int32)
    earlier = positions[:, None] > positions[None, :]
    same_owner = req_owner[:, :, None] == req_owner[:, None, :]
    req_rank = jnp.sum((same_owner & earlier[None]).astype(jnp.int32), axis=2)
    rank_ids = jnp.arange(capacity, dtype=jnp.int32)
    chosen = (req_owner == ctx_rank)[:, :, None] & (req_rank[:, :, None] == rank_ids[None, None, :])
    send_local = jnp.sum(jnp.where(chosen, req_local[:, :, None], 0), axis=1)
    outgoing = pair_blocks[:, send_local.reshape(-1)].reshape(
        local_heads, ctx_count, capacity, BLK, width_pair
    )
    incoming = lax.all_to_all(outgoing, "ctx", split_axis=1, concat_axis=1, tiled=True)
    my_owner = lax.dynamic_index_in_dim(req_owner, ctx_rank, 0, keepdims=False)
    my_rank = lax.dynamic_index_in_dim(req_rank, ctx_rank, 0, keepdims=False)
    slot_index = my_owner * capacity + my_rank
    random_pairs = incoming.reshape(local_heads, ctx_count * capacity, BLK, width_pair)[
        :, slot_index
    ]
    random_pairs = random_pairs.reshape(local_heads, block_local, NR, BLK, width_pair)

    def assemble(first_block):
        region = lax.dynamic_slice_in_dim(extended, first_block * BLK, (per_step + 2) * BLK, 1)
        region = region.reshape(local_heads, per_step + 2, BLK, width_pair)
        window = jnp.stack(
            [region[:, shift_pos : shift_pos + per_step] for shift_pos in range(3)], axis=2
        )
        glob_part = jnp.broadcast_to(
            global_pairs[:, None], (local_heads, per_step, NG, BLK, width_pair)
        )
        rand_part = lax.dynamic_slice_in_dim(random_pairs, first_block, per_step, 1)
        gathered = jnp.concatenate([window, glob_part, rand_part], axis=2).reshape(
            local_heads, per_step, key_slots * BLK, width_pair
        )
        whole_ids = ctx_rank * block_local + first_block + jnp.arange(per_step, dtype=jnp.int32)
        neighbour = whole_ids[:, None] - 1 + jnp.arange(3, dtype=jnp.int32)[None, :]
        inside = (neighbour >= 0) & (neighbour < block_local * ctx_count)
        slot_ok = jnp.concatenate([inside, jnp.ones((per_step, NG + NR), jnp.bool_)], axis=1)
        return (gathered, jnp.repeat(slot_ok, BLK, axis=1))

    def scores_of(query_rows, gathered, key_mask):
        raw_scores = (
            jnp.einsum(
                "hjqd,hjkd->hjqk",
                query_rows,
                gathered[..., :HD],
                preferred_element_type=jnp.float32,
            )
            * scale_factor
        )
        return jnp.where(key_mask[None, :, None, :], raw_scores, NEG_FILL)

    def rows_of(source, first_block):
        sliced = lax.dynamic_slice_in_dim(source, first_block * BLK, per_step * BLK, 1)
        return sliced.reshape(local_heads, per_step, BLK, source.shape[2])

    step_count = block_local // per_step
    step_ids = jnp.arange(step_count, dtype=jnp.int32)

    def forward_step(state_in, step_id):
        first_block = step_id * per_step
        gathered, key_mask = assemble(first_block)
        query_rows = rows_of(query_heads, first_block)
        scores = scores_of(query_rows, gathered, key_mask)
        row_max = jnp.max(scores, axis=3)
        weights = jnp.exp(scores - row_max[..., None])
        row_sum = jnp.sum(weights, axis=3)
        weights_low = (weights / row_sum[..., None]).astype(jnp.bfloat16)
        attended = jnp.einsum(
            "hjqk,hjkd->hjqd", weights_low, gathered[..., HD:], preferred_element_type=jnp.float32
        ).astype(jnp.bfloat16)
        return (state_in, (attended, row_max, row_sum))

    unused, (attended_all, max_all, sum_all) = lax.scan(
        forward_step, jnp.zeros((), jnp.float32), step_ids
    )
    out_heads = jnp.transpose(attended_all, (1, 0, 2, 3, 4)).reshape(local_heads, seg_rows, HD)

    def backward_step(state_in, step_id):
        window_acc, global_acc = state_in
        first_block = step_id * per_step
        gathered, key_mask = assemble(first_block)
        query_rows = rows_of(query_heads, first_block)
        dout_rows = rows_of(dout_heads, first_block)
        scores = scores_of(query_rows, gathered, key_mask)
        probs_full = jnp.exp(scores - max_all[step_id][..., None]) / sum_all[step_id][..., None]
        weights_low = probs_full.astype(jnp.bfloat16)
        dprobs = jnp.einsum(
            "hjqd,hjkd->hjqk", dout_rows, gathered[..., HD:], preferred_element_type=jnp.float32
        )
        centre = jnp.sum(probs_full * dprobs, axis=3, keepdims=True)
        dscores = (probs_full * (dprobs - centre)).astype(jnp.bfloat16)
        dquery = (
            jnp.einsum(
                "hjqk,hjkd->hjqd", dscores, gathered[..., :HD], preferred_element_type=jnp.float32
            )
            * scale_factor
        ).astype(jnp.bfloat16)
        key_grads = (
            jnp.einsum("hjqk,hjqd->hjkd", dscores, query_rows, preferred_element_type=jnp.float32)
            * scale_factor
        )
        value_grads = jnp.einsum(
            "hjqk,hjqd->hjkd", weights_low, dout_rows, preferred_element_type=jnp.float32
        )
        pair_terms = jnp.concatenate([key_grads, value_grads], axis=3).reshape(
            local_heads, per_step, key_slots, BLK, width_pair
        )
        spread = jnp.zeros((local_heads, per_step + 2, BLK, width_pair), jnp.float32)
        for shift_pos in range(3):
            spread = spread.at[:, shift_pos : shift_pos + per_step].add(pair_terms[:, :, shift_pos])
        current = lax.dynamic_slice_in_dim(window_acc, first_block * BLK, (per_step + 2) * BLK, 1)
        updated = current + spread.reshape(local_heads, (per_step + 2) * BLK, width_pair)
        window_acc = lax.dynamic_update_slice_in_dim(window_acc, updated, first_block * BLK, 1)
        global_acc = global_acc + jnp.sum(pair_terms[:, :, 3 : 3 + NG], axis=1)
        return ((window_acc, global_acc), (dquery, pair_terms[:, :, 3 + NG :].astype(jnp.bfloat16)))

    start_state = (
        jnp.zeros((local_heads, seg_rows + 2 * BLK, width_pair), jnp.float32),
        jnp.zeros((local_heads, NG, BLK, width_pair), jnp.float32),
    )
    (window_acc, global_acc), (dquery_all, rand_grads) = lax.scan(
        backward_step, start_state, step_ids
    )
    dq_heads = jnp.transpose(dquery_all, (1, 0, 2, 3, 4)).reshape(local_heads, seg_rows, HD)
    own_rows = window_acc[:, BLK : BLK + seg_rows]
    from_right = shifted(window_acc[:, :BLK], "ctx", -1)
    from_left = shifted(window_acc[:, BLK + seg_rows :], "ctx", 1)
    own_rows = own_rows.at[:, :BLK].add(from_left).at[:, seg_rows - BLK :].add(from_right)
    summed_global = lax.psum(global_acc, "ctx")
    own_blocks = own_rows.reshape(local_heads, block_local, BLK, width_pair)
    for glob_slot in range(NG):
        share = jnp.where(glob_owner[glob_slot] == ctx_rank, summed_global[:, glob_slot], 0.0)
        own_blocks = own_blocks.at[:, glob_local[glob_slot]].add(share)
    rand_flat = jnp.transpose(rand_grads, (1, 0, 2, 3, 4, 5)).reshape(
        local_heads, request_count, BLK, width_pair
    )
    replies = jnp.zeros((local_heads, ctx_count * capacity, BLK, width_pair), jnp.bfloat16)
    replies = replies.at[:, slot_index].set(rand_flat)
    replies = replies.reshape(local_heads, ctx_count, capacity, BLK, width_pair)
    returned = lax.all_to_all(replies, "ctx", split_axis=1, concat_axis=1, tiled=True)
    returned = returned.reshape(local_heads, ctx_count * capacity, BLK, width_pair).astype(
        jnp.float32
    )
    own_blocks = own_blocks.at[:, send_local.reshape(-1)].add(returned)
    pair_grads = own_blocks.reshape(local_heads, seg_rows, width_pair).astype(jnp.bfloat16)
    out_back, dq_back, pair_back = (
        lax.all_to_all(out_heads, "heads", split_axis=1, concat_axis=0, tiled=True),
        lax.all_to_all(dq_heads, "heads", split_axis=1, concat_axis=0, tiled=True),
        lax.all_to_all(pair_grads, "heads", split_axis=1, concat_axis=0, tiled=True),
    )
    pair_sum = jnp.sum(
        pair_back.astype(jnp.float32).reshape(KVH, group_size, local_tokens, width_pair), axis=1
    ).astype(jnp.bfloat16)
    pair_sum = jnp.transpose(pair_sum, (1, 0, 2))
    attn_out = jnp.transpose(out_back, (1, 0, 2)).reshape(local_tokens, H * HD)
    grad_query = jnp.transpose(dq_back, (1, 0, 2)).reshape(local_tokens, H * HD)
    grad_keys = pair_sum[:, :, :HD].reshape(local_tokens, KVH * HD)
    grad_values = pair_sum[:, :, HD:].reshape(local_tokens, KVH * HD)
    return (attn_out, grad_query, grad_keys, grad_values)


def solution(mesh):
    in_specs = (
        P(("ctx", "heads"), None),
        P(("ctx", "heads"), None),
        P(("ctx", "heads"), None),
        P(("ctx", "heads"), None),
        P(),
        P(),
    )
    out_specs = (
        P(("ctx", "heads"), None),
        P(("ctx", "heads"), None),
        P(("ctx", "heads"), None),
        P(("ctx", "heads"), None),
    )
    return jax.shard_map(shards, mesh=mesh, in_specs=in_specs, out_specs=out_specs, check_vma=False)
```

profile of v0, /device:TPU:0, one launch (start us, length us, event | category | flops | bytes accessed | tf_op | source)
XLA Modules:
  0.0 547.1 jit_solution(13775073427089429024)
XLA Ops:
  7.2 2.3 copy.277
  9.5 7.3 %all-to-all-start = ((bf16[32,128,128]{1,2,0:T(8,128)(2,1)}), bf16[32,128,128]{1,2,0:T(8,128)(2,1)S(1)}, u32[]{:S(2)}, u32[]{:S(2)}) async-start(bf16[32,128,128]{1,2,0:T(8,128)(2,1)} %bitcast.14), calls=%async_computation | async-start | bytes 2097152 | tf_op jit(solution)/shard_map/all_to_all | solution.py:59
  17.0 25.5 %all-to-all-done = bf16[32,128,128]{1,2,0:T(8,128)(2,1)S(1)} async-done(((bf16[32,128,128]{1,2,0:T(8,128)(2,1)}), bf16[32,128,128]{1,2,0:T(8,128)(2,1)S(1)}, u32[]{:S(2)}, u32[]{:S(2)}) %all-to-all-start) | async-done | bytes 1048608 | tf_op jit(solution)/shard_map/all_to_all | solution.py:59
  44.1 3.7 all-to-all-start.1
  47.8 2.3 copy.292
  50.1 46.1 %all-to-all-done.1 = bf16[32,128,256]{2,1,0:T(8,128)(2,1)S(1)} async-done(((bf16[32,128,256]{2,1,0:T(8,128)(2,1)}), bf16[32,128,256]{2,1,0:T(8,128)(2,1)S(1)}, u32[]{:S(2)}, u32[]{:S(2)}) %all-to-all-start.1) | async-done | bytes 2097184 | tf_op jit(solution)/shard_map/all_to_all | solution.py:60
  96.2 4.3 all-to-all-start.4
  104.4 3.1 copy.283
  107.5 18.6 %all-to-all-done.4 = bf16[32,128,128]{1,2,0:T(8,128)(2,1)} async-done(((bf16[32,128,128]{1,2,0:T(8,128)(2,1)}), bf16[32,128,128]{1,2,0:T(8,128)(2,1)}, u32[]{:S(2)}, u32[]{:S(2)}) %all-to-all-start.4) | async-done | bytes 1048608 | tf_op jit(solution)/shard_map/all_to_all | solution.py:61
  126.1 4.5 all-to-all-start.2
  139.7 2.3 collective-permute-start
  144.8 2.3 copy.294
  147.0 26.6 %all-reduce.9.cloned.1.call-done = (bf16[4,1,128,256]{3,2,0,1:T(8,128)(2,1)}, bf16[4,1,128,256]{3,2,0,1:T(8,128)(2,1)}) async-done(((bf16[4,1,128,256]{3,2,0,1:T(8,128)(2,1)}, bf16[4,1,128,256]{3,2,0,1:T(8,128)(2,1)}), (bf16[4,1,128,256]{3,2,0,1:T(8,128)(2,1)}, bf16[4,1,128,256]{3,2,0,1:T(8,128)(2,1)})) %all-reduce.9.cloned.1.call-update) | async-done | bytes 524304 | tf_op jit(solution)/shard_map/psum | solution.py:34
  176.6 3.1 copy.284
  179.8 3.6 gather_fusion.1
  183.4 3.1 copy.286
  187.7 22.6 %while.43 = (s32[]{:T(128)}, bf16[2,4,4,128,128]{4,3,2,0,1:T(8,128)(2,1)}, f32[2,4,4,128]{3,2,1,0:T(4,128)S(1)}, f32[2,4,4,128]{3,2,1,0:T(4,128)S(1)}, s32[2]{0:...) while((s32[]{:T(128)}, ...), condition=%wide.region_7.8_spmd, body=%wide.region_4.7_spmd.sunk | while | flops 824438848 | bytes 58288652 | solution.py:151
  195.6 2.4 fusion.115
  206.9 2.4 fusion.115
  211.6 2.9 broadcast_in_dim.169
  214.5 129.3 %while.44 = (s32[]{:T(128)}, f32[4,1280,256]{2,1,0:T(8,128)}, f32[4,2,128,256]{3,2,1,0:T(8,128)}, bf16[2,4,4,128,128]{4,3,2,0,1:T(8,128)(2,1)}, bf16[2,4,4,1,128...) while((s32[]{:T(128)}, f32[4,1280,256]{2,1,0:T(8,128)}, ...), condition=%wide.region_11.12_spmd.clone, body=%wide.region_8.11_spmd.clone.sunk | while | flops 2037381120 | bytes 296825664 | solution.py:199
  225.8 3.0 multiply_reduce_fusion.2
  229.4 3.7 fusion.133
  233.1 3.7 fusion.130
  236.8 3.6 broadcast_multiply_fusion.2
  240.4 10.4 %pad_maximum_fusion.5 = f32[4,4,768,256]{2,3,1,0:T(8,128)} fusion(f32[4,4,768,128]{2,3,1,0:T(8,128)} %fusion.130, f32[4,4,768,128]{2,3,1,0:T(8,128)} %broadcast_multiply_fusion.2), kind=kLoop, calls=%fused_computation.38.clone.1 | loop fusion | flops 3145728 | bytes 25165824 | tf_op jit(solution)/shard_map/while/body/eval_jaxpr/concatenate | solution.py:183
  250.8 12.6 %copy.337 = f32[4,4,768,256]{3,2,1,0:T(8,128)} copy(f32[4,4,768,256]{2,3,1,0:T(8,128)} %pad_maximum_fusion.5) | data formatting | bytes 25165824 | tf_op jit(solution)/shard_map/while/body/eval_jaxpr/concatenate | solution.py:183
  263.4 2.8 slice_reduce_fusion.2
  268.7 2.6 slice_bitcast_fusion.10
  271.6 2.3 fusion.131
  276.7 2.4 copy-done
  290.4 2.9 multiply_reduce_fusion.2
  294.0 3.7 fusion.133
  297.8 3.7 fusion.130
  301.4 3.6 broadcast_multiply_fusion.2
  305.1 10.4 %pad_maximum_fusion.5 = f32[4,4,768,256]{2,3,1,0:T(8,128)} fusion(f32[4,4,768,128]{2,3,1,0:T(8,128)} %fusion.130, f32[4,4,768,128]{2,3,1,0:T(8,128)} %broadcast_multiply_fusion.2), kind=kLoop, calls=%fused_computation.38.clone.1 | loop fusion | flops 3145728 | bytes 25165824 | tf_op jit(solution)/shard_map/while/body/eval_jaxpr/concatenate | solution.py:183
  315.4 12.6 %copy.337 = f32[4,4,768,256]{3,2,1,0:T(8,128)} copy(f32[4,4,768,256]{2,3,1,0:T(8,128)} %pad_maximum_fusion.5) | data formatting | bytes 25165824 | tf_op jit(solution)/shard_map/while/body/eval_jaxpr/concatenate | solution.py:183
  328.0 2.8 slice_reduce_fusion.2
  333.3 2.6 slice_bitcast_fusion.10
  336.3 2.3 fusion.131
  338.6 2.1 fusion.132
  341.4 2.4 copy-done
  343.8 3.2 copy.303
  347.2 3.4 scatter_fusion
  352.1 3.8 all-to-all-start.6
  357.7 23.7 %all-to-all-done.6 = bf16[4,4,2,128,256]{4,3,2,0,1:T(8,128)(2,1)S(1)} async-done(((bf16[4,4,2,128,256]{4,3,2,0,1:T(8,128)(2,1)}), bf16[4,4,2,128,256]{4,3,2,0,1:T(8,128)(2,1)S(1)}, u32[]{:S(2)}, u32[]{:S(2)}) %all-to-all-start.6) | async-done | bytes 2097184 | tf_op jit(solution)/shard_map/all_to_all | solution.py:218
  381.3 5.5 %all-to-all-start.3 = ((bf16[4,1024,128]{2,0,1:T(4,128)(2,1)}), bf16[4,1024,128]{2,0,1:T(4,128)(2,1)S(1)}, u32[]{:S(2)}, u32[]{:S(2)}) async-start(bf16[4,1024,128]{2,0,1:T(4,128)(2,1)} %copy.288), calls=%async_computation.3 | async-start | bytes 2097152 | tf_op jit(solution)/shard_map/all_to_all | solution.py:225
  388.7 2.2 collective-permute-start.2
  391.0 4.5 slice.338
  397.2 15.3 %all-to-all-done.3 = bf16[4,1024,128]{2,0,1:T(4,128)(2,1)S(1)} async-done(((bf16[4,1024,128]{2,0,1:T(4,128)(2,1)}), bf16[4,1024,128]{2,0,1:T(4,128)(2,1)S(1)}, u32[]{:S(2)}, u32[]{:S(2)}) %all-to-all-start.3) | async-done | bytes 1048608 | tf_op jit(solution)/shard_map/all_to_all | solution.py:225
  412.5 4.2 all-to-all-start.5
  416.8 2.4 fusion.67
  425.5 33.1 %all-reduce.7.cloned.1.call-done = f32[4,2,128,256]{3,2,1,0:T(8,128)} async-done(((f32[4,2,128,256]{3,2,1,0:T(8,128)}), f32[4,2,128,256]{3,2,1,0:T(8,128)}) %all-reduce.7.cloned.1.call-update) | async-done | bytes 1048592 | tf_op jit(solution)/shard_map/psum | solution.py:207
  458.7 2.7 fusion.58
  461.4 2.7 fusion.59
  464.8 2.4 copy.306
  467.2 9.1 %scatter_fusion.1 = f32[4,8,128,256]{3,2,1,0:T(8,128)} fusion(f32[4,8,128,256]{3,2,1,0:T(8,128)} %fusion.59, s32[8]{0:T(128)S(1)} %copy-done.19, f32[8,4,128,256]{3,2,1,0:T(8,128)} %copy.306), kind=kCustom, calls=%fused_computation.3 | custom fusion | flops 1048576 | bytes 12582944 | tf_op jit(solution)/shard_map/scatter-add | solution.py:222
  476.3 2.5 convert_element_type.70
  478.7 2.9 copy.307
  481.7 5.5 %all-to-all-start.7 = ((bf16[4,1024,256]{2,0,1:T(4,128)(2,1)}), bf16[4,1024,256]{2,0,1:T(4,128)(2,1)S(1)}, u32[]{:S(2)}, u32[]{:S(2)}) async-start(bf16[4,1024,256]{2,0,1:T(4,128)(2,1)} %copy.307), calls=%async_computation.7 | async-start | bytes 4194304 | tf_op jit(solution)/shard_map/all_to_all | solution.py:227
  488.8 2.3 copy.310
  493.8 2.3 copy.311
  496.1 39.2 %all-to-all-done.7 = bf16[4,1024,256]{2,0,1:T(4,128)(2,1)S(1)} async-done(((bf16[4,1024,256]{2,0,1:T(4,128)(2,1)}), bf16[4,1024,256]{2,0,1:T(4,128)(2,1)S(1)}, u32[]{:S(2)}, u32[]{:S(2)}) %all-to-all-start.7) | async-done | bytes 2097184 | tf_op jit(solution)/shard_map/all_to_all | solution.py:227
  535.3 3.0 convert_reduce_fusion
  (221 shorter events, 78.2 us)
Async XLA Ops:
  7.2 9.6 %copy-start.14 = (bf16[128,512]{1,0:T(8,128)(2,1)S(1)}, bf16[128,512]{1,0:T(8,128)(2,1)}, u32[]{:S(2)}) copy-start(bf16[128,512]{1,0:T(8,128)(2,1)} %param.25) | copy-start | bytes 393220
  7.2 9.6 %copy-start.15 = (bf16[128,512]{1,0:T(8,128)(2,1)S(1)}, bf16[128,512]{1,0:T(8,128)(2,1)}, u32[]{:S(2)}) copy-start(bf16[128,512]{1,0:T(8,128)(2,1)} %param.26) | copy-start | bytes 393220
  9.5 33.0 %all-to-all-start = ((bf16[32,128,128]{1,2,0:T(8,128)(2,1)}), bf16[32,128,128]{1,2,0:T(8,128)(2,1)S(1)}, u32[]{:S(2)}, u32[]{:S(2)}) async-start(bf16[32,128,128]{1,2,0:T(8,128)(2,1)} %bitcast.14), calls=%async_computation | async-start | bytes 2097152 | tf_op jit(solution)/shard_map/all_to_all | solution.py:59
  44.1 56.9 %copy-start.21 = (s32[32,1]{0,1:T(1,128)S(1)}, s32[32,1]{0,1:T(1,128)}, u32[]{:S(2)}) copy-start(s32[32,1]{0,1:T(1,128)} %param.28) | copy-start | bytes 388
  44.1 52.1 %all-to-all-start.1 = ((bf16[32,128,256]{2,1,0:T(8,128)(2,1)}), bf16[32,128,256]{2,1,0:T(8,128)(2,1)S(1)}, u32[]{:S(2)}, u32[]{:S(2)}) async-start(bf16[32,128,256]{2,1,0:T(8,128)(2,1)} %bitcast.296), calls=%async_computation.1 | async-start | bytes 4194304 | tf_op jit(solution)/shard_map/all_to_all | solution.py:60
  96.2 29.9 %all-to-all-start.4 = ((bf16[32,128,128]{1,2,0:T(8,128)(2,1)}), bf16[32,128,128]{1,2,0:T(8,128)(2,1)}, u32[]{:S(2)}, u32[]{:S(2)}) async-start(bf16[32,128,128]{1,2,0:T(8,128)(2,1)} %bitcast.302), calls=%async_computation.4 | async-start | bytes 2097152 | tf_op jit(solution)/shard_map/all_to_all | solution.py:61
  102.3 5.2 copy-start.18
  104.4 26.2 %copy-start.22 = (s32[2]{0:T(128)S(1)}, s32[2]{0:T(128)}, u32[]{:S(2)}) copy-start(s32[2]{0:T(128)} %param.29) | copy-start | bytes 28
  126.1 50.5 %all-to-all-start.2 = ((bf16[4,4,2,128,256]{4,3,2,0,1:T(8,128)(2,1)}), bf16[4,4,2,128,256]{4,3,2,0,1:T(8,128)(2,1)}, u32[]{:S(2)}, u32[]{:S(2)}) async-start(bf16[4,4,2,128,256]{4,3,2,0,1:T(8,128)(2,1)} %copy.283), calls=%async_computation.2 | async-start | bytes 4194304 | tf_op jit(solution)/shard_map/all_to_all | solution.py:90
  130.6 43.0 %all-reduce.9.cloned.1.call-start = ((), (), s32[]{:S(2)}) async-start(), calls=%async_computation.9 | async-start | bytes 1048576 | tf_op jit(solution)/shard_map/psum | solution.py:34
  139.7 35.0 %collective-permute-start = (bf16[4,128,256]{2,1,0:T(8,128)(2,1)S(1)}, bf16[4,128,256]{2,1,0:T(8,128)(2,1)S(1)}, u32[]{:S(2)}, u32[]{:S(2)}) collective-permute-start(bf16[4,128,256]{2,1,0:T(8,128)(2,1)S(1)} %get-tuple-element.783), channel_id=1, source_target_pairs={{0,1},{1,2},{2,3},{4,5},{5,6},{6,7},{8,9},{9,10},{10,11},{12,13},{... | collective-permute-start | bytes 786440 | tf_op jit(solution)/shard_map/ppermute | solution.py:26
  142.1 32.7 %collective-permute-start.1 = (bf16[4,128,256]{2,1,0:T(8,128)(2,1)S(1)}, bf16[4,128,256]{2,1,0:T(8,128)(2,1)}, u32[]{:S(2)}, u32[]{:S(2)}) collective-permute-start(bf16[4,128,256]{2,1,0:T(8,128)(2,1)S(1)} %get-tuple-element.784), channel_id=1, source_target_pairs={{1,0},{2,1},{3,2},{5,4},{6,5},{7,6},{9,8},{10,9},{11,10},{13,12},{... | collective-permute-start | bytes 786440 | tf_op jit(solution)/shard_map/ppermute | solution.py:27
  143.4 31.4 %copy-start.16 = (s32[8]{0:T(128)}, s32[8]{0:T(128)S(1)}, u32[]{:S(2)}) copy-start(s32[8]{0:T(128)S(1)} %fusion.66) | copy-start | bytes 100
  190.9 1.6 copy-start.4
  194.0 1.6 copy-start.9
  198.0 1.0 copy-start.10
  202.3 1.6 copy-start.4
  205.3 1.6 copy-start.9
  209.4 1.0 copy-start.10
  214.5 4.2 copy-start.2
  221.4 1.6 copy-start.5
  223.1 2.7 copy-start.1
  263.4 2.8 copy-start.6
  263.4 3.2 copy-start.12
  266.6 5.0 copy-start.7
  268.7 2.9 copy-start.13
  271.2 4.8 slice-start
  271.6 4.4 slice-start.1
  276.0 3.1 copy-start.3
  276.7 2.4 copy-start
  279.1 4.2 copy-start.2
  286.1 1.6 copy-start.5
  287.8 2.7 copy-start.1
  328.0 2.8 copy-start.6
  328.0 3.2 copy-start.12
  331.2 5.0 copy-start.7
  333.3 2.9 copy-start.13
  335.9 4.8 slice-start
  336.3 4.4 slice-start.1
  340.7 3.1 copy-start.3
  341.3 2.4 copy-start
  343.8 3.4 copy-start.17
  350.6 5.3 copy-start.11
  352.1 29.3 %all-to-all-start.6 = ((bf16[4,4,2,128,256]{4,3,2,0,1:T(8,128)(2,1)}), bf16[4,4,2,128,256]{4,3,2,0,1:T(8,128)(2,1)S(1)}, u32[]{:S(2)}, u32[]{:S(2)}) async-start(bf16[4,4,2,128,256]{4,3,2,0,1:T(8,128)(2,1)} %copy.304), calls=%async_computation.6 | async-start | bytes 4194304 | tf_op jit(solution)/shard_map/all_to_all | solution.py:218
  381.3 31.2 %all-to-all-start.3 = ((bf16[4,1024,128]{2,0,1:T(4,128)(2,1)}), bf16[4,1024,128]{2,0,1:T(4,128)(2,1)S(1)}, u32[]{:S(2)}, u32[]{:S(2)}) async-start(bf16[4,1024,128]{2,0,1:T(4,128)(2,1)} %copy.288), calls=%async_computation.3 | async-start | bytes 2097152 | tf_op jit(solution)/shard_map/all_to_all | solution.py:225
  388.7 6.7 %copy-start.8 = (bf16[2,4,4,128,128]{4,3,2,0,1:T(8,128)(2,1)S(1)}, bf16[2,4,4,128,128]{4,3,2,0,1:T(8,128)(2,1)}, u32[]{:S(2)}) copy-start(bf16[2,4,4,128,128]{4,3,2,0,1:T(8,128)(2,1)} %get-tuple-element.450) | copy-start | bytes 3145732
  388.7 28.1 %collective-permute-start.2 = (f32[4,128,256]{2,1,0:T(8,128)}, f32[4,128,256]{2,1,0:T(8,128)}, u32[]{:S(2)}, u32[]{:S(2)}) collective-permute-start(f32[4,128,256]{2,1,0:T(8,128)} %slice.340), channel_id=1, source_target_pairs={{0,1},{1,2},{2,3},{4,5},{5,6},{6,7},{8,9},{9,10},{10,11},{12,13},{... | collective-permute-start | bytes 1572872 | tf_op jit(solution)/shard_map/ppermute | solution.py:40
  395.4 26.3 %copy-start.20 = (s32[4]{0:T(128)S(1)}, s32[4]{0:T(128)}, u32[]{:S(2)}) copy-start(s32[4]{0:T(128)} %constant.447.clone.1) | copy-start | bytes 52
  412.5 69.2 %all-to-all-start.5 = ((bf16[4,1024,128]{2,0,1:T(4,128)(2,1)}), bf16[4,1024,128]{2,0,1:T(4,128)(2,1)}, u32[]{:S(2)}, u32[]{:S(2)}) async-start(bf16[4,1024,128]{2,0,1:T(4,128)(2,1)} %copy.298), calls=%async_computation.5 | async-start | bytes 2097152 | tf_op jit(solution)/shard_map/all_to_all | solution.py:226
  416.8 41.9 %all-reduce.7.cloned.1.call-start = ((), (), s32[]{:S(2)}) async-start(), calls=%async_computation.8 | async-start | bytes 2097152 | tf_op jit(solution)/shard_map/psum | solution.py:207
  419.3 4.1 collective-permute-start.3
  464.8 2.4 copy-start.19
  481.7 53.6 %all-to-all-start.7 = ((bf16[4,1024,256]{2,0,1:T(4,128)(2,1)}), bf16[4,1024,256]{2,0,1:T(4,128)(2,1)S(1)}, u32[]{:S(2)}, u32[]{:S(2)}) async-start(bf16[4,1024,256]{2,0,1:T(4,128)(2,1)} %copy.307), calls=%async_computation.7 | async-start | bytes 4194304 | tf_op jit(solution)/shard_map/all_to_all | solution.py:227
Sparse Core Ops, SparseCore 0:
  138.8 34.7 all-reduce.8
  420.7 37.8 all-reduce.6
where the time goes:
time: 550 us; the launch traced here: 547 us
  waiting for transfers between devices  229 us (42%)
  local copies, waits for them, and re-layouts  131 us (24%)
  other arithmetic  72.8 us (13%)
  starting transfers between devices  46 us (8%)
  matrix products  37.5 us (7%)
  between operations  20.6 us (4%)
  loops' own time  9.81 us (2%)
    all_to_all x1, waiting for transfers between devices, shards(): lax.all_to_all(pairs_wide, 'heads', split_axis=0, concat_axis=1, tiled=True)  46.1 us
    all_to_all x1, waiting for transfers between devices, shards(): lax.all_to_all(pair_grads, 'heads', split_axis=1, concat_axis=0, tiled=True)  39.2 us
    psum x1, waiting for transfers between devices, shards(): summed_global = lax.psum(global_acc, 'ctx')  33.1 us
    psum x1, waiting for transfers between devices, broadcast(): return lax.psum(jnp.where(mine, value, jnp.zeros_like(value)), axis)  26.6 us
    all_to_all x1, waiting for transfers between devices, shards(): lax.all_to_all(query_wide, 'heads', split_axis=0, concat_axis=1, tiled=True)  25.5 us
    concatenate x2, local copies, waits for them, and re-layouts, backward_step(): jnp.concatenate([key_grads, value_grads], axis=3)  25.2 us
    all_to_all x1, waiting for transfers between devices, shards(): lax.all_to_all(replies, 'ctx', split_axis=1, concat_axis=1, tiled=True)  23.7 us
    concatenate x2, other arithmetic, backward_step(): jnp.concatenate([key_grads, value_grads], axis=3)  20.7 us
  transfers between devices with their start and end apart: 14, of which 9 were waited for; matrix products, arithmetic and copies ran while one was open for 12% of the time, Pallas kernels for 0%

commit v1 on v0

v1 whole, which is shorter than its diff:
```python
import functools
import math

import jax
import jax.numpy as jnp
from jax import lax
from jax.experimental import pallas as pl
from jax.experimental.pallas import tpu as pltpu
from jax.sharding import PartitionSpec as P

HD = 128
H = 32
KVH = 4
BLK = 128
NG = 2
GROUP = H // KVH
SCALE = 1.0 / math.sqrt(HD)
NEG_FILL = -1e30
AXES = ("ctx", "heads")
FAR = 1 + NG
SLOTS = 3 + FAR
WIDE = GROUP * BLK
PAIR = 2 * BLK
BF16 = jnp.bfloat16
F32 = jnp.float32

NT = (((1,), (1,)), ((), ()))


def params(mib, **kw):
    return pltpu.CompilerParams(vmem_limit_bytes=mib << 20, **kw)


def all_to_all(value):
    return lax.all_to_all(value, AXES, split_axis=0, concat_axis=0, tiled=True)


def shifted(value, steps):
    heads, ctx = lax.axis_size("heads"), lax.axis_size("ctx")
    count = heads * ctx
    place = lambda block: (block % heads) * ctx + block // heads
    pairs = [
        (place(i), place(i + steps)) for i in range(count) if 0 <= i + steps < count
    ]
    return lax.ppermute(value, ("heads", "ctx"), pairs)


def pack_kernel(k_ref, v_ref, out_ref):
    for g in range(KVH):
        cols = slice(g * HD, (g + 1) * HD)
        out_ref[0, g] = k_ref[:, cols]
        out_ref[1, g] = v_ref[:, cols]


def pack(keys, values):
    return pl.pallas_call(
        pack_kernel,
        out_shape=jax.ShapeDtypeStruct((2, KVH, BLK, HD), BF16),
        compiler_params=params(8),
        name="pack",
    )(keys, values)


def select_kernel(rand_ref, glob_ref, in_ref, out_ref):
    count = in_ref.shape[0]
    globs = [in_ref[glob_ref[slot]] for slot in range(NG)]
    for i in range(count):
        out_ref[i, 0] = in_ref[rand_ref[i, 0]]
        for slot in range(NG):
            out_ref[i, 1 + slot] = globs[slot]


def select(rand_blocks, glob_blocks, slices):
    count, rows, _ = slices.shape
    if rows % 16:
        rand_part = slices[rand_blocks[:, 0]]
        glob_part = jnp.broadcast_to(slices[glob_blocks][None], (count, NG, rows, HD))
        return jnp.concatenate([rand_part[:, None], glob_part], axis=1)
    return pl.pallas_call(
        select_kernel,
        out_shape=jax.ShapeDtypeStruct((count, FAR, rows, HD), BF16),
        in_specs=[
            pl.BlockSpec(memory_space=pltpu.SMEM),
            pl.BlockSpec(memory_space=pltpu.SMEM),
            pl.BlockSpec(memory_space=pltpu.VMEM),
        ],
        out_specs=pl.BlockSpec(memory_space=pltpu.VMEM),
        compiler_params=params(8),
        name="select",
    )(rand_blocks, glob_blocks, slices)


def combine_kernel(rand_ref, glob_ref, in_ref, out_ref, acc_ref):
    count = in_ref.shape[0]
    acc_ref[...] = jnp.zeros_like(acc_ref)
    for slot in range(NG):
        total = in_ref[0, 1 + slot].astype(F32)
        for i in range(1, count):
            total = total + in_ref[i, 1 + slot].astype(F32)
        acc_ref[glob_ref[slot]] += total
    for i in range(count):
        acc_ref[rand_ref[i, 0]] += in_ref[i, 0].astype(F32)
    out_ref[...] = acc_ref[...].astype(BF16)


def combine(rand_blocks, glob_blocks, terms):
    count, _, rows, _ = terms.shape
    if rows % 16:
        wide = terms.astype(F32)
        total = jnp.zeros((count, rows, HD), F32)
        total = total.at[glob_blocks].add(jnp.sum(wide[:, 1:], axis=0))
        return total.at[rand_blocks[:, 0]].add(wide[:, 0]).astype(BF16)
    return pl.pallas_call(
        combine_kernel,
        out_shape=jax.ShapeDtypeStruct((count, rows, HD), BF16),
        in_specs=[
            pl.BlockSpec(memory_space=pltpu.SMEM),
            pl.BlockSpec(memory_space=pltpu.SMEM),
            pl.BlockSpec(memory_space=pltpu.VMEM),
        ],
        out_specs=pl.BlockSpec(memory_space=pltpu.VMEM),
        scratch_shapes=[pltpu.VMEM((count, rows, HD), F32)],
        compiler_params=params(16),
        name="combine",
    )(rand_blocks, glob_blocks, terms)


def stacked(ref):
    return jnp.concatenate(
        [ref[:, h * HD : (h + 1) * HD] for h in range(GROUP)], axis=0
    )


def keys_of(kind, own_ref, left_ref, right_ref, far_ref):
    blocks = [left_ref[kind, 0], own_ref[kind, 0], right_ref[kind, 0]]
    for slot in (1, 2, 0):
        blocks.append(far_ref[kind, :, slot].reshape(BLK, HD))
    return blocks


def scores_kernel(
    edge_ref, q_ref, do_ref, own_ref, left_ref, right_ref, far_ref,
    probs_ref, ds_ref, terms_ref, s_ref, dp_ref,
):
    keys = keys_of(0, own_ref, left_ref, right_ref, far_ref)
    values = keys_of(1, own_ref, left_ref, right_ref, far_ref)
    queries, douts = stacked(q_ref), stacked(do_ref)
    factor = SCALE / math.log(2.0)
    for pair in range(WIDE // PAIR):
        cols = slice(pair * PAIR, (pair + 1) * PAIR)
        q, do = queries[cols], douts[cols]
        row_max = None
        for b in range(SLOTS):
            s = lax.dot_general(keys[b], q, NT, preferred_element_type=F32)
            if b == 0:
                s = jnp.where(edge_ref[0] == 0, s, NEG_FILL)
            if b == 2:
                s = jnp.where(edge_ref[1] == 0, s, NEG_FILL)
            s_ref[b * BLK : (b + 1) * BLK] = s
            top = jnp.max(s, axis=0, keepdims=True)
            row_max = top if row_max is None else jnp.maximum(row_max, top)
        row_sum = jnp.zeros((1, PAIR), F32)
        centre = jnp.zeros((1, PAIR), F32)
        for b in range(SLOTS):
            rows = slice(b * BLK, (b + 1) * BLK)
            w = jnp.exp2((s_ref[rows] - row_max) * factor)
            dp = lax.dot_general(values[b], do, NT, preferred_element_type=F32)
            s_ref[rows] = w
            dp_ref[rows] = dp
            row_sum = row_sum + jnp.sum(w, axis=0, keepdims=True)
            centre = centre + jnp.sum(w * dp, axis=0, keepdims=True)
        inverse = 1.0 / row_sum
        centre = centre * inverse
        for b in range(SLOTS):
            rows = slice(b * BLK, (b + 1) * BLK)
            p = s_ref[rows] * inverse
            probs_ref[0, rows, cols] = p.astype(BF16)
            ds_ref[0, rows, cols] = (p * (dp_ref[rows] - centre)).astype(BF16)
    share = terms_ref.shape[1]
    for slot, b in enumerate((5, 3, 4)):
        rows = slice(b * BLK, (b + 1) * BLK)
        dk = jnp.dot(ds_ref[0, rows], queries, preferred_element_type=F32) * SCALE
        dv = jnp.dot(probs_ref[0, rows], douts, preferred_element_type=F32)
        terms_ref[0, :, slot] = dk.astype(BF16).reshape(share, BLK // share, HD)
        terms_ref[1, :, slot] = dv.astype(BF16).reshape(share, BLK // share, HD)


def outputs_kernel(
    q_ref, do_ref, own_ref, left_ref, right_ref, far_ref, probs_ref, ds_ref,
    out_ref, dq_ref, to_left_ref, to_right_ref, near_ref,
):
    keys_t = jnp.concatenate(
        [k.T for k in keys_of(0, own_ref, left_ref, right_ref, far_ref)], axis=1
    )
    values_t = jnp.concatenate(
        [v.T for v in keys_of(1, own_ref, left_ref, right_ref, far_ref)], axis=1
    )
    for pair in range(WIDE // PAIR):
        cols = slice(pair * PAIR, (pair + 1) * PAIR)
        out_t = jnp.dot(values_t, probs_ref[0, :, cols], preferred_element_type=F32)
        dq_t = jnp.dot(keys_t, ds_ref[0, :, cols], preferred_element_type=F32) * SCALE
        for half in range(2):
            part = slice(half * HD, (half + 1) * HD)
            dest = slice(pair * PAIR + half * HD, pair * PAIR + (half + 1) * HD)
            out_ref[:, dest] = out_t[:, part].T.astype(BF16)
            dq_ref[:, dest] = dq_t[:, part].T.astype(BF16)
    queries, douts = stacked(q_ref), stacked(do_ref)
    for b, dest in enumerate((to_left_ref, near_ref, to_right_ref)):
        rows = slice(b * BLK, (b + 1) * BLK)
        dk = jnp.dot(ds_ref[0, rows], queries, preferred_element_type=F32) * SCALE
        dv = jnp.dot(probs_ref[0, rows], douts, preferred_element_type=F32)
        dest[0, 0] = dk.astype(dest.dtype)
        dest[1, 0] = dv.astype(dest.dtype)


def finish_kernel(near_ref, left_ref, right_ref, far_ref, dk_ref, dv_ref):
    for kind, dest in enumerate((dk_ref, dv_ref)):
        for g in range(KVH):
            total = near_ref[kind, g] + left_ref[kind, g].astype(F32)
            total = total + right_ref[kind, g].astype(F32)
            total = total + far_ref[kind, g].astype(F32)
            dest[:, g * HD : (g + 1) * HD] = total.astype(BF16)


def finish(near, left, right, far):
    shape = jax.ShapeDtypeStruct((BLK, KVH * HD), BF16)
    return pl.pallas_call(
        finish_kernel,
        out_shape=(shape, shape),
        compiler_params=params(8),
        name="finish",
    )(near, left, right, far)


def group_specs(share):
    token = pl.BlockSpec((BLK, WIDE), lambda g, *_: (0, g))
    block = pl.BlockSpec((2, 1, BLK, HD), lambda g, *_: (0, g, 0, 0))
    far = pl.BlockSpec(
        (2, share, FAR, BLK // share, HD), lambda g, *_: (0, g, 0, 0, 0)
    )
    square = pl.BlockSpec((1, SLOTS * BLK, WIDE), lambda g, *_: (g, 0, 0))
    return token, block, far, square


def shards(queries, keys_in, values_in, cotangent, rand_blocks, glob_blocks):
    heads, ctx = lax.axis_size("heads"), lax.axis_size("ctx")
    count = heads * ctx
    mine = lax.axis_index("ctx") * heads + lax.axis_index("heads")
    edges = jnp.array([mine == 0, mine == count - 1]).astype(jnp.int32)
    rows = 2 * KVH * BLK // count
    packed = pack(keys_in, values_in)
    slices = all_to_all(packed.reshape(count, rows, HD))
    left = shifted(packed, 1)
    right = shifted(packed, -1)
    far = all_to_all(select(rand_blocks, glob_blocks, slices))
    if rows % 16:
        share = 1
        far = jnp.transpose(
            far.reshape(2, KVH, BLK // rows, FAR, rows, HD), (0, 1, 3, 2, 4, 5)
        )
    else:
        share = BLK // rows
    far = far.reshape(2, KVH * share, FAR, BLK // share, HD)
    token, block, far_spec, square = group_specs(share)
    square_shape = jax.ShapeDtypeStruct((KVH, SLOTS * BLK, WIDE), BF16)
    block_shape = jax.ShapeDtypeStruct((2, KVH, BLK, HD), BF16)
    flops = 2 * H * BLK * SLOTS * BLK * HD
    probs, ds, terms = pl.pallas_call(
        scores_kernel,
        grid_spec=pltpu.PrefetchScalarGridSpec(
            num_scalar_prefetch=1,
            grid=(KVH,),
            in_specs=[token, token, block, block, block, far_spec],
            out_specs=[square, square, far_spec],
            scratch_shapes=[pltpu.VMEM((SLOTS * BLK, PAIR), F32)] * 2,
        ),
        out_shape=(
            square_shape,
            square_shape,
            jax.ShapeDtypeStruct(far.shape, BF16),
        ),
        compiler_params=params(32, dimension_semantics=("arbitrary",)),
        cost_estimate=pl.CostEstimate(
            flops=3 * flops, bytes_accessed=16 << 20, transcendentals=H * BLK * SLOTS * BLK
        ),
        name="scores",
    )(edges, queries, cotangent, packed, left, right, far)
    if rows % 16:
        terms = jnp.transpose(
            terms.reshape(2, KVH, FAR, BLK // rows, rows, HD), (0, 1, 3, 2, 4, 5)
        )
    arrived = all_to_all(terms.reshape(count, FAR, rows, HD))
    token_shape = jax.ShapeDtypeStruct(queries.shape, BF16)
    attn_out, grad_query, to_left, to_right, near = pl.pallas_call(
        outputs_kernel,
        grid=(KVH,),
        in_specs=[token, token, block, block, block, far_spec, square, square],
        out_specs=[token, token, block, block, block],
        out_shape=(
            token_shape,
            token_shape,
            block_shape,
            block_shape,
            jax.ShapeDtypeStruct((2, KVH, BLK, HD), F32),
        ),
        compiler_params=params(32, dimension_semantics=("arbitrary",)),
        cost_estimate=pl.CostEstimate(
            flops=3 * flops, bytes_accessed=18 << 20, transcendentals=0
        ),
        name="outputs",
    )(queries, cotangent, packed, left, right, far, probs, ds)
    from_right = shifted(to_left, -1)
    from_left = shifted(to_right, 1)
    summed = combine(rand_blocks, glob_blocks, arrived)
    returned = all_to_all(summed).reshape(2, KVH, BLK, HD)
    grad_keys, grad_values = finish(near, from_left, from_right, returned)
    return attn_out, grad_query, grad_keys, grad_values


def solution(mesh):
    spec = P(AXES, None)
    return jax.shard_map(
        shards,
        mesh=mesh,
        in_specs=(spec, spec, spec, spec, P(), P()),
        out_specs=(spec, spec, spec, spec),
        check_vma=False,
    )
```

time: 550 us -> 138 us (0.25)
  waiting for transfers between devices: 229 us -> 43 us
  local copies, waits for them, and re-layouts: 131 us -> 19.3 us
  other arithmetic: 72.8 us -> 0.08 us
  matrix products: 37.5 us -> 0 us
  blocking collectives: 0 us -> 26.5 us
  Pallas kernels: 0 us -> 24.3 us
  starting transfers between devices: 46 us -> 23.3 us
  between operations: 20.6 us -> 0.76 us
  loops' own time: 9.81 us -> 0 us
    all_to_all x8 -> x3, waiting for transfers between devices: 168 us -> 13.5 us  [all_to_all(): return lax.all_to_all(value, AXES, split_axis=0, concat_axis=0, tiled=True)]
    psum x2 -> x0, waiting for transfers between devices: 59.7 us -> none  [the longest x1 33.1 us: shards(): summed_global = lax.psum(global_acc, 'ctx')]
    dot_general x14 -> x0, matrix products: 37.5 us -> none  [the longest x4 8.58 us: scores_of(): jnp.einsum('hjqd,hjkd->hjqk', query_rows, gathered[..., :HD], preferred_e...]
    ppermute x4, waiting for transfers between devices: 0.97 us -> 29.5 us  [shifted(): return lax.ppermute(value, ('heads', 'ctx'), pairs)]
    all_to_all x0 -> x1, blocking collectives: none -> 26.5 us  [all_to_all(): return lax.all_to_all(value, AXES, split_axis=0, concat_axis=0, tiled=True)]
    all_to_all x8 -> x3, starting transfers between devices: 38.8 us -> 12.6 us  [all_to_all(): return lax.all_to_all(value, AXES, split_axis=0, concat_axis=0, tiled=True)]
    concatenate x11 -> x0, local copies, waits for them, and re-layouts: 25.6 us -> none  [the longest x2 25.2 us: backward_step(): jnp.concatenate([key_grads, value_grads], axis=3)]
    scatter-add x8 -> x0, other arithmetic: 25.5 us -> none  [the longest x1 9.11 us: shards(): own_blocks = own_blocks.at[:, send_local.reshape(-1)].add(returned)]
  transfers between devices with their start and end apart: 14 -> 7, of which waited for: 9 -> 6; matrix products, arithmetic and copies ran while one was open for 12% -> 1% of each run, Pallas kernels for 0% -> 4%
where the time goes in v1:
time: 138 us; the launch traced here: 137 us
  waiting for transfers between devices  43 us (31%)
  blocking collectives  26.5 us (19%)
  Pallas kernels  24.3 us (18%)
  starting transfers between devices  23.3 us (17%)
  local copies, waits for them, and re-layouts  19.3 us (14%)
    ppermute x4, waiting for transfers between devices, shifted(): return lax.ppermute(value, ('heads', 'ctx'), pairs)  29.5 us
    all_to_all x1, blocking collectives, all_to_all(): return lax.all_to_all(value, AXES, split_axis=0, concat_axis=0, tiled=True)  26.5 us
    unnamed x33, local copies, waits for them, and re-layouts  19.3 us
    all_to_all x3, waiting for transfers between devices, all_to_all(): return lax.all_to_all(value, AXES, split_axis=0, concat_axis=0, tiled=True)  13.5 us
    pallas_call x1, Pallas kernels, shards(): pl.pallas_call(scores_kernel, grid_spec=pltpu.PrefetchScalarGridSpec(num_...  13.2 us
    all_to_all x3, starting transfers between devices, all_to_all(): return lax.all_to_all(value, AXES, split_axis=0, concat_axis=0, tiled=True)  12.6 us
    ppermute x4, starting transfers between devices, shifted(): return lax.ppermute(value, ('heads', 'ctx'), pairs)  10.7 us
    pallas_call x1, Pallas kernels, shards(): pl.pallas_call(outputs_kernel, grid=(KVH,), in_specs=[token, token, block...  6.04 us
  transfers between devices with their start and end apart: 7, of which 6 were waited for; matrix products, arithmetic and copies ran while one was open for 1% of the time, Pallas kernels for 4%

profile of v1, /device:TPU:0, one launch (start us, length us, event | category | flops | bytes accessed | tf_op | source)
XLA Modules:
  0.0 137.2 jit_solution(15651734654720883344)
XLA Ops:
  0.6 0.0 copy-start.12
  0.6 0.9 copy-done.12
  1.5 0.0 copy-start.13
  1.5 0.9 copy-done.13
  2.4 0.8 pack.1.own_ref
  3.2 7.3 %all-to-all-start = ((bf16[32,32,128]{2,1,0:T(8,128)(2,1)}), bf16[32,32,128]{2,1,0:T(8,128)(2,1)S(1)}, u32[]{:S(2)}, u32[]{:S(2)}) async-start(bf16[32,32,128]{2,1,0:T(8,128)(2,1)} %bitcast), calls=%async_computation | async-start | bytes 524288 | tf_op jit(solution)/shard_map/all_to_all | solution.py:35
  10.5 0.7 copy.10.rand_ref
  11.2 9.9 %all-to-all-done.in_ref = bf16[32,32,128]{2,1,0:T(8,128)(2,1)S(1)} async-done(((bf16[32,32,128]{2,1,0:T(8,128)(2,1)}), bf16[32,32,128]{2,1,0:T(8,128)(2,1)S(1)}, u32[]{:S(2)}, u32[]{:S(2)}) %all-to-all-start) | async-done | bytes 262176 | tf_op jit(solution)/shard_map/all_to_all | solution.py:35
  21.1 0.0 copy-start.14
  21.1 0.7 copy-done.14
  21.8 0.0 copy-start.7
  21.8 1.8 %select.1 = bf16[32,3,32,128]{3,2,1,0:T(8,128)(2,1)} custom-call(s32[32,1]{1,0:T(8,128)S(1)} %copy.10.rand_ref, s32[2]{0:T(128)S(1)} %copy-done.14, bf16[32,32,128]{2,1,0:T(8,128)(2,1)S(1)} %all-to-all-done.in_ref), custom_call_target="tpu_custom_call" | custom-call | tf_op jit(solution)/shard_map/select/pallas_call | solution.py:79
  23.6 0.0 copy-start.15
  23.6 0.0 copy-start.5
  23.6 2.8 %all-to-all-start.1 = ((bf16[32,3,32,128]{3,2,1,0:T(8,128)(2,1)}), bf16[32,3,32,128]{3,2,1,0:T(8,128)(2,1)S(1)}, u32[]{:S(2)}, u32[]{:S(2)}) async-start(bf16[32,3,32,128]{3,2,1,0:T(8,128)(2,1)} %select.1), calls=%async_computation.1 | async-start | bytes 1572864 | tf_op jit(solution)/shard_map/all_to_all | solution.py:35
  26.3 1.3 collective-permute-start.1
  27.6 4.6 %collective-permute-start = (bf16[2,4,128,128]{3,2,1,0:T(8,128)(2,1)}, bf16[2,4,128,128]{3,2,1,0:T(8,128)(2,1)S(1)}, u32[]{:S(2)}, u32[]{:S(2)}) collective-permute-start(bf16[2,4,128,128]{3,2,1,0:T(8,128)(2,1)} %pack.1.own_ref), channel_id=1, source_target_pairs={{0,4},{4,8},{8,12},{12,16},{16,20},{20,24},{24,28},{28,1},{1,5},{5... | collective-permute-start | bytes 786440 | tf_op jit(solution)/shard_map/ppermute | solution.py:45
  32.2 0.1 add_convert_fusion.edge_ref
  32.3 10.3 %collective-permute-done.1.right_ref = bf16[2,4,128,128]{3,2,1,0:T(8,128)(2,1)S(1)} collective-permute-done((bf16[2,4,128,128]{3,2,1,0:T(8,128)(2,1)}, bf16[2,4,128,128]{3,2,1,0:T(8,128)(2,1)S(1)}, u32[]{:S(2)}, u32[]{:S(2)}) %collective-permute-start.1) | collective-permute-done | bytes 262176 | tf_op jit(solution)/shard_map/ppermute | solution.py:45
  42.6 4.9 %collective-permute-done.left_ref = bf16[2,4,128,128]{3,2,1,0:T(8,128)(2,1)S(1)} collective-permute-done((bf16[2,4,128,128]{3,2,1,0:T(8,128)(2,1)}, bf16[2,4,128,128]{3,2,1,0:T(8,128)(2,1)S(1)}, u32[]{:S(2)}, u32[]{:S(2)}) %collective-permute-start) | collective-permute-done | bytes 262176 | tf_op jit(solution)/shard_map/ppermute | solution.py:45
  47.5 0.0 copy-start.10
  47.5 3.6 %all-to-all-done.1 = bf16[32,3,32,128]{3,2,1,0:T(8,128)(2,1)S(1)} async-done(((bf16[32,3,32,128]{3,2,1,0:T(8,128)(2,1)}), bf16[32,3,32,128]{3,2,1,0:T(8,128)(2,1)S(1)}, u32[]{:S(2)}, u32[]{:S(2)}) %all-to-all-start.1) | async-done | bytes 786464 | tf_op jit(solution)/shard_map/all_to_all | solution.py:35
  51.1 0.0 copy-start.4
  51.1 1.2 copy-done.4
  52.4 0.0 copy-start.6
  52.4 1.2 copy-done.6
  53.6 13.2 %scores.1 = (bf16[4,768,1024]{2,1,0:T(8,128)(2,1)S(1)}, bf16[4,768,1024]{2,1,0:T(8,128)(2,1)S(1)}, bf16[2,16,3,32,128]{4,3,2,1,0:T(8,128)(2,1)S(1)}) custom-call(s32[2]{0:T(128)S(1)} %add_convert_fusion.edge_ref, bf16[128,4096]{1,0:T(8,128)(2,1)S(1)} %copy-done.4, bf16[128,4096]{1,0:T(8,128)(2,1)S(1)} %copy-done.6, bf16[2,4,128,128]{3,2,1,0:T(8,128)(2,1)} %pack.1.own_ref, ...), custom_call_target="tpu_custom_call" | custom-call | flops 2415919104 | bytes 16777216 | tf_op jit(solution)/shard_map/scores/pallas_call | solution.py:268
  66.8 0.0 copy-start
  66.8 2.6 %copy-done = bf16[4,768,1024]{2,1,0:T(8,128)(2,1)} copy-done((bf16[4,768,1024]{2,1,0:T(8,128)(2,1)}, bf16[4,768,1024]{2,1,0:T(8,128)(2,1)S(1)}, u32[]{:S(2)}) %copy-start) | copy-done | bytes 6291480
  69.4 0.0 copy-start.2
  69.4 2.6 %copy-done.2 = bf16[4,768,1024]{2,1,0:T(8,128)(2,1)} copy-done((bf16[4,768,1024]{2,1,0:T(8,128)(2,1)}, bf16[4,768,1024]{2,1,0:T(8,128)(2,1)S(1)}, u32[]{:S(2)}) %copy-start.2) | copy-done | bytes 6291480
  72.0 26.5 %all_to_all.20.in_ref = bf16[32,3,32,128]{3,2,1,0:T(8,128)(2,1)S(1)} all-to-all(bf16[32,3,32,128]{3,2,1,0:T(8,128)(2,1)S(1)} %bitcast.9), channel_id=1, replica_groups=mesh['heads'=8,'ctx'=4] {'ctx','heads'}, dimensions={0} | all-to-all | bytes 1572864 | tf_op jit(solution)/shard_map/all_to_all | solution.py:35
  98.5 0.0 copy-done.15
  98.5 1.7 %combine.1 = bf16[32,32,128]{2,1,0:T(8,128)(2,1)} custom-call(s32[32,1]{1,0:T(8,128)S(1)} %copy.10.rand_ref, s32[2]{0:T(128)S(1)} %copy-done.15, bf16[32,3,32,128]{3,2,1,0:T(8,128)(2,1)S(1)} %all_to_all.20.in_ref), custom_call_target="tpu_custom_call" | custom-call | tf_op jit(solution)/shard_map/combine/pallas_call | solution.py:113
  100.2 0.0 copy-done.10
  100.2 2.6 %all-to-all-start.3 = ((bf16[32,32,128]{2,1,0:T(8,128)(2,1)}), bf16[32,32,128]{2,1,0:T(8,128)(2,1)S(1)}, u32[]{:S(2)}, u32[]{:S(2)}) async-start(bf16[32,32,128]{2,1,0:T(8,128)(2,1)} %combine.1), calls=%async_computation.3 | async-start | bytes 524288 | tf_op jit(solution)/shard_map/all_to_all | solution.py:35
  102.8 0.0 copy-done.7
  102.8 0.0 copy-done.5
  102.8 0.0 copy-start.1
  102.8 2.8 %copy-done.1 = bf16[4,768,1024]{2,1,0:T(8,128)(2,1)S(1)} copy-done((bf16[4,768,1024]{2,1,0:T(8,128)(2,1)S(1)}, bf16[4,768,1024]{2,1,0:T(8,128)(2,1)}, u32[]{:S(2)}) %copy-start.1) | copy-done | bytes 6291480
  105.6 0.0 copy-start.3
  105.6 2.8 %copy-done.3 = bf16[4,768,1024]{2,1,0:T(8,128)(2,1)S(1)} copy-done((bf16[4,768,1024]{2,1,0:T(8,128)(2,1)S(1)}, bf16[4,768,1024]{2,1,0:T(8,128)(2,1)}, u32[]{:S(2)}) %copy-start.3) | copy-done | bytes 6291480
  108.4 0.0 copy-start.11
  108.4 0.9 copy-done.11
  109.4 6.0 %outputs.1 = (bf16[128,4096]{1,0:T(8,128)(2,1)}, bf16[128,4096]{1,0:T(8,128)(2,1)}, bf16[2,4,128,128]{3,2,1,0:T(8,128)(2,1)S(1)}, bf16[2,4,128,128]{3,2,1,0:T(8,128)(2,1)S(1)}, f32[2,4,128,128]{3,2,1,0:T(8,128)S(1)}) custom-call(bf16[128,4096]{1,0:T(8,128)(2,1)S(1)} %copy-done.5, bf16[128,4096]{1,0:T(8,128)(2,1)S(1)} %copy-done.7, ...), custom_call_target="tpu_custom_call" | custom-call | flops 2415919104 | bytes 18874368 | tf_op jit(solution)/shard_map/outputs/pallas_call | solution.py:294
  115.4 0.0 copy-start.8
  115.4 0.8 copy-done.8
  116.2 3.5 %collective-permute-start.2 = (bf16[2,4,128,128]{3,2,1,0:T(8,128)(2,1)S(1)}, bf16[2,4,128,128]{3,2,1,0:T(8,128)(2,1)S(1)}, u32[]{:S(2)}, u32[]{:S(2)}) collective-permute-start(bf16[2,4,128,128]{3,2,1,0:T(8,128)(2,1)S(1)} %get-tuple-element.19), channel_id=1, source_target_pairs={{0,4},{4,8},{8,12},{12,16},{16,20},{20,24},{24,28},{28,1},{1,5},{5... | collective-permute-start | bytes 786440 | tf_op jit(solution)/shard_map/ppermute | solution.py:45
  119.8 1.3 collective-permute-start.3
  121.1 10.2 %collective-permute-done.2.left_ref = bf16[2,4,128,128]{3,2,1,0:T(8,128)(2,1)S(1)} collective-permute-done((bf16[2,4,128,128]{3,2,1,0:T(8,128)(2,1)S(1)}, bf16[2,4,128,128]{3,2,1,0:T(8,128)(2,1)S(1)}, u32[]{:S(2)}, u32[]{:S(2)}) %collective-permute-start.2) | collective-permute-done | bytes 262176 | tf_op jit(solution)/shard_map/ppermute | solution.py:45
  131.2 4.1 %collective-permute-done.3.right_ref = bf16[2,4,128,128]{3,2,1,0:T(8,128)(2,1)S(1)} collective-permute-done((bf16[2,4,128,128]{3,2,1,0:T(8,128)(2,1)S(1)}, bf16[2,4,128,128]{3,2,1,0:T(8,128)(2,1)S(1)}, u32[]{:S(2)}, u32[]{:S(2)}) %collective-permute-start.3) | collective-permute-done | bytes 262176 | tf_op jit(solution)/shard_map/ppermute | solution.py:45
  135.3 0.0 all-to-all-done.3
  135.3 0.0 copy-start.9
  135.3 1.0 copy-done.9
  136.4 0.8 finish.1
Async XLA Ops:
  0.6 0.9 copy-start.12
  1.5 0.9 copy-start.13
  3.2 18.0 %all-to-all-start = ((bf16[32,32,128]{2,1,0:T(8,128)(2,1)}), bf16[32,32,128]{2,1,0:T(8,128)(2,1)S(1)}, u32[]{:S(2)}, u32[]{:S(2)}) async-start(bf16[32,32,128]{2,1,0:T(8,128)(2,1)} %bitcast), calls=%async_computation | async-start | bytes 524288 | tf_op jit(solution)/shard_map/all_to_all | solution.py:35
  21.1 0.7 copy-start.14
  21.8 81.0 %copy-start.7 = (bf16[128,4096]{1,0:T(8,128)(2,1)S(1)}, bf16[128,4096]{1,0:T(8,128)(2,1)}, u32[]{:S(2)}) copy-start(bf16[128,4096]{1,0:T(8,128)(2,1)} %do_ref.3) | copy-start | bytes 3145732
  23.6 74.9 %copy-start.15 = (s32[2]{0:T(128)S(1)}, s32[2]{0:T(128)}, u32[]{:S(2)}) copy-start(s32[2]{0:T(128)} %glob_ref.3) | copy-start | bytes 28
  23.6 79.2 %copy-start.5 = (bf16[128,4096]{1,0:T(8,128)(2,1)S(1)}, bf16[128,4096]{1,0:T(8,128)(2,1)}, u32[]{:S(2)}) copy-start(bf16[128,4096]{1,0:T(8,128)(2,1)} %q_ref.3) | copy-start | bytes 3145732
  23.6 27.5 %all-to-all-start.1 = ((bf16[32,3,32,128]{3,2,1,0:T(8,128)(2,1)}), bf16[32,3,32,128]{3,2,1,0:T(8,128)(2,1)S(1)}, u32[]{:S(2)}, u32[]{:S(2)}) async-start(bf16[32,3,32,128]{3,2,1,0:T(8,128)(2,1)} %select.1), calls=%async_computation.1 | async-start | bytes 1572864 | tf_op jit(solution)/shard_map/all_to_all | solution.py:35
  26.3 16.3 %collective-permute-start.1 = (bf16[2,4,128,128]{3,2,1,0:T(8,128)(2,1)}, bf16[2,4,128,128]{3,2,1,0:T(8,128)(2,1)S(1)}, u32[]{:S(2)}, u32[]{:S(2)}) collective-permute-start(bf16[2,4,128,128]{3,2,1,0:T(8,128)(2,1)} %pack.1.own_ref), channel_id=1, source_target_pairs={{4,0},{8,4},{12,8},{16,12},{20,16},{24,20},{28,24},{1,28},{5,1},{9... | collective-permute-start | bytes 786440 | tf_op jit(solution)/shard_map/ppermute | solution.py:45
  27.6 19.9 %collective-permute-start = (bf16[2,4,128,128]{3,2,1,0:T(8,128)(2,1)}, bf16[2,4,128,128]{3,2,1,0:T(8,128)(2,1)S(1)}, u32[]{:S(2)}, u32[]{:S(2)}) collective-permute-start(bf16[2,4,128,128]{3,2,1,0:T(8,128)(2,1)} %pack.1.own_ref), channel_id=1, source_target_pairs={{0,4},{4,8},{8,12},{12,16},{16,20},{20,24},{24,28},{28,1},{1,5},{5... | collective-permute-start | bytes 786440 | tf_op jit(solution)/shard_map/ppermute | solution.py:45
  47.5 52.7 %copy-start.10 = (bf16[2,4,128,128]{3,2,1,0:T(8,128)(2,1)}, bf16[2,4,128,128]{3,2,1,0:T(8,128)(2,1)S(1)}, u32[]{:S(2)}) copy-start(bf16[2,4,128,128]{3,2,1,0:T(8,128)(2,1)S(1)} %collective-permute-done.left_ref) | copy-start | bytes 786436
  51.1 1.2 copy-start.4
  52.4 1.2 copy-start.6
  66.8 2.6 %copy-start = (bf16[4,768,1024]{2,1,0:T(8,128)(2,1)}, bf16[4,768,1024]{2,1,0:T(8,128)(2,1)S(1)}, u32[]{:S(2)}) copy-start(bf16[4,768,1024]{2,1,0:T(8,128)(2,1)S(1)} %get-tuple-element.14.probs_ref) | copy-start | bytes 18874372
  69.4 2.6 %copy-start.2 = (bf16[4,768,1024]{2,1,0:T(8,128)(2,1)}, bf16[4,768,1024]{2,1,0:T(8,128)(2,1)S(1)}, u32[]{:S(2)}) copy-start(bf16[4,768,1024]{2,1,0:T(8,128)(2,1)S(1)} %get-tuple-element.15.ds_ref) | copy-start | bytes 18874372
  100.2 35.1 %all-to-all-start.3 = ((bf16[32,32,128]{2,1,0:T(8,128)(2,1)}), bf16[32,32,128]{2,1,0:T(8,128)(2,1)S(1)}, u32[]{:S(2)}, u32[]{:S(2)}) async-start(bf16[32,32,128]{2,1,0:T(8,128)(2,1)} %combine.1), calls=%async_computation.3 | async-start | bytes 524288 | tf_op jit(solution)/shard_map/all_to_all | solution.py:35
  102.8 2.8 %copy-start.1 = (bf16[4,768,1024]{2,1,0:T(8,128)(2,1)S(1)}, bf16[4,768,1024]{2,1,0:T(8,128)(2,1)}, u32[]{:S(2)}) copy-start(bf16[4,768,1024]{2,1,0:T(8,128)(2,1)} %copy-done) | copy-start | bytes 18874372
  105.6 2.8 %copy-start.3 = (bf16[4,768,1024]{2,1,0:T(8,128)(2,1)S(1)}, bf16[4,768,1024]{2,1,0:T(8,128)(2,1)}, u32[]{:S(2)}) copy-start(bf16[4,768,1024]{2,1,0:T(8,128)(2,1)} %copy-done.2) | copy-start | bytes 18874372
  108.4 0.9 copy-start.11
  115.4 0.8 copy-start.8
  116.2 15.0 %collective-permute-start.2 = (bf16[2,4,128,128]{3,2,1,0:T(8,128)(2,1)S(1)}, bf16[2,4,128,128]{3,2,1,0:T(8,128)(2,1)S(1)}, u32[]{:S(2)}, u32[]{:S(2)}) collective-permute-start(bf16[2,4,128,128]{3,2,1,0:T(8,128)(2,1)S(1)} %get-tuple-element.19), channel_id=1, source_target_pairs={{0,4},{4,8},{8,12},{12,16},{16,20},{20,24},{24,28},{28,1},{1,5},{5... | collective-permute-start | bytes 786440 | tf_op jit(solution)/shard_map/ppermute | solution.py:45
  119.8 15.6 %collective-permute-start.3 = (bf16[2,4,128,128]{3,2,1,0:T(8,128)(2,1)S(1)}, bf16[2,4,128,128]{3,2,1,0:T(8,128)(2,1)S(1)}, u32[]{:S(2)}, u32[]{:S(2)}) collective-permute-start(bf16[2,4,128,128]{3,2,1,0:T(8,128)(2,1)S(1)} %get-tuple-element.20), channel_id=1, source_target_pairs={{4,0},{8,4},{12,8},{16,12},{20,16},{24,20},{28,24},{1,28},{5,1},{9... | collective-permute-start | bytes 786440 | tf_op jit(solution)/shard_map/ppermute | solution.py:45
  135.3 1.0 copy-start.9

commit v2 on v1

--- a/solution.py
+++ b/solution.py
@@ -279,7 +279,7 @@
             square_shape,
             jax.ShapeDtypeStruct(far.shape, BF16),
         ),
-        compiler_params=params(32, dimension_semantics=("arbitrary",)),
+        compiler_params=params(56, dimension_semantics=("arbitrary",)),
         cost_estimate=pl.CostEstimate(
             flops=3 * flops, bytes_accessed=16 << 20, transcendentals=H * BLK * SLOTS * BLK
         ),
@@ -303,12 +303,13 @@
             block_shape,
             jax.ShapeDtypeStruct((2, KVH, BLK, HD), F32),
         ),
-        compiler_params=params(32, dimension_semantics=("arbitrary",)),
+        compiler_params=params(56, dimension_semantics=("arbitrary",)),
         cost_estimate=pl.CostEstimate(
             flops=3 * flops, bytes_accessed=18 << 20, transcendentals=0
         ),
         name="outputs",
     )(queries, cotangent, packed, left, right, far, probs, ds)
+    arrived, to_left, to_right = lax.optimization_barrier((arrived, to_left, to_right))
     from_right = shifted(to_left, -1)
     from_left = shifted(to_right, 1)
     summed = combine(rand_blocks, glob_blocks, arrived)

time: 138 us -> 120 us (0.87)
  blocking collectives: 26.5 us -> 0 us
  local copies, waits for them, and re-layouts: 19.3 us -> 5.19 us
  waiting for transfers between devices: 43 us -> 55.8 us
  Pallas kernels: 24.3 us -> 29.3 us
  starting transfers between devices: 23.3 us -> 27.9 us
    all_to_all x1 -> x0, blocking collectives: 26.5 us -> none  [all_to_all(): return lax.all_to_all(value, AXES, split_axis=0, concat_axis=0, tiled=True)]
    unnamed x33 -> x17, local copies, waits for them, and re-layouts: 19.3 us -> 5.19 us
    all_to_all x3 -> x4, waiting for transfers between devices: 13.5 us -> 26.3 us  [all_to_all(): return lax.all_to_all(value, AXES, split_axis=0, concat_axis=0, tiled=True)]
    all_to_all x3 -> x4, starting transfers between devices: 12.6 us -> 17.2 us  [all_to_all(): return lax.all_to_all(value, AXES, split_axis=0, concat_axis=0, tiled=True)]
    pallas_call x1, Pallas kernels: 6.04 us -> 9.16 us  [shards(): pl.pallas_call(outputs_kernel, grid=(KVH,), in_specs=[token, token, block...]
    pallas_call x1, Pallas kernels: 13.2 us -> 15.1 us  [shards(): pl.pallas_call(scores_kernel, grid_spec=pltpu.PrefetchScalarGridSpec(num_...]
  transfers between devices with their start and end apart: 7 -> 8, of which waited for: 6 -> 7; matrix products, arithmetic and copies ran while one was open for 1% -> 1% of each run, Pallas kernels for 4% -> 8%
where the time goes in v2:
time: 120 us; the launch traced here: 119 us
  waiting for transfers between devices  55.8 us (46%)
  Pallas kernels  29.3 us (24%)
  starting transfers between devices  27.9 us (23%)
  local copies, waits for them, and re-layouts  5.19 us (4%)
    ppermute x4, waiting for transfers between devices, shifted(): return lax.ppermute(value, ('heads', 'ctx'), pairs)  29.5 us
    all_to_all x4, waiting for transfers between devices, all_to_all(): return lax.all_to_all(value, AXES, split_axis=0, concat_axis=0, tiled=True)  26.3 us
    all_to_all x4, starting transfers between devices, all_to_all(): return lax.all_to_all(value, AXES, split_axis=0, concat_axis=0, tiled=True)  17.2 us
    pallas_call x1, Pallas kernels, shards(): pl.pallas_call(scores_kernel, grid_spec=pltpu.PrefetchScalarGridSpec(num_...  15.1 us
    ppermute x4, starting transfers between devices, shifted(): return lax.ppermute(value, ('heads', 'ctx'), pairs)  10.7 us
    pallas_call x1, Pallas kernels, shards(): pl.pallas_call(outputs_kernel, grid=(KVH,), in_specs=[token, token, block...  9.16 us
    unnamed x17, local copies, waits for them, and re-layouts  5.19 us
  transfers between devices with their start and end apart: 8, of which 7 were waited for; matrix products, arithmetic and copies ran while one was open for 1% of the time, Pallas kernels for 8%

profile of v2, /device:TPU:0, one launch (start us, length us, event | category | flops | bytes accessed | tf_op | source)
XLA Modules:
  0.0 119.4 jit_solution(3324442420217214649)
XLA Ops:
  0.6 0.0 copy-start.1
  0.6 0.9 copy-done.1
  1.5 0.0 copy-start.2
  1.5 0.9 copy-done.2
  2.4 0.8 pack.1.own_ref
  3.2 7.3 %all-to-all-start = ((bf16[32,32,128]{2,1,0:T(8,128)(2,1)}), bf16[32,32,128]{2,1,0:T(8,128)(2,1)S(1)}, u32[]{:S(2)}, u32[]{:S(2)}) async-start(bf16[32,32,128]{2,1,0:T(8,128)(2,1)} %bitcast), calls=%async_computation | async-start | bytes 524288 | tf_op jit(solution)/shard_map/all_to_all | solution.py:35
  10.5 0.7 copy.10.rand_ref
  11.2 9.9 %all-to-all-done.in_ref = bf16[32,32,128]{2,1,0:T(8,128)(2,1)S(1)} async-done(((bf16[32,32,128]{2,1,0:T(8,128)(2,1)}), bf16[32,32,128]{2,1,0:T(8,128)(2,1)S(1)}, u32[]{:S(2)}, u32[]{:S(2)}) %all-to-all-start) | async-done | bytes 262176 | tf_op jit(solution)/shard_map/all_to_all | solution.py:35
  21.2 0.0 copy-start.3
  21.2 0.7 copy-done.3
  21.8 1.8 %select.1 = bf16[32,3,32,128]{3,2,1,0:T(8,128)(2,1)} custom-call(s32[32,1]{1,0:T(8,128)S(1)} %copy.10.rand_ref, s32[2]{0:T(128)S(1)} %copy-done.3, bf16[32,32,128]{2,1,0:T(8,128)(2,1)S(1)} %all-to-all-done.in_ref), custom_call_target="tpu_custom_call" | custom-call | tf_op jit(solution)/shard_map/select/pallas_call | solution.py:79
  23.6 2.6 %all-to-all-start.1 = ((bf16[32,3,32,128]{3,2,1,0:T(8,128)(2,1)}), bf16[32,3,32,128]{3,2,1,0:T(8,128)(2,1)S(1)}, u32[]{:S(2)}, u32[]{:S(2)}) async-start(bf16[32,3,32,128]{3,2,1,0:T(8,128)(2,1)} %select.1), calls=%async_computation.1 | async-start | bytes 1572864 | tf_op jit(solution)/shard_map/all_to_all | solution.py:35
  26.2 1.3 %collective-permute-start.1 = (bf16[2,4,128,128]{3,2,1,0:T(8,128)(2,1)}, bf16[2,4,128,128]{3,2,1,0:T(8,128)(2,1)S(1)}, u32[]{:S(2)}, u32[]{:S(2)}) collective-permute-start(bf16[2,4,128,128]{3,2,1,0:T(8,128)(2,1)} %pack.1.own_ref), channel_id=1, source_target_pairs={{4,0},{8,4},{12,8},{16,12},{20,16},{24,20},{28,24},{1,28},{5,1},{9... | collective-permute-start | bytes 786440 | tf_op jit(solution)/shard_map/ppermute | solution.py:45
  27.5 4.6 %collective-permute-start = (bf16[2,4,128,128]{3,2,1,0:T(8,128)(2,1)}, bf16[2,4,128,128]{3,2,1,0:T(8,128)(2,1)S(1)}, u32[]{:S(2)}, u32[]{:S(2)}) collective-permute-start(bf16[2,4,128,128]{3,2,1,0:T(8,128)(2,1)} %pack.1.own_ref), channel_id=1, source_target_pairs={{0,4},{4,8},{8,12},{12,16},{16,20},{20,24},{24,28},{28,1},{1,5},{5... | collective-permute-start | bytes 786440 | tf_op jit(solution)/shard_map/ppermute | solution.py:45
  32.1 0.6 add_convert_fusion.edge_ref
  32.7 9.8 %collective-permute-done.1.right_ref = bf16[2,4,128,128]{3,2,1,0:T(8,128)(2,1)S(1)} collective-permute-done((bf16[2,4,128,128]{3,2,1,0:T(8,128)(2,1)}, bf16[2,4,128,128]{3,2,1,0:T(8,128)(2,1)S(1)}, u32[]{:S(2)}, u32[]{:S(2)}) %collective-permute-start.1) | collective-permute-done | bytes 262176 | tf_op jit(solution)/shard_map/ppermute | solution.py:45
  42.5 0.0 copy-start.6
  42.5 4.9 %collective-permute-done.left_ref = bf16[2,4,128,128]{3,2,1,0:T(8,128)(2,1)S(1)} collective-permute-done((bf16[2,4,128,128]{3,2,1,0:T(8,128)(2,1)}, bf16[2,4,128,128]{3,2,1,0:T(8,128)(2,1)S(1)}, u32[]{:S(2)}, u32[]{:S(2)}) %collective-permute-start) | collective-permute-done | bytes 262176 | tf_op jit(solution)/shard_map/ppermute | solution.py:45
  47.4 0.0 copy-start.7
  47.4 3.6 %all-to-all-done.1 = bf16[32,3,32,128]{3,2,1,0:T(8,128)(2,1)S(1)} async-done(((bf16[32,3,32,128]{3,2,1,0:T(8,128)(2,1)}), bf16[32,3,32,128]{3,2,1,0:T(8,128)(2,1)S(1)}, u32[]{:S(2)}, u32[]{:S(2)}) %all-to-all-start.1) | async-done | bytes 786464 | tf_op jit(solution)/shard_map/all_to_all | solution.py:35
  51.0 0.0 copy-start.5
  51.0 0.0 copy-done.6
  51.0 0.0 copy-done.7
  51.0 0.9 copy-done.5
  51.9 15.1 %scores.1 = (bf16[4,768,1024]{2,1,0:T(8,128)(2,1)}, bf16[4,768,1024]{2,1,0:T(8,128)(2,1)}, bf16[2,16,3,32,128]{4,3,2,1,0:T(8,128)(2,1)}) custom-call(s32[2]{0:T(128)} %add_convert_fusion.edge_ref, bf16[128,4096]{1,0:T(8,128)(2,1)} %q_ref.3, bf16[128,4096]{1,0:T(8,128)(2,1)} %do_ref.3, bf16[2,4,128,128]{3,2,1,0:T(8,128)(2,1)} %pack.1.own_ref, ...), custom_call_target="tpu_custom_call" | custom-call | flops 2415919104 | bytes 16777216 | tf_op jit(solution)/shard_map/scores/pallas_call | solution.py:268
  67.0 4.7 %all-to-all-start.2 = ((bf16[32,3,32,128]{3,2,1,0:T(8,128)(2,1)}), bf16[32,3,32,128]{3,2,1,0:T(8,128)(2,1)S(1)}, u32[]{:S(2)}, u32[]{:S(2)}) async-start(bf16[32,3,32,128]{3,2,1,0:T(8,128)(2,1)} %bitcast.9), calls=%async_computation.2 | async-start | bytes 1572864 | tf_op jit(solution)/shard_map/all_to_all | solution.py:35
  71.7 0.0 copy-start.4
  71.7 9.2 %outputs.1 = (bf16[128,4096]{1,0:T(8,128)(2,1)}, bf16[128,4096]{1,0:T(8,128)(2,1)}, bf16[2,4,128,128]{3,2,1,0:T(8,128)(2,1)}, bf16[2,4,128,128]{3,2,1,0:T(8,128)(2,1)}, f32[2,4,128,128]{3,2,1,0:T(8,128)}) custom-call(bf16[128,4096]{1,0:T(8,128)(2,1)} %q_ref.3, bf16[128,4096]{1,0:T(8,128)(2,1)} %do_ref.3, bf16[2,4,128,128]{3,2,1,0:T(8,128)(2,1)} %pack.1.own_ref, ...), custom_call_target="tpu_custom_call" | custom-call | flops 2415919104 | bytes 18874368 | tf_op jit(solution)/shard_map/outputs/pallas_call | solution.py:294
  80.9 12.8 %all-to-all-done.2.in_ref = bf16[32,3,32,128]{3,2,1,0:T(8,128)(2,1)S(1)} async-done(((bf16[32,3,32,128]{3,2,1,0:T(8,128)(2,1)}), bf16[32,3,32,128]{3,2,1,0:T(8,128)(2,1)S(1)}, u32[]{:S(2)}, u32[]{:S(2)}) %all-to-all-start.2) | async-done | bytes 786464 | tf_op jit(solution)/shard_map/all_to_all | solution.py:35
  93.7 0.0 copy-done.4
  93.7 1.7 %combine.1 = bf16[32,32,128]{2,1,0:T(8,128)(2,1)} custom-call(s32[32,1]{1,0:T(8,128)S(1)} %copy.10.rand_ref, s32[2]{0:T(128)S(1)} %copy-done.4, bf16[32,3,32,128]{3,2,1,0:T(8,128)(2,1)S(1)} %all-to-all-done.2.in_ref), custom_call_target="tpu_custom_call" | custom-call | tf_op jit(solution)/shard_map/combine/pallas_call | solution.py:113
  95.4 2.6 %all-to-all-start.3 = ((bf16[32,32,128]{2,1,0:T(8,128)(2,1)}), bf16[32,32,128]{2,1,0:T(8,128)(2,1)S(1)}, u32[]{:S(2)}, u32[]{:S(2)}) async-start(bf16[32,32,128]{2,1,0:T(8,128)(2,1)} %combine.1), calls=%async_computation.3 | async-start | bytes 524288 | tf_op jit(solution)/shard_map/all_to_all | solution.py:35
  98.0 3.6 %collective-permute-start.2 = (bf16[2,4,128,128]{3,2,1,0:T(8,128)(2,1)}, bf16[2,4,128,128]{3,2,1,0:T(8,128)(2,1)S(1)}, u32[]{:S(2)}, u32[]{:S(2)}) collective-permute-start(bf16[2,4,128,128]{3,2,1,0:T(8,128)(2,1)} %get-tuple-element.25), channel_id=1, source_target_pairs={{0,4},{4,8},{8,12},{12,16},{16,20},{20,24},{24,28},{28,1},{1,5},{5... | collective-permute-start | bytes 786440 | tf_op jit(solution)/shard_map/ppermute | solution.py:45
  101.6 1.3 %collective-permute-start.3 = (bf16[2,4,128,128]{3,2,1,0:T(8,128)(2,1)}, bf16[2,4,128,128]{3,2,1,0:T(8,128)(2,1)S(1)}, u32[]{:S(2)}, u32[]{:S(2)}) collective-permute-start(bf16[2,4,128,128]{3,2,1,0:T(8,128)(2,1)} %get-tuple-element.26), channel_id=1, source_target_pairs={{4,0},{8,4},{12,8},{16,12},{20,16},{24,20},{28,24},{1,28},{5,1},{9... | collective-permute-start | bytes 786440 | tf_op jit(solution)/shard_map/ppermute | solution.py:45
  102.9 11.6 %collective-permute-done.2.left_ref = bf16[2,4,128,128]{3,2,1,0:T(8,128)(2,1)S(1)} collective-permute-done((bf16[2,4,128,128]{3,2,1,0:T(8,128)(2,1)}, bf16[2,4,128,128]{3,2,1,0:T(8,128)(2,1)S(1)}, u32[]{:S(2)}, u32[]{:S(2)}) %collective-permute-start.2) | collective-permute-done | bytes 262176 | tf_op jit(solution)/shard_map/ppermute | solution.py:45
  114.4 3.2 %collective-permute-done.3.right_ref = bf16[2,4,128,128]{3,2,1,0:T(8,128)(2,1)S(1)} collective-permute-done((bf16[2,4,128,128]{3,2,1,0:T(8,128)(2,1)}, bf16[2,4,128,128]{3,2,1,0:T(8,128)(2,1)S(1)}, u32[]{:S(2)}, u32[]{:S(2)}) %collective-permute-start.3) | collective-permute-done | bytes 262176 | tf_op jit(solution)/shard_map/ppermute | solution.py:45
  117.6 0.0 all-to-all-done.3
  117.6 0.0 copy-start
  117.6 1.0 copy-done
  118.7 0.8 finish.1
Async XLA Ops:
  0.6 0.9 copy-start.1
  1.5 0.9 copy-start.2
  3.2 18.0 %all-to-all-start = ((bf16[32,32,128]{2,1,0:T(8,128)(2,1)}), bf16[32,32,128]{2,1,0:T(8,128)(2,1)S(1)}, u32[]{:S(2)}, u32[]{:S(2)}) async-start(bf16[32,32,128]{2,1,0:T(8,128)(2,1)} %bitcast), calls=%async_computation | async-start | bytes 524288 | tf_op jit(solution)/shard_map/all_to_all | solution.py:35
  21.2 0.7 copy-start.3
  23.6 27.4 %all-to-all-start.1 = ((bf16[32,3,32,128]{3,2,1,0:T(8,128)(2,1)}), bf16[32,3,32,128]{3,2,1,0:T(8,128)(2,1)S(1)}, u32[]{:S(2)}, u32[]{:S(2)}) async-start(bf16[32,3,32,128]{3,2,1,0:T(8,128)(2,1)} %select.1), calls=%async_computation.1 | async-start | bytes 1572864 | tf_op jit(solution)/shard_map/all_to_all | solution.py:35
  26.2 16.3 %collective-permute-start.1 = (bf16[2,4,128,128]{3,2,1,0:T(8,128)(2,1)}, bf16[2,4,128,128]{3,2,1,0:T(8,128)(2,1)S(1)}, u32[]{:S(2)}, u32[]{:S(2)}) collective-permute-start(bf16[2,4,128,128]{3,2,1,0:T(8,128)(2,1)} %pack.1.own_ref), channel_id=1, source_target_pairs={{4,0},{8,4},{12,8},{16,12},{20,16},{24,20},{28,24},{1,28},{5,1},{9... | collective-permute-start | bytes 786440 | tf_op jit(solution)/shard_map/ppermute | solution.py:45
  27.5 19.9 %collective-permute-start = (bf16[2,4,128,128]{3,2,1,0:T(8,128)(2,1)}, bf16[2,4,128,128]{3,2,1,0:T(8,128)(2,1)S(1)}, u32[]{:S(2)}, u32[]{:S(2)}) collective-permute-start(bf16[2,4,128,128]{3,2,1,0:T(8,128)(2,1)} %pack.1.own_ref), channel_id=1, source_target_pairs={{0,4},{4,8},{8,12},{12,16},{16,20},{20,24},{24,28},{28,1},{1,5},{5... | collective-permute-start | bytes 786440 | tf_op jit(solution)/shard_map/ppermute | solution.py:45
  42.5 8.5 %copy-start.6 = (bf16[2,4,128,128]{3,2,1,0:T(8,128)(2,1)}, bf16[2,4,128,128]{3,2,1,0:T(8,128)(2,1)S(1)}, u32[]{:S(2)}) copy-start(bf16[2,4,128,128]{3,2,1,0:T(8,128)(2,1)S(1)} %collective-permute-done.1.right_ref) | copy-start | bytes 786436
  47.4 3.6 %copy-start.7 = (bf16[2,4,128,128]{3,2,1,0:T(8,128)(2,1)}, bf16[2,4,128,128]{3,2,1,0:T(8,128)(2,1)S(1)}, u32[]{:S(2)}) copy-start(bf16[2,4,128,128]{3,2,1,0:T(8,128)(2,1)S(1)} %collective-permute-done.left_ref) | copy-start | bytes 786436
  51.0 0.9 copy-start.5
  67.0 26.7 %all-to-all-start.2 = ((bf16[32,3,32,128]{3,2,1,0:T(8,128)(2,1)}), bf16[32,3,32,128]{3,2,1,0:T(8,128)(2,1)S(1)}, u32[]{:S(2)}, u32[]{:S(2)}) async-start(bf16[32,3,32,128]{3,2,1,0:T(8,128)(2,1)} %bitcast.9), calls=%async_computation.2 | async-start | bytes 1572864 | tf_op jit(solution)/shard_map/all_to_all | solution.py:35
  71.7 22.0 %copy-start.4 = (s32[2]{0:T(128)S(1)}, s32[2]{0:T(128)}, u32[]{:S(2)}) copy-start(s32[2]{0:T(128)} %glob_ref.3) | copy-start | bytes 28
  95.4 22.2 %all-to-all-start.3 = ((bf16[32,32,128]{2,1,0:T(8,128)(2,1)}), bf16[32,32,128]{2,1,0:T(8,128)(2,1)S(1)}, u32[]{:S(2)}, u32[]{:S(2)}) async-start(bf16[32,32,128]{2,1,0:T(8,128)(2,1)} %combine.1), calls=%async_computation.3 | async-start | bytes 524288 | tf_op jit(solution)/shard_map/all_to_all | solution.py:35
  98.0 16.5 %collective-permute-start.2 = (bf16[2,4,128,128]{3,2,1,0:T(8,128)(2,1)}, bf16[2,4,128,128]{3,2,1,0:T(8,128)(2,1)S(1)}, u32[]{:S(2)}, u32[]{:S(2)}) collective-permute-start(bf16[2,4,128,128]{3,2,1,0:T(8,128)(2,1)} %get-tuple-element.25), channel_id=1, source_target_pairs={{0,4},{4,8},{8,12},{12,16},{16,20},{20,24},{24,28},{28,1},{1,5},{5... | collective-permute-start | bytes 786440 | tf_op jit(solution)/shard_map/ppermute | solution.py:45
  101.6 16.1 %collective-permute-start.3 = (bf16[2,4,128,128]{3,2,1,0:T(8,128)(2,1)}, bf16[2,4,128,128]{3,2,1,0:T(8,128)(2,1)S(1)}, u32[]{:S(2)}, u32[]{:S(2)}) collective-permute-start(bf16[2,4,128,128]{3,2,1,0:T(8,128)(2,1)} %get-tuple-element.26), channel_id=1, source_target_pairs={{4,0},{8,4},{12,8},{16,12},{20,16},{24,20},{28,24},{1,28},{5,1},{9... | collective-permute-start | bytes 786440 | tf_op jit(solution)/shard_map/ppermute | solution.py:45
  117.6 1.0 copy-start

commit v3 on v1

v3 whole, which is shorter than its diff:
```python
import math

import jax
import jax.numpy as jnp
from jax import lax
from jax.experimental import pallas as pl
from jax.experimental.pallas import tpu as pltpu
from jax.sharding import PartitionSpec as P

HD = 128
H = 32
KVH = 4
BLK = 128
NG = 2
GROUP = H // KVH
SCALE = 1.0 / math.sqrt(HD)
NEG_FILL = -1e30
AXES = ("ctx", "heads")
MATES = 2
GL = KVH // MATES
FAR = MATES + NG
SLOTS = 3 + NG + 1
WIDE = GROUP * BLK
PAIR = 2 * BLK
HALF_ROWS = 2 * GL * BLK
BF16 = jnp.bfloat16
F32 = jnp.float32
NT = (((1,), (1,)), ((), ()))


def params(mib, **kw):
    return pltpu.CompilerParams(vmem_limit_bytes=mib << 20, **kw)


def all_to_all(value):
    return lax.all_to_all(value, AXES, split_axis=0, concat_axis=0, tiled=True)


def mate(value):
    count = lax.axis_size("ctx")
    return lax.ppermute(value, "ctx", [(i, i ^ 1) for i in range(count)])


def neighbour_pairs(step, of_mate):
    heads, ctx = lax.axis_size("heads"), lax.axis_size("ctx")
    pairs = []
    for c in range(ctx):
        for h in range(heads):
            block = (c ^ 1 if of_mate else c) * heads + h + step
            if 0 <= block < heads * ctx:
                source = (block // heads) & ~1 | c & 1
                pairs.append(((block % heads) * ctx + source, h * ctx + c))
    return pairs


def permute(value, pairs):
    return lax.ppermute(value, ("heads", "ctx"), pairs)


def swap(pairs):
    return [(j, i) for i, j in pairs]


MATE, LEFT, RIGHT, LAST, FIRST, CORE = 0, 1, 3, 5, 6, 7


def table_of():
    heads, ctx = lax.axis_size("heads"), lax.axis_size("ctx")
    h, c = lax.axis_index("heads"), lax.axis_index("ctx")
    own, other = c * heads + h, (c ^ 1) * heads + h
    last = heads * ctx - 1
    flags = [
        c & 1,
        own == 0,
        other == 0,
        own == last,
        other == last,
        h == heads - 1,
        h == 0,
    ]
    return jnp.stack([jnp.asarray(f).astype(jnp.int32) for f in flags])


def pack_kernel(k_ref, v_ref, out_ref):
    share = out_ref.shape[0] // (2 * GL)
    for kind, ref in enumerate((k_ref, v_ref)):
        for half in range(MATES):
            for g in range(GL):
                first = (kind * GL + g) * share
                column = (half * GL + g) * HD
                out_ref[first : first + share, half] = ref[
                    :, column : column + HD
                ].reshape(share, BLK // share, HD)


def pack(keys, values, count):
    rows = HALF_ROWS // count
    if rows % 16:
        both = jnp.stack([keys, values]).reshape(2, BLK, MATES, GL, HD)
        both = jnp.transpose(both, (0, 3, 1, 2, 4)).reshape(count, rows, MATES, HD)
        return jnp.transpose(both, (0, 2, 1, 3))
    return pl.pallas_call(
        pack_kernel,
        out_shape=jax.ShapeDtypeStruct((count, MATES, rows, HD), BF16),
        compiler_params=params(8),
        name="pack",
    )(keys, values)


def side_of(i, heads):
    return (i // heads) % MATES


def mate_of(i, heads):
    return (i // heads ^ 1) * heads + i % heads


def select_kernel(heads, table_ref, in_ref, out_ref):
    count = in_ref.shape[0]
    for i in range(count):
        side = side_of(i, heads)
        out_ref[i, 0] = in_ref[table_ref[i], side]
        out_ref[i, 1] = in_ref[table_ref[mate_of(i, heads)], side]
        for slot in range(NG):
            out_ref[i, MATES + slot] = in_ref[table_ref[count + slot], side]


def select(wanted, slices, heads):
    count, _, rows, _ = slices.shape
    if rows % 16:
        i = jnp.arange(count)
        blocks = jnp.stack(
            [wanted[i], wanted[mate_of(i, heads)]]
            + [jnp.broadcast_to(wanted[count + slot], (count,)) for slot in range(NG)],
            axis=1,
        )
        return slices[blocks, side_of(i, heads)[:, None]]
    return pl.pallas_call(
        lambda *refs: select_kernel(heads, *refs),
        out_shape=jax.ShapeDtypeStruct((count, FAR, rows, HD), BF16),
        in_specs=[
            pl.BlockSpec(memory_space=pltpu.SMEM),
            pl.BlockSpec(memory_space=pltpu.VMEM),
        ],
        out_specs=pl.BlockSpec(memory_space=pltpu.VMEM),
        compiler_params=params(8),
        name="select",
    )(wanted, slices)


def combine_kernel(heads, table_ref, in_ref, out_ref, acc_ref):
    count = in_ref.shape[0]
    acc_ref[...] = jnp.zeros_like(acc_ref)
    for slot in range(NG):
        for side in range(MATES):
            total = None
            for i in range(count):
                if side_of(i, heads) == side:
                    term = in_ref[i, MATES + slot].astype(F32)
                    total = term if total is None else total + term
            acc_ref[table_ref[count + slot], side] += total
    for i in range(count):
        side = side_of(i, heads)
        acc_ref[table_ref[i], side] += in_ref[i, 0].astype(F32)
        acc_ref[table_ref[mate_of(i, heads)], side] += in_ref[i, 1].astype(F32)
    out_ref[...] = acc_ref[...].astype(BF16)


def combine(wanted, terms, heads):
    count, _, rows, _ = terms.shape
    if rows % 16:
        i = jnp.arange(count)
        side = side_of(i, heads)
        wide = terms.astype(F32)
        total = jnp.zeros((count, MATES, rows, HD), F32)
        total = total.at[wanted[i], side].add(wide[:, 0])
        total = total.at[wanted[mate_of(i, heads)], side].add(wide[:, 1])
        for slot in range(NG):
            block = jnp.broadcast_to(wanted[count + slot], (count,))
            total = total.at[block, side].add(wide[:, MATES + slot])
        return total.astype(BF16)
    return pl.pallas_call(
        lambda *refs: combine_kernel(heads, *refs),
        out_shape=jax.ShapeDtypeStruct((count, MATES, rows, HD), BF16),
        in_specs=[
            pl.BlockSpec(memory_space=pltpu.SMEM),
            pl.BlockSpec(memory_space=pltpu.VMEM),
        ],
        out_specs=pl.BlockSpec(memory_space=pltpu.VMEM),
        scratch_shapes=[pltpu.VMEM((count, MATES, rows, HD), F32)],
        compiler_params=params(16),
        name="combine",
    )(wanted, terms)


def send_kernel(table_ref, k_ref, v_ref, mk_ref, mv_ref, *out_refs):
    first = table_ref[MATE] * GL
    for g in range(GL):
        cols = pl.ds(pl.multiple_of((first + g) * HD, HD), HD)
        for kind, (own, other) in enumerate(((k_ref, mk_ref), (v_ref, mv_ref))):
            a, b = own[:, cols], other[:, cols]
            for flag, dest in ((LAST, 0), (FIRST, 2)):
                crossed = table_ref[flag] != 0
                out_refs[dest][kind, g] = jnp.where(crossed, b, a)
                out_refs[dest + 1][kind, g] = jnp.where(crossed, a, b)


def send(table, keys, values, mate_keys, mate_values):
    shape = jax.ShapeDtypeStruct((2, GL, BLK, HD), BF16)
    vmem = pl.BlockSpec(memory_space=pltpu.VMEM)
    return pl.pallas_call(
        send_kernel,
        out_shape=(shape,) * 4,
        in_specs=[pl.BlockSpec(memory_space=pltpu.SMEM)] + [vmem] * 4,
        out_specs=(vmem,) * 4,
        compiler_params=params(8),
        name="send",
    )(table, keys, values, mate_keys, mate_values)


def stacked(value):
    return jnp.concatenate(
        [value[:, h * HD : (h + 1) * HD] for h in range(GROUP)], axis=0
    )


def chosen(s, own, other):
    return jnp.where(s == 0, own, other)


def blocks_of(kind, s, own, other, left, mate_left, right, mate_right, far_ref):
    blocks = [
        chosen(s, left[kind, 0], mate_left[kind, 0]),
        chosen(s, own[...], other[...]),
        chosen(s, right[kind, 0], mate_right[kind, 0]),
    ]
    for slot in range(NG):
        blocks.append(far_ref[kind, 0, :, MATES + slot].reshape(BLK, HD))
    blocks.append(far_ref[kind, 0, :, s].reshape(BLK, HD))
    return blocks


def grads_of(b, queries, douts, probs_ref, ds_ref):
    rows = slice(b * BLK, (b + 1) * BLK)
    dk = jnp.dot(ds_ref[0, 0, rows], queries, preferred_element_type=F32) * SCALE
    dv = jnp.dot(probs_ref[0, 0, rows], douts, preferred_element_type=F32)
    return dk, dv


def scores_kernel(
    table_ref, q_ref, mq_ref, do_ref, mdo_ref, k_ref, mk_ref, v_ref, mv_ref,
    left, mate_left, right, mate_right, far_ref,
    probs_ref, ds_ref, terms_ref, s_ref, dp_ref, glob_ref,
):
    s = pl.program_id(1)
    near = (left, mate_left, right, mate_right, far_ref)
    keys = blocks_of(0, s, k_ref, mk_ref, *near)
    values = blocks_of(1, s, v_ref, mv_ref, *near)
    queries = stacked(chosen(s, q_ref[...], mq_ref[...]))
    douts = stacked(chosen(s, do_ref[...], mdo_ref[...]))
    outside = {0: table_ref[LEFT + s] != 0, 2: table_ref[RIGHT + s] != 0}
    factor = SCALE / math.log(2.0)
    for pair in range(WIDE // PAIR):
        cols = slice(pair * PAIR, (pair + 1) * PAIR)
        q, do = queries[cols], douts[cols]
        row_max = None
        for b in range(SLOTS):
            score = lax.dot_general(keys[b], q, NT, preferred_element_type=F32)
            if b in outside:
                score = jnp.where(outside[b], NEG_FILL, score)
            s_ref[b * BLK : (b + 1) * BLK] = score
            top = jnp.max(score, axis=0, keepdims=True)
            row_max = top if row_max is None else jnp.maximum(row_max, top)
        row_sum = jnp.zeros((1, PAIR), F32)
        centre = jnp.zeros((1, PAIR), F32)
        for b in range(SLOTS):
            rows = slice(b * BLK, (b + 1) * BLK)
            w = jnp.exp2((s_ref[rows] - row_max) * factor)
            dp = lax.dot_general(values[b], do, NT, preferred_element_type=F32)
            s_ref[rows] = w
            dp_ref[rows] = dp
            row_sum = row_sum + jnp.sum(w, axis=0, keepdims=True)
            centre = centre + jnp.sum(w * dp, axis=0, keepdims=True)
        inverse = 1.0 / row_sum
        centre = centre * inverse
        for b in range(SLOTS):
            rows = slice(b * BLK, (b + 1) * BLK)
            p = s_ref[rows] * inverse
            probs_ref[0, 0, rows, cols] = p.astype(BF16)
            ds_ref[0, 0, rows, cols] = (p * (dp_ref[rows] - centre)).astype(BF16)
    share = terms_ref.shape[2]

    def put(slot, pair):
        for kind, term in enumerate(pair):
            terms_ref[kind, 0, :, slot] = term.astype(BF16).reshape(
                share, BLK // share, HD
            )

    put(s, grads_of(5, queries, douts, probs_ref, ds_ref))
    globs = [grads_of(3 + slot, queries, douts, probs_ref, ds_ref) for slot in range(NG)]

    @pl.when(s == 0)
    def _():
        for slot in range(NG):
            for kind in range(2):
                glob_ref[slot, kind] = globs[slot][kind]

    @pl.when(s == 1)
    def _():
        for slot in range(NG):
            put(MATES + slot, [globs[slot][kind] + glob_ref[slot, kind] for kind in range(2)])


def outputs_kernel(
    table_ref, q_ref, mq_ref, do_ref, mdo_ref, k_ref, mk_ref, v_ref, mv_ref,
    left, mate_left, right, mate_right, far_ref, probs_ref, ds_ref,
    out_ref, mate_out_ref, dq_ref, mate_dq_ref,
    to_left, mate_to_left, to_right, mate_to_right, near_ref, both_ref,
):
    s = pl.program_id(1)
    near = (left, mate_left, right, mate_right, far_ref)
    keys_t, values_t = (
        jnp.concatenate([x.T for x in blocks_of(kind, s, own, other, *near)], axis=1)
        for kind, own, other in ((0, k_ref, mk_ref), (1, v_ref, mv_ref))
    )
    for pair in range(WIDE // PAIR):
        cols = slice(pair * PAIR, (pair + 1) * PAIR)
        out_t = jnp.dot(values_t, probs_ref[0, 0, :, cols], preferred_element_type=F32)
        dq_t = jnp.dot(keys_t, ds_ref[0, 0, :, cols], preferred_element_type=F32) * SCALE
        for half in range(2):
            part = slice(half * HD, (half + 1) * HD)
            dest = slice(pair * PAIR + half * HD, pair * PAIR + (half + 1) * HD)
            both_ref[0, :, dest] = out_t[:, part].T.astype(BF16)
            both_ref[1, :, dest] = dq_t[:, part].T.astype(BF16)
    queries = stacked(chosen(s, q_ref[...], mq_ref[...]))
    douts = stacked(chosen(s, do_ref[...], mdo_ref[...]))
    terms = [grads_of(b, queries, douts, probs_ref, ds_ref) for b in range(3)]
    for kind in range(2):
        near_ref[0, kind, 0] = terms[1][kind]

    def write(out, dq, to_left, to_right):
        out[...] = both_ref[0]
        dq[...] = both_ref[1]
        for kind in range(2):
            to_left[kind, 0] = terms[0][kind].astype(BF16)
            to_right[kind, 0] = terms[2][kind].astype(BF16)

    @pl.when(s == 0)
    def _():
        write(out_ref, dq_ref, to_left, to_right)

    @pl.when(s == 1)
    def _():
        write(mate_out_ref, mate_dq_ref, mate_to_left, mate_to_right)


def merge_kernel(table_ref, near_ref, lo, lm, ro, rm, own_ref, other_ref):
    last, first = table_ref[LAST] != 0, table_ref[FIRST] != 0
    a, b, c, d = (ref[...].astype(F32) for ref in (lo, lm, ro, rm))
    own_ref[...] = near_ref[0] + jnp.where(last, b, a) + jnp.where(first, d, c)
    other_ref[...] = near_ref[1] + jnp.where(last, a, b) + jnp.where(first, c, d)


def merge(table, near, terms):
    shape = jax.ShapeDtypeStruct((2, GL, BLK, HD), F32)
    vmem = pl.BlockSpec(memory_space=pltpu.VMEM)
    return pl.pallas_call(
        merge_kernel,
        out_shape=(shape, shape),
        in_specs=[pl.BlockSpec(memory_space=pltpu.SMEM)] + [vmem] * 5,
        out_specs=(vmem, vmem),
        compiler_params=params(16),
        name="merge",
    )(table, near, *terms)


def finish_kernel(table_ref, own_ref, other_ref, far_ref, dk_ref, dv_ref):
    mine = table_ref[MATE]
    share = far_ref.shape[2]
    for kind, dest in enumerate((dk_ref, dv_ref)):
        for half in range(MATES):
            for g in range(GL):
                near = jnp.where(mine == half, own_ref[kind, g], other_ref[kind, g])
                far = far_ref[kind, g, :, half].reshape(BLK, HD).astype(F32)
                column = (half * GL + g) * HD
                dest[:, column : column + HD] = (near + far).astype(BF16)


def finish(table, own, other, far):
    shape = jax.ShapeDtypeStruct((BLK, KVH * HD), BF16)
    vmem = pl.BlockSpec(memory_space=pltpu.VMEM)
    return pl.pallas_call(
        finish_kernel,
        out_shape=(shape, shape),
        in_specs=[pl.BlockSpec(memory_space=pltpu.SMEM)] + [vmem] * 3,
        out_specs=(vmem, vmem),
        compiler_params=params(8),
        name="finish",
    )(table, own, other, far)


def shards(queries, keys_in, values_in, cotangent, rand_blocks, glob_blocks):
    heads = lax.axis_size("heads")
    count = heads * lax.axis_size("ctx")
    rows = HALF_ROWS // count
    plain = rows % 16 == 0
    share = BLK // rows if plain else 1
    table = table_of()
    wanted = jnp.concatenate([rand_blocks[:, 0], glob_blocks])

    slices = all_to_all(pack(keys_in, values_in, count))
    mate_keys, mate_values = mate(keys_in), mate(values_in)
    mate_queries, mate_cotangent = mate(queries), mate(cotangent)
    sent = send(table, keys_in, values_in, mate_keys, mate_values)
    routes = [neighbour_pairs(step, of_mate) for step in (-1, 1) for of_mate in (False, True)]
    near = [permute(value, pairs) for value, pairs in zip(sent, routes)]
    far = all_to_all(select(wanted, slices, heads))
    if not plain:
        far = far.reshape(2, GL, BLK // rows, FAR, rows, HD)
        far = jnp.transpose(far, (0, 1, 3, 2, 4, 5))
    far = far.reshape(2, GL, share, FAR, BLK // share, HD)

    token = pl.BlockSpec((BLK, WIDE), lambda g, s, t: (0, t[MATE] * GL + g))
    token_half = pl.BlockSpec((BLK, WIDE), lambda g, s, t: (0, g))
    key = pl.BlockSpec((BLK, HD), lambda g, s, t: (0, t[MATE] * GL + g))
    block = pl.BlockSpec((2, 1, BLK, HD), lambda g, s, t: (0, g, 0, 0))
    far_spec = pl.BlockSpec(
        (2, 1, share, FAR, BLK // share, HD), lambda g, s, t: (0, g, 0, 0, 0, 0)
    )
    square = pl.BlockSpec((1, 1, SLOTS * BLK, WIDE), lambda g, s, t: (g, s, 0, 0))
    square_shape = jax.ShapeDtypeStruct((GL, MATES, SLOTS * BLK, WIDE), BF16)
    block_shape = jax.ShapeDtypeStruct((2, GL, BLK, HD), BF16)
    token_shape = jax.ShapeDtypeStruct(queries.shape, BF16)
    half_shape = jax.ShapeDtypeStruct((BLK, GL * WIDE), BF16)
    flops = 2 * H * BLK * SLOTS * BLK * HD
    operands = (
        table, queries, mate_queries, cotangent, mate_cotangent,
        keys_in, mate_keys, values_in, mate_values, *near, far,
    )
    in_specs = [token] * 4 + [key] * 4 + [block] * 4 + [far_spec]
    order = ("arbitrary", "arbitrary")
    probs, ds, terms = pl.pallas_call(
        scores_kernel,
        grid_spec=pltpu.PrefetchScalarGridSpec(
            num_scalar_prefetch=1,
            grid=(GL, MATES),
            in_specs=in_specs,
            out_specs=[square, square, far_spec],
            scratch_shapes=[pltpu.VMEM((SLOTS * BLK, PAIR), F32)] * 2
            + [pltpu.VMEM((NG, 2, BLK, HD), F32)],
        ),
        out_shape=(square_shape, square_shape, jax.ShapeDtypeStruct(far.shape, BF16)),
        compiler_params=params(56, dimension_semantics=order),
        cost_estimate=pl.CostEstimate(
            flops=3 * flops, bytes_accessed=16 << 20, transcendentals=H * BLK * SLOTS * BLK
        ),
        name="scores",
    )(*operands)
    if not plain:
        terms = jnp.transpose(
            terms.reshape(2, GL, FAR, BLK // rows, rows, HD), (0, 1, 3, 2, 4, 5)
        )
    arrived = all_to_all(terms.reshape(count, FAR, rows, HD))
    near_spec = pl.BlockSpec((1, 2, 1, BLK, HD), lambda g, s, t: (s, 0, g, 0, 0))
    out, mate_out, dq, mate_dq, *back, near_grads = pl.pallas_call(
        outputs_kernel,
        grid_spec=pltpu.PrefetchScalarGridSpec(
            num_scalar_prefetch=1,
            grid=(GL, MATES),
            in_specs=in_specs + [square, square],
            out_specs=[token, token_half, token, token_half] + [block] * 4 + [near_spec],
            scratch_shapes=[pltpu.VMEM((2, BLK, WIDE), BF16)],
        ),
        out_shape=(token_shape, half_shape, token_shape, half_shape)
        + (block_shape,) * 4
        + (jax.ShapeDtypeStruct((MATES, 2, GL, BLK, HD), F32),),
        compiler_params=params(56, dimension_semantics=order),
        cost_estimate=pl.CostEstimate(
            flops=3 * flops, bytes_accessed=18 << 20, transcendentals=0
        ),
        name="outputs",
    )(*operands, probs, ds)
    back = [permute(value, swap(pairs)) for value, pairs in zip(back, routes)]
    other_column = (1 - table[MATE]) * (GL * WIDE)
    attn_out = lax.dynamic_update_slice(out, mate(mate_out), (0, other_column))
    grad_query = lax.dynamic_update_slice(dq, mate(mate_dq), (0, other_column))
    arrived, *back = lax.optimization_barrier((arrived, *back))
    own_grads, mate_grads = merge(table, near_grads, back)
    other_grads = mate(mate_grads)
    returned = all_to_all(combine(wanted, arrived, heads))
    if not plain:
        returned = returned.reshape(2, GL, BLK // rows, MATES, rows, HD)
        returned = jnp.transpose(returned, (0, 1, 3, 2, 4, 5))
    returned = returned.reshape(2, GL, share, MATES, BLK // share, HD)
    grad_keys, grad_values = finish(table, own_grads, other_grads, returned)
    return attn_out, grad_query, grad_keys, grad_values


def solution(mesh):
    spec = P(AXES, None)
    return jax.shard_map(
        shards,
        mesh=mesh,
        in_specs=(spec, spec, spec, spec, P(), P()),
        out_specs=(spec, spec, spec, spec),
        check_vma=False,
    )
```

time: 138 us -> 122 us (0.88)
  blocking collectives: 26.5 us -> 0 us
  starting transfers between devices: 23.3 us -> 47.7 us
  waiting for transfers between devices: 43 us -> 31.1 us
  local copies, waits for them, and re-layouts: 19.3 us -> 7.54 us
  Pallas kernels: 24.3 us -> 33.3 us
    all_to_all x1 -> x0, blocking collectives: 26.5 us -> none  [all_to_all(): return lax.all_to_all(value, AXES, split_axis=0, concat_axis=0, tiled=True)]
    ppermute x4 -> x15, starting transfers between devices: 10.7 us -> 29.4 us  [the longest x8 22.4 us: permute(): return lax.ppermute(value, ('heads', 'ctx'), pairs)]
    ppermute x4 -> x15, waiting for transfers between devices: 29.5 us -> 14.9 us  [the longest x8 13.7 us: permute(): return lax.ppermute(value, ('heads', 'ctx'), pairs)]
    unnamed x33 -> x30, local copies, waits for them, and re-layouts: 19.3 us -> 5.79 us
    pallas_call x5 -> x7, Pallas kernels: 11.1 us -> 17.2 us  [the longest x1 11 us: shards(): pl.pallas_call(outputs_kernel, grid_spec=pltpu.PrefetchScalarGridSpec(num...]
    all_to_all x3 -> x4, starting transfers between devices: 12.6 us -> 18.3 us  [all_to_all(): return lax.all_to_all(value, AXES, split_axis=0, concat_axis=0, tiled=True)]
    pallas_call x1, Pallas kernels: 13.2 us -> 16.1 us  [shards(): pl.pallas_call(scores_kernel, grid_spec=pltpu.PrefetchScalarGridSpec(num_...]
    all_to_all x3 -> x4, waiting for transfers between devices: 13.5 us -> 16.2 us  [all_to_all(): return lax.all_to_all(value, AXES, split_axis=0, concat_axis=0, tiled=True)]
  transfers between devices with their start and end apart: 7 -> 19, of which waited for: 6 -> 8; matrix products, arithmetic and copies ran while one was open for 1% -> 2% of each run, Pallas kernels for 4% -> 12%
where the time goes in v3:
time: 122 us; the launch traced here: 121 us
  starting transfers between devices  47.7 us (39%)
  Pallas kernels  33.3 us (27%)
  waiting for transfers between devices  31.1 us (25%)
  local copies, waits for them, and re-layouts  7.54 us (6%)
    ppermute x8, starting transfers between devices, permute(): return lax.ppermute(value, ('heads', 'ctx'), pairs)  22.4 us
    all_to_all x4, starting transfers between devices, all_to_all(): return lax.all_to_all(value, AXES, split_axis=0, concat_axis=0, tiled=True)  18.3 us
    all_to_all x4, waiting for transfers between devices, all_to_all(): return lax.all_to_all(value, AXES, split_axis=0, concat_axis=0, tiled=True)  16.2 us
    pallas_call x1, Pallas kernels, shards(): pl.pallas_call(scores_kernel, grid_spec=pltpu.PrefetchScalarGridSpec(num_...  16.1 us
    ppermute x8, waiting for transfers between devices, permute(): return lax.ppermute(value, ('heads', 'ctx'), pairs)  13.7 us
    pallas_call x1, Pallas kernels, shards(): pl.pallas_call(outputs_kernel, grid_spec=pltpu.PrefetchScalarGridSpec(num...  11 us
    ppermute x7, starting transfers between devices, mate(): return lax.ppermute(value, 'ctx', [(i, i ^ 1) for i in range(count)])  6.97 us
    unnamed x30, local copies, waits for them, and re-layouts  5.79 us
  transfers between devices with their start and end apart: 19, of which 8 were waited for; matrix products, arithmetic and copies ran while one was open for 2% of the time, Pallas kernels for 12%

profile of v3, /device:TPU:0, one launch (start us, length us, event | category | flops | bytes accessed | tf_op | source)
XLA Modules:
  0.0 121.3 jit_solution(16047169705625986527)
XLA Ops:
  0.6 0.0 copy-start
  0.6 0.9 copy-done
  1.5 0.9 copy-done.2
  2.4 0.7 pack.1
  3.2 7.3 %all-to-all-start = ((bf16[32,2,16,128]{3,2,1,0:T(8,128)(2,1)}), bf16[32,2,16,128]{3,2,1,0:T(8,128)(2,1)S(1)}, u32[]{:S(2)}, u32[]{:S(2)}) async-start(bf16[32,2,16,128]{3,2,1,0:T(8,128)(2,1)} %pack.1), calls=%async_computation | async-start | bytes 524288 | tf_op jit(solution)/shard_map/all_to_all | solution.py:36
  10.5 0.3 collective-permute-start
  10.8 0.3 collective-permute-start.1
  11.1 0.7 pad_add_fusion.refs_0_
  11.8 9.3 %all-to-all-done.refs_1_ = bf16[32,2,16,128]{3,2,1,0:T(8,128)(2,1)S(1)} async-done(((bf16[32,2,16,128]{3,2,1,0:T(8,128)(2,1)}), bf16[32,2,16,128]{3,2,1,0:T(8,128)(2,1)S(1)}, u32[]{:S(2)}, u32[]{:S(2)}) %all-to-all-start) | async-done | bytes 262176 | tf_op jit(solution)/shard_map/all_to_all | solution.py:36
  21.1 1.4 %select.1 = bf16[32,4,16,128]{3,2,1,0:T(8,128)(2,1)} custom-call(s32[34]{0:T(128)S(1)} %pad_add_fusion.refs_0_, bf16[32,2,16,128]{3,2,1,0:T(8,128)(2,1)S(1)} %all-to-all-done.refs_1_), custom_call_target="tpu_custom_call" | custom-call | tf_op jit(solution)/shard_map/select/pallas_call | solution.py:138
  22.5 2.6 %all-to-all-start.1 = ((bf16[32,4,16,128]{3,2,1,0:T(8,128)(2,1)}), bf16[32,4,16,128]{3,2,1,0:T(8,128)(2,1)S(1)}, u32[]{:S(2)}, u32[]{:S(2)}) async-start(bf16[32,4,16,128]{3,2,1,0:T(8,128)(2,1)} %select.1), calls=%async_computation.1 | async-start | bytes 1048576 | tf_op jit(solution)/shard_map/all_to_all | solution.py:36
  25.1 0.2 collective-permute-start.2
  25.3 0.4 collective-permute-start.3
  25.7 0.1 stack.55.table_ref
  25.8 1.0 collective-permute-done.2.mk_ref
  26.8 0.2 collective-permute-done.3.mv_ref
  26.9 0.9 copy-done.1
  27.8 0.9 copy-done.3
  28.8 0.6 send.1
  29.4 3.5 %collective-permute-start.4 = (bf16[2,2,128,128]{3,2,1,0:T(8,128)(2,1)S(1)}, bf16[2,2,128,128]{3,2,1,0:T(8,128)(2,1)S(1)}, u32[]{:S(2)}, u32[]{:S(2)}) collective-permute-start(bf16[2,2,128,128]{3,2,1,0:T(8,128)(2,1)S(1)} %get-tuple-element.29), channel_id=1, source_target_pairs={{0,4},{4,8},{8,12},{12,16},{16,20},{20,24},{24,28},{29,1},{1,5},{5... | collective-permute-start | bytes 393224 | tf_op jit(solution)/shard_map/ppermute | solution.py:57
  32.9 3.4 %collective-permute-start.5 = (bf16[2,2,128,128]{3,2,1,0:T(8,128)(2,1)S(1)}, bf16[2,2,128,128]{3,2,1,0:T(8,128)(2,1)S(1)}, u32[]{:S(2)}, u32[]{:S(2)}) collective-permute-start(bf16[2,2,128,128]{3,2,1,0:T(8,128)(2,1)S(1)} %get-tuple-element.30), channel_id=1, source_target_pairs={{28,0},{0,4},{4,8},{8,12},{12,16},{16,20},{20,24},{24,28},{1,5},{5... | collective-permute-start | bytes 393224 | tf_op jit(solution)/shard_map/ppermute | solution.py:57
  36.4 5.1 %collective-permute-start.6 = (bf16[2,2,128,128]{3,2,1,0:T(8,128)(2,1)S(1)}, bf16[2,2,128,128]{3,2,1,0:T(8,128)(2,1)S(1)}, u32[]{:S(2)}, u32[]{:S(2)}) collective-permute-start(bf16[2,2,128,128]{3,2,1,0:T(8,128)(2,1)S(1)} %get-tuple-element.31), channel_id=1, source_target_pairs={{4,0},{8,4},{12,8},{16,12},{20,16},{24,20},{28,24},{0,28},{5,1},{9... | collective-permute-start | bytes 393224 | tf_op jit(solution)/shard_map/ppermute | solution.py:57
  41.5 0.0 collective-permute-done.4.left
  41.5 1.3 %collective-permute-start.7 = (bf16[2,2,128,128]{3,2,1,0:T(8,128)(2,1)S(1)}, bf16[2,2,128,128]{3,2,1,0:T(8,128)(2,1)S(1)}, u32[]{:S(2)}, u32[]{:S(2)}) collective-permute-start(bf16[2,2,128,128]{3,2,1,0:T(8,128)(2,1)S(1)} %get-tuple-element.32), channel_id=1, source_target_pairs={{4,0},{8,4},{12,8},{16,12},{20,16},{24,20},{28,24},{2,28},{5,1},{9... | collective-permute-start | bytes 393224 | tf_op jit(solution)/shard_map/ppermute | solution.py:57
  42.8 2.1 %collective-permute-done.5.mate_left = bf16[2,2,128,128]{3,2,1,0:T(8,128)(2,1)S(1)} collective-permute-done((bf16[2,2,128,128]{3,2,1,0:T(8,128)(2,1)S(1)}, bf16[2,2,128,128]{3,2,1,0:T(8,128)(2,1)S(1)}, u32[]{:S(2)}, u32[]{:S(2)}) %collective-permute-start.5) | collective-permute-done | bytes 131104 | tf_op jit(solution)/shard_map/ppermute | solution.py:57
  44.9 3.1 %collective-permute-done.6.right = bf16[2,2,128,128]{3,2,1,0:T(8,128)(2,1)S(1)} collective-permute-done((bf16[2,2,128,128]{3,2,1,0:T(8,128)(2,1)S(1)}, bf16[2,2,128,128]{3,2,1,0:T(8,128)(2,1)S(1)}, u32[]{:S(2)}, u32[]{:S(2)}) %collective-permute-start.6) | collective-permute-done | bytes 131104 | tf_op jit(solution)/shard_map/ppermute | solution.py:57
  48.1 2.7 %collective-permute-done.7.mate_right = bf16[2,2,128,128]{3,2,1,0:T(8,128)(2,1)S(1)} collective-permute-done((bf16[2,2,128,128]{3,2,1,0:T(8,128)(2,1)S(1)}, bf16[2,2,128,128]{3,2,1,0:T(8,128)(2,1)S(1)}, u32[]{:S(2)}, u32[]{:S(2)}) %collective-permute-start.7) | collective-permute-done | bytes 131104 | tf_op jit(solution)/shard_map/ppermute | solution.py:57
  50.8 0.0 collective-permute-done.mq_ref
  50.8 0.0 collective-permute-done.1.mdo_ref
  50.8 0.0 all-to-all-done.1
  50.8 0.0 copy-start.9
  50.8 0.0 copy-done.7
  50.8 0.0 copy-done.4
  50.8 0.0 copy-done.5
  50.8 0.0 copy-done.11
  50.9 0.6 copy-done.14
  51.4 0.4 copy-done.10
  51.8 0.1 copy-done.9
  52.0 16.1 %scores.1 = (bf16[2,2,768,1024]{3,2,1,0:T(8,128)(2,1)}, bf16[2,2,768,1024]{3,2,1,0:T(8,128)(2,1)}, bf16[2,2,8,4,16,128]{5,4,3,2,1,0:T(8,128)(2,1)}) custom-call(s32[7]{0:T(128)} %copy-done.7, bf16[128,4096]{1,0:T(8,128)(2,1)} %q_ref.3, bf16[128,4096]{1,0:T(8,128)(2,1)} %copy-done.10, bf16[128,4096]{1,0:T(8,128)(2,1)} %do_ref.3, ...), custom_call_target="tpu_custom_call" | custom-call | flops 2415919104 | bytes 16777216 | tf_op jit(solution)/shard_map/scores/pallas_call | solution.py:442
  68.1 3.6 %all-to-all-start.2 = ((bf16[32,4,16,128]{3,2,1,0:T(8,128)(2,1)}), bf16[32,4,16,128]{3,2,1,0:T(8,128)(2,1)S(1)}, u32[]{:S(2)}, u32[]{:S(2)}) async-start(bf16[32,4,16,128]{3,2,1,0:T(8,128)(2,1)} %bitcast.14), calls=%async_computation.2 | async-start | bytes 1048576 | tf_op jit(solution)/shard_map/all_to_all | solution.py:36
  71.6 11.0 %outputs.1 = (bf16[128,4096]{1,0:T(8,128)(2,1)}, bf16[128,2048]{1,0:T(8,128)(2,1)}, bf16[128,4096]{1,0:T(8,128)(2,1)}, bf16[128,2048]{1,0:T(8,128)(2,1)}, bf16[2...) custom-call(s32[7]{0:T(128)} %copy-done.7, ...), custom_call_target="tpu_custom_call" | custom-call | flops 2415919104 | bytes 18874368 | tf_op jit(solution)/shard_map/outputs/pallas_call | solution.py:465
  82.6 0.3 collective-permute-start.8
  82.9 1.3 %collective-permute-start.10 = (bf16[2,2,128,128]{3,2,1,0:T(8,128)(2,1)}, bf16[2,2,128,128]{3,2,1,0:T(8,128)(2,1)S(1)}, u32[]{:S(2)}, u32[]{:S(2)}) collective-permute-start(bf16[2,2,128,128]{3,2,1,0:T(8,128)(2,1)} %get-tuple-element.41), channel_id=1, source_target_pairs={{4,0},{8,4},{12,8},{16,12},{20,16},{24,20},{28,24},{1,29},{5,1},{9... | collective-permute-start | bytes 393224 | tf_op jit(solution)/shard_map/ppermute | solution.py:57
  84.2 5.2 %collective-permute-start.9 = (bf16[128,2048]{1,0:T(8,128)(2,1)}, bf16[128,2048]{1,0:T(8,128)(2,1)S(1)}, u32[]{:S(2)}, u32[]{:S(2)}) collective-permute-start(bf16[128,2048]{1,0:T(8,128)(2,1)} %get-tuple-element.38), channel_id=1, source_target_pairs={{0,1},{1,0},{2,3},{3,2},{4,5},{5,4},{6,7},{7,6},{8,9},{9,8},{10,11... | collective-permute-start | bytes 1572872 | tf_op jit(solution)/shard_map/ppermute | solution.py:41
  89.4 2.4 %collective-permute-start.11 = (bf16[2,2,128,128]{3,2,1,0:T(8,128)(2,1)}, bf16[2,2,128,128]{3,2,1,0:T(8,128)(2,1)S(1)}, u32[]{:S(2)}, u32[]{:S(2)}) collective-permute-start(bf16[2,2,128,128]{3,2,1,0:T(8,128)(2,1)} %get-tuple-element.42), channel_id=1, source_target_pairs={{0,28},{4,0},{8,4},{12,8},{16,12},{20,16},{24,20},{28,24},{5,1},{9... | collective-permute-start | bytes 393224 | tf_op jit(solution)/shard_map/ppermute | solution.py:57
  91.9 3.4 %collective-permute-start.12 = (bf16[2,2,128,128]{3,2,1,0:T(8,128)(2,1)}, bf16[2,2,128,128]{3,2,1,0:T(8,128)(2,1)S(1)}, u32[]{:S(2)}, u32[]{:S(2)}) collective-permute-start(bf16[2,2,128,128]{3,2,1,0:T(8,128)(2,1)} %get-tuple-element.43), channel_id=1, source_target_pairs={{0,4},{4,8},{8,12},{12,16},{16,20},{20,24},{24,28},{28,0},{1,5},{5... | collective-permute-start | bytes 393224 | tf_op jit(solution)/shard_map/ppermute | solution.py:57
  95.3 0.0 collective-permute-done.10.lo
  95.3 1.9 %collective-permute-start.13 = (bf16[2,2,128,128]{3,2,1,0:T(8,128)(2,1)}, bf16[2,2,128,128]{3,2,1,0:T(8,128)(2,1)S(1)}, u32[]{:S(2)}, u32[]{:S(2)}) collective-permute-start(bf16[2,2,128,128]{3,2,1,0:T(8,128)(2,1)} %get-tuple-element.44), channel_id=1, source_target_pairs={{0,4},{4,8},{8,12},{12,16},{16,20},{20,24},{24,28},{28,2},{1,5},{5... | collective-permute-start | bytes 393224 | tf_op jit(solution)/shard_map/ppermute | solution.py:57
  97.2 0.0 collective-permute-done.11.lm
  97.2 5.7 %collective-permute-done.12.ro = bf16[2,2,128,128]{3,2,1,0:T(8,128)(2,1)S(1)} collective-permute-done((bf16[2,2,128,128]{3,2,1,0:T(8,128)(2,1)}, bf16[2,2,128,128]{3,2,1,0:T(8,128)(2,1)S(1)}, u32[]{:S(2)}, u32[]{:S(2)}) %collective-permute-start.12) | collective-permute-done | bytes 131104 | tf_op jit(solution)/shard_map/ppermute | solution.py:57
  102.9 0.0 collective-permute-done.13.rm
  102.9 0.0 all-to-all-done.2.refs_1_
  102.9 1.5 %combine.1 = bf16[32,2,16,128]{3,2,1,0:T(8,128)(2,1)} custom-call(s32[34]{0:T(128)S(1)} %pad_add_fusion.refs_0_, bf16[32,4,16,128]{3,2,1,0:T(8,128)(2,1)S(1)} %all-to-all-done.2.refs_1_), custom_call_target="tpu_custom_call" | custom-call | tf_op jit(solution)/shard_map/combine/pallas_call | solution.py:182
  104.5 4.9 %all-to-all-start.3 = ((bf16[32,2,16,128]{3,2,1,0:T(8,128)(2,1)}), bf16[32,2,16,128]{3,2,1,0:T(8,128)(2,1)S(1)}, u32[]{:S(2)}, u32[]{:S(2)}) async-start(bf16[32,2,16,128]{3,2,1,0:T(8,128)(2,1)} %combine.1), calls=%async_computation.3 | async-start | bytes 524288 | tf_op jit(solution)/shard_map/all_to_all | solution.py:36
  109.4 1.0 copy-done.6
  110.4 0.7 merge.1
  111.1 0.3 collective-permute-start.14
  111.4 0.0 collective-permute-done.8
  111.4 0.8 constant_dynamic-update-slice_fusion.1
  112.3 0.0 collective-permute-done.9
  112.3 0.8 constant_dynamic-update-slice_fusion
  113.1 0.0 collective-permute-done.14.other_ref
  113.1 6.9 %all-to-all-done.3 = bf16[32,2,16,128]{3,2,1,0:T(8,128)(2,1)S(1)} async-done(((bf16[32,2,16,128]{3,2,1,0:T(8,128)(2,1)}), bf16[32,2,16,128]{3,2,1,0:T(8,128)(2,1)S(1)}, u32[]{:S(2)}, u32[]{:S(2)}) %all-to-all-start.3) | async-done | bytes 262176 | tf_op jit(solution)/shard_map/all_to_all | solution.py:36
  120.0 1.3 %finish.1 = (bf16[128,512]{1,0:T(8,128)(2,1)}, bf16[128,512]{1,0:T(8,128)(2,1)}) custom-call(s32[7]{0:T(128)S(1)} %copy-done.8, f32[2,2,128,128]{3,2,1,0:T(8,128)S(1)} %get-tuple-element.49.own_ref, f32[2,2,128,128]{3,2,1,0:T(8,128)S(1)} %collective-permute-done.14.other_ref, bf16[2,2,8,2,16,128]{5,4,3,2,1,0:T(8,128)(2,1)S(1)} %bitcast.11), custom_call_target="tpu_custom_call" | custom-call | tf_op jit(solution)/shard_map/finish/pallas_call | solution.py:392
  (16 shorter events, 0.0 us)
Async XLA Ops:
  0.6 0.9 copy-start
  1.5 0.9 copy-start.2
  3.2 18.0 %all-to-all-start = ((bf16[32,2,16,128]{3,2,1,0:T(8,128)(2,1)}), bf16[32,2,16,128]{3,2,1,0:T(8,128)(2,1)S(1)}, u32[]{:S(2)}, u32[]{:S(2)}) async-start(bf16[32,2,16,128]{3,2,1,0:T(8,128)(2,1)} %pack.1), calls=%async_computation | async-start | bytes 524288 | tf_op jit(solution)/shard_map/all_to_all | solution.py:36
  10.5 40.3 %collective-permute-start = (bf16[128,4096]{1,0:T(8,128)(2,1)}, bf16[128,4096]{1,0:T(8,128)(2,1)S(1)}, u32[]{:S(2)}, u32[]{:S(2)}) collective-permute-start(bf16[128,4096]{1,0:T(8,128)(2,1)} %q_ref.3), channel_id=1, source_target_pairs={{0,1},{1,0},{2,3},{3,2},{4,5},{5,4},{6,7},{7,6},{8,9},{9,8},{10,11... | collective-permute-start | bytes 3145736 | tf_op jit(solution)/shard_map/ppermute | solution.py:41
  10.8 40.0 %collective-permute-start.1 = (bf16[128,4096]{1,0:T(8,128)(2,1)}, bf16[128,4096]{1,0:T(8,128)(2,1)}, u32[]{:S(2)}, u32[]{:S(2)}) collective-permute-start(bf16[128,4096]{1,0:T(8,128)(2,1)} %do_ref.3), channel_id=1, source_target_pairs={{0,1},{1,0},{2,3},{3,2},{4,5},{5,4},{6,7},{7,6},{8,9},{9,8},{10,11... | collective-permute-start | bytes 3145736 | tf_op jit(solution)/shard_map/ppermute | solution.py:41
  22.5 28.3 %all-to-all-start.1 = ((bf16[32,4,16,128]{3,2,1,0:T(8,128)(2,1)}), bf16[32,4,16,128]{3,2,1,0:T(8,128)(2,1)S(1)}, u32[]{:S(2)}, u32[]{:S(2)}) async-start(bf16[32,4,16,128]{3,2,1,0:T(8,128)(2,1)} %select.1), calls=%async_computation.1 | async-start | bytes 1048576 | tf_op jit(solution)/shard_map/all_to_all | solution.py:36
  25.1 1.6 %collective-permute-start.2 = (bf16[128,512]{1,0:T(8,128)(2,1)}, bf16[128,512]{1,0:T(8,128)(2,1)S(1)}, u32[]{:S(2)}, u32[]{:S(2)}) collective-permute-start(bf16[128,512]{1,0:T(8,128)(2,1)} %k_ref.7), channel_id=1, source_target_pairs={{0,1},{1,0},{2,3},{3,2},{4,5},{5,4},{6,7},{7,6},{8,9},{9,8},{10,11... | collective-permute-start | bytes 393224 | tf_op jit(solution)/shard_map/ppermute | solution.py:41
  25.3 1.6 %collective-permute-start.3 = (bf16[128,512]{1,0:T(8,128)(2,1)}, bf16[128,512]{1,0:T(8,128)(2,1)S(1)}, u32[]{:S(2)}, u32[]{:S(2)}) collective-permute-start(bf16[128,512]{1,0:T(8,128)(2,1)} %v_ref.7), channel_id=1, source_target_pairs={{0,1},{1,0},{2,3},{3,2},{4,5},{5,4},{6,7},{7,6},{8,9},{9,8},{10,11... | collective-permute-start | bytes 393224 | tf_op jit(solution)/shard_map/ppermute | solution.py:41
  25.8 25.0 %copy-start.7 = (s32[7]{0:T(128)}, s32[7]{0:T(128)S(1)}, u32[]{:S(2)}) copy-start(s32[7]{0:T(128)S(1)} %stack.55.table_ref) | copy-start | bytes 88
  26.8 24.1 %copy-start.4 = (bf16[128,512]{1,0:T(8,128)(2,1)}, bf16[128,512]{1,0:T(8,128)(2,1)S(1)}, u32[]{:S(2)}) copy-start(bf16[128,512]{1,0:T(8,128)(2,1)S(1)} %collective-permute-done.2.mk_ref) | copy-start | bytes 393220
  26.9 0.9 copy-start.1
  27.8 0.9 copy-start.3
  28.8 22.1 %copy-start.5 = (bf16[128,512]{1,0:T(8,128)(2,1)}, bf16[128,512]{1,0:T(8,128)(2,1)S(1)}, u32[]{:S(2)}) copy-start(bf16[128,512]{1,0:T(8,128)(2,1)S(1)} %collective-permute-done.3.mv_ref) | copy-start | bytes 393220
  29.4 12.1 %collective-permute-start.4 = (bf16[2,2,128,128]{3,2,1,0:T(8,128)(2,1)S(1)}, bf16[2,2,128,128]{3,2,1,0:T(8,128)(2,1)S(1)}, u32[]{:S(2)}, u32[]{:S(2)}) collective-permute-start(bf16[2,2,128,128]{3,2,1,0:T(8,128)(2,1)S(1)} %get-tuple-element.29), channel_id=1, source_target_pairs={{0,4},{4,8},{8,12},{12,16},{16,20},{20,24},{24,28},{29,1},{1,5},{5... | collective-permute-start | bytes 393224 | tf_op jit(solution)/shard_map/ppermute | solution.py:57
  32.9 12.0 %collective-permute-start.5 = (bf16[2,2,128,128]{3,2,1,0:T(8,128)(2,1)S(1)}, bf16[2,2,128,128]{3,2,1,0:T(8,128)(2,1)S(1)}, u32[]{:S(2)}, u32[]{:S(2)}) collective-permute-start(bf16[2,2,128,128]{3,2,1,0:T(8,128)(2,1)S(1)} %get-tuple-element.30), channel_id=1, source_target_pairs={{28,0},{0,4},{4,8},{8,12},{12,16},{16,20},{20,24},{24,28},{1,5},{5... | collective-permute-start | bytes 393224 | tf_op jit(solution)/shard_map/ppermute | solution.py:57
  36.4 11.7 %collective-permute-start.6 = (bf16[2,2,128,128]{3,2,1,0:T(8,128)(2,1)S(1)}, bf16[2,2,128,128]{3,2,1,0:T(8,128)(2,1)S(1)}, u32[]{:S(2)}, u32[]{:S(2)}) collective-permute-start(bf16[2,2,128,128]{3,2,1,0:T(8,128)(2,1)S(1)} %get-tuple-element.31), channel_id=1, source_target_pairs={{4,0},{8,4},{12,8},{16,12},{20,16},{24,20},{28,24},{0,28},{5,1},{9... | collective-permute-start | bytes 393224 | tf_op jit(solution)/shard_map/ppermute | solution.py:57
  41.5 9.3 %copy-start.11 = (bf16[2,2,128,128]{3,2,1,0:T(8,128)(2,1)}, bf16[2,2,128,128]{3,2,1,0:T(8,128)(2,1)S(1)}, u32[]{:S(2)}) copy-start(bf16[2,2,128,128]{3,2,1,0:T(8,128)(2,1)S(1)} %collective-permute-done.4.left) | copy-start | bytes 393220
  41.5 9.3 %collective-permute-start.7 = (bf16[2,2,128,128]{3,2,1,0:T(8,128)(2,1)S(1)}, bf16[2,2,128,128]{3,2,1,0:T(8,128)(2,1)S(1)}, u32[]{:S(2)}, u32[]{:S(2)}) collective-permute-start(bf16[2,2,128,128]{3,2,1,0:T(8,128)(2,1)S(1)} %get-tuple-element.32), channel_id=1, source_target_pairs={{4,0},{8,4},{12,8},{16,12},{20,16},{24,20},{28,24},{2,28},{5,1},{9... | collective-permute-start | bytes 393224 | tf_op jit(solution)/shard_map/ppermute | solution.py:57
  44.9 5.9 %copy-start.12 = (bf16[2,2,128,128]{3,2,1,0:T(8,128)(2,1)}, bf16[2,2,128,128]{3,2,1,0:T(8,128)(2,1)S(1)}, u32[]{:S(2)}) copy-start(bf16[2,2,128,128]{3,2,1,0:T(8,128)(2,1)S(1)} %collective-permute-done.5.mate_left) | copy-start | bytes 393220
  48.1 2.8 %copy-start.13 = (bf16[2,2,128,128]{3,2,1,0:T(8,128)(2,1)}, bf16[2,2,128,128]{3,2,1,0:T(8,128)(2,1)S(1)}, u32[]{:S(2)}) copy-start(bf16[2,2,128,128]{3,2,1,0:T(8,128)(2,1)S(1)} %collective-permute-done.6.right) | copy-start | bytes 393220
  50.8 0.7 copy-start.14
  50.8 1.1 copy-start.10
  50.8 1.2 copy-start.9
  68.1 34.9 %all-to-all-start.2 = ((bf16[32,4,16,128]{3,2,1,0:T(8,128)(2,1)}), bf16[32,4,16,128]{3,2,1,0:T(8,128)(2,1)S(1)}, u32[]{:S(2)}, u32[]{:S(2)}) async-start(bf16[32,4,16,128]{3,2,1,0:T(8,128)(2,1)} %bitcast.14), calls=%async_computation.2 | async-start | bytes 1048576 | tf_op jit(solution)/shard_map/all_to_all | solution.py:36
  71.6 37.7 %copy-start.8 = (s32[7]{0:T(128)S(1)}, s32[7]{0:T(128)}, u32[]{:S(2)}) copy-start(s32[7]{0:T(128)} %copy-done.7) | copy-start | bytes 88
  82.6 28.8 %collective-permute-start.8 = (bf16[128,2048]{1,0:T(8,128)(2,1)}, bf16[128,2048]{1,0:T(8,128)(2,1)S(1)}, u32[]{:S(2)}, u32[]{:S(2)}) collective-permute-start(bf16[128,2048]{1,0:T(8,128)(2,1)} %get-tuple-element.36), channel_id=1, source_target_pairs={{0,1},{1,0},{2,3},{3,2},{4,5},{5,4},{6,7},{7,6},{8,9},{9,8},{10,11... | collective-permute-start | bytes 1572872 | tf_op jit(solution)/shard_map/ppermute | solution.py:41
  82.9 12.3 %collective-permute-start.10 = (bf16[2,2,128,128]{3,2,1,0:T(8,128)(2,1)}, bf16[2,2,128,128]{3,2,1,0:T(8,128)(2,1)S(1)}, u32[]{:S(2)}, u32[]{:S(2)}) collective-permute-start(bf16[2,2,128,128]{3,2,1,0:T(8,128)(2,1)} %get-tuple-element.41), channel_id=1, source_target_pairs={{4,0},{8,4},{12,8},{16,12},{20,16},{24,20},{28,24},{1,29},{5,1},{9... | collective-permute-start | bytes 393224 | tf_op jit(solution)/shard_map/ppermute | solution.py:57
  84.2 28.0 %collective-permute-start.9 = (bf16[128,2048]{1,0:T(8,128)(2,1)}, bf16[128,2048]{1,0:T(8,128)(2,1)S(1)}, u32[]{:S(2)}, u32[]{:S(2)}) collective-permute-start(bf16[128,2048]{1,0:T(8,128)(2,1)} %get-tuple-element.38), channel_id=1, source_target_pairs={{0,1},{1,0},{2,3},{3,2},{4,5},{5,4},{6,7},{7,6},{8,9},{9,8},{10,11... | collective-permute-start | bytes 1572872 | tf_op jit(solution)/shard_map/ppermute | solution.py:41
  89.4 7.8 %collective-permute-start.11 = (bf16[2,2,128,128]{3,2,1,0:T(8,128)(2,1)}, bf16[2,2,128,128]{3,2,1,0:T(8,128)(2,1)S(1)}, u32[]{:S(2)}, u32[]{:S(2)}) collective-permute-start(bf16[2,2,128,128]{3,2,1,0:T(8,128)(2,1)} %get-tuple-element.42), channel_id=1, source_target_pairs={{0,28},{4,0},{8,4},{12,8},{16,12},{20,16},{24,20},{28,24},{5,1},{9... | collective-permute-start | bytes 393224 | tf_op jit(solution)/shard_map/ppermute | solution.py:57
  91.9 11.1 %collective-permute-start.12 = (bf16[2,2,128,128]{3,2,1,0:T(8,128)(2,1)}, bf16[2,2,128,128]{3,2,1,0:T(8,128)(2,1)S(1)}, u32[]{:S(2)}, u32[]{:S(2)}) collective-permute-start(bf16[2,2,128,128]{3,2,1,0:T(8,128)(2,1)} %get-tuple-element.43), channel_id=1, source_target_pairs={{0,4},{4,8},{8,12},{12,16},{16,20},{20,24},{24,28},{28,0},{1,5},{5... | collective-permute-start | bytes 393224 | tf_op jit(solution)/shard_map/ppermute | solution.py:57
  95.3 7.7 %collective-permute-start.13 = (bf16[2,2,128,128]{3,2,1,0:T(8,128)(2,1)}, bf16[2,2,128,128]{3,2,1,0:T(8,128)(2,1)S(1)}, u32[]{:S(2)}, u32[]{:S(2)}) collective-permute-start(bf16[2,2,128,128]{3,2,1,0:T(8,128)(2,1)} %get-tuple-element.44), channel_id=1, source_target_pairs={{0,4},{4,8},{8,12},{12,16},{16,20},{20,24},{24,28},{28,2},{1,5},{5... | collective-permute-start | bytes 393224 | tf_op jit(solution)/shard_map/ppermute | solution.py:57
  104.5 15.5 %all-to-all-start.3 = ((bf16[32,2,16,128]{3,2,1,0:T(8,128)(2,1)}), bf16[32,2,16,128]{3,2,1,0:T(8,128)(2,1)S(1)}, u32[]{:S(2)}, u32[]{:S(2)}) async-start(bf16[32,2,16,128]{3,2,1,0:T(8,128)(2,1)} %combine.1), calls=%async_computation.3 | async-start | bytes 524288 | tf_op jit(solution)/shard_map/all_to_all | solution.py:36
  109.4 1.0 copy-start.6
  111.1 2.0 %collective-permute-start.14 = (f32[2,2,128,128]{3,2,1,0:T(8,128)S(1)}, f32[2,2,128,128]{3,2,1,0:T(8,128)S(1)}, u32[]{:S(2)}, u32[]{:S(2)}) collective-permute-start(f32[2,2,128,128]{3,2,1,0:T(8,128)S(1)} %get-tuple-element.50), channel_id=1, source_target_pairs={{0,1},{1,0},{2,3},{3,2},{4,5},{5,4},{6,7},{7,6},{8,9},{9,8},{10,11... | collective-permute-start | bytes 786440 | tf_op jit(solution)/shard_map/ppermute | solution.py:41

commit v4 on v1

v4 whole, which is shorter than its diff:
```python
import math

import jax
import jax.numpy as jnp
from jax import lax
from jax.experimental import pallas as pl
from jax.experimental.pallas import tpu as pltpu
from jax.sharding import PartitionSpec as P

HD = 128
H = 32
KVH = 4
BLK = 128
NG = 2
GROUP = H // KVH
SCALE = 1.0 / math.sqrt(HD)
NEG_FILL = -1e30
AXES = ("ctx", "heads")
MATES = 2
SLOTS = 3 + NG + 1
WIDE = GROUP * BLK
PAIR = 2 * BLK
BF16 = jnp.bfloat16
F32 = jnp.float32

NT = (((1,), (1,)), ((), ()))


def params(mib, **kw):
    return pltpu.CompilerParams(vmem_limit_bytes=mib << 20, **kw)


def all_to_all(value):
    return lax.all_to_all(value, AXES, split_axis=0, concat_axis=0, tiled=True)


def mate(value):
    count = lax.axis_size("ctx")
    return lax.ppermute(value, "ctx", [(i, i ^ 1) for i in range(count)])


def swap_inner(value):
    heads = lax.axis_size("heads")
    return lax.ppermute(value, "heads", [(h, h ^ 1) for h in range(heads)])


def swap_outer(value):
    heads, ctx = lax.axis_size("heads"), lax.axis_size("ctx")
    pairs = []
    for i in range(1, heads * ctx - 1):
        j = i + 1 if i % 2 else i - 1
        pairs.append(tuple(b % heads * ctx + b // heads for b in (i, j)))
    return lax.ppermute(value, ("heads", "ctx"), pairs)


def pack_kernel(k_ref, v_ref, out_ref):
    for g in range(KVH):
        cols = slice(g * HD, (g + 1) * HD)
        out_ref[0, g] = k_ref[:, cols]
        out_ref[1, g] = v_ref[:, cols]


def pack(keys, values):
    return pl.pallas_call(
        pack_kernel,
        out_shape=jax.ShapeDtypeStruct((2, KVH, BLK, HD), BF16),
        compiler_params=params(58),
        name="pack",
    )(keys, values)


def side_of(i, heads):
    return i // heads % MATES


def select_kernel(heads, wanted_ref, in_ref, out_ref):
    count = in_ref.shape[0]
    globs = [in_ref[wanted_ref[count + slot]] for slot in range(NG)]
    for i in range(count):
        out_ref[i, 0] = in_ref[wanted_ref[i]]
        out_ref[i, 1] = globs[side_of(i, heads)]


def select(wanted, slices, heads):
    count, rows, _ = slices.shape
    if rows % 16:
        i = jnp.arange(count)
        glob = wanted[count + side_of(i, heads)]
        return slices[jnp.stack([wanted[i], glob], axis=1)]
    return pl.pallas_call(
        lambda *refs: select_kernel(heads, *refs),
        out_shape=jax.ShapeDtypeStruct((count, 2, rows, HD), BF16),
        in_specs=[
            pl.BlockSpec(memory_space=pltpu.SMEM),
            pl.BlockSpec(memory_space=pltpu.VMEM),
        ],
        out_specs=pl.BlockSpec(memory_space=pltpu.VMEM),
        compiler_params=params(8),
        name="select",
    )(wanted, slices)


def combine_kernel(heads, wanted_ref, in_ref, out_ref, acc_ref):
    count = in_ref.shape[0]
    acc_ref[...] = jnp.zeros_like(acc_ref)
    for side in range(MATES):
        total = None
        for i in range(count):
            if side_of(i, heads) == side:
                term = in_ref[i, 1].astype(F32)
                total = term if total is None else total + term
        acc_ref[wanted_ref[count + side]] += total
    for i in range(count):
        acc_ref[wanted_ref[i]] += in_ref[i, 0].astype(F32)
    out_ref[...] = acc_ref[...].astype(BF16)


def combine(wanted, terms, heads):
    count, _, rows, _ = terms.shape
    if rows % 16:
        i = jnp.arange(count)
        wide = terms.astype(F32)
        total = jnp.zeros((count, rows, HD), F32).at[wanted[i]].add(wide[:, 0])
        return total.at[wanted[count + side_of(i, heads)]].add(wide[:, 1]).astype(BF16)
    return pl.pallas_call(
        lambda *refs: combine_kernel(heads, *refs),
        out_shape=jax.ShapeDtypeStruct((count, rows, HD), BF16),
        in_specs=[
            pl.BlockSpec(memory_space=pltpu.SMEM),
            pl.BlockSpec(memory_space=pltpu.VMEM),
        ],
        out_specs=pl.BlockSpec(memory_space=pltpu.VMEM),
        scratch_shapes=[pltpu.VMEM((count, rows, HD), F32)],
        compiler_params=params(16),
        name="combine",
    )(wanted, terms)


def join_kernel(random_ref, glob_ref, other_ref, out_ref):
    out_ref[:, 0] = random_ref[...]
    out_ref[:, 1] = (glob_ref[...] + other_ref[...].astype(F32)).astype(BF16)


def join(random, glob, other):
    count, rows, _ = random.shape
    if rows % 16:
        total = (glob + other.astype(F32)).astype(BF16)
        return jnp.stack([random, total], axis=1)
    return pl.pallas_call(
        join_kernel,
        out_shape=jax.ShapeDtypeStruct((count, 2, rows, HD), BF16),
        compiler_params=params(58),
        name="join",
    )(random, glob, other)


def stacked(ref):
    return jnp.concatenate(
        [ref[:, h * HD : (h + 1) * HD] for h in range(GROUP)], axis=0
    )


def blocks_of(kind, own_ref, inner_ref, outer_ref, far_ref, other_ref):
    blocks = [inner_ref[kind, 0], outer_ref[kind, 0], own_ref[kind, 0]]
    for ref, slot in ((far_ref, 1), (other_ref, 1), (far_ref, 0)):
        blocks.append(ref[kind, :, slot].reshape(BLK, HD))
    return blocks


def grads_of(b, queries, douts, probs_ref, ds_ref):
    rows = slice(b * BLK, (b + 1) * BLK)
    dk = jnp.dot(ds_ref[0, rows], queries, preferred_element_type=F32) * SCALE
    dv = jnp.dot(probs_ref[0, rows], douts, preferred_element_type=F32)
    return dk, dv


def scores_kernel(
    edge_ref, q_ref, do_ref, own_ref, inner_ref, outer_ref, far_ref, other_ref,
    probs_ref, ds_ref, random_ref, glob_ref, mate_ref, s_ref, dp_ref,
):
    near = (own_ref, inner_ref, outer_ref, far_ref, other_ref)
    keys, values = blocks_of(0, *near), blocks_of(1, *near)
    queries, douts = stacked(q_ref), stacked(do_ref)
    factor = SCALE / math.log(2.0)
    for pair in range(WIDE // PAIR):
        cols = slice(pair * PAIR, (pair + 1) * PAIR)
        q, do = queries[cols], douts[cols]
        row_max = None
        for b in range(SLOTS):
            s = lax.dot_general(keys[b], q, NT, preferred_element_type=F32)
            if b == 1:
                s = jnp.where(edge_ref[0] == 0, s, NEG_FILL)
            s_ref[b * BLK : (b + 1) * BLK] = s
            top = jnp.max(s, axis=0, keepdims=True)
            row_max = top if row_max is None else jnp.maximum(row_max, top)
        row_sum = jnp.zeros((1, PAIR), F32)
        centre = jnp.zeros((1, PAIR), F32)
        for b in range(SLOTS):
            rows = slice(b * BLK, (b + 1) * BLK)
            w = jnp.exp2((s_ref[rows] - row_max) * factor)
            dp = lax.dot_general(values[b], do, NT, preferred_element_type=F32)
            s_ref[rows] = w
            dp_ref[rows] = dp
            row_sum = row_sum + jnp.sum(w, axis=0, keepdims=True)
            centre = centre + jnp.sum(w * dp, axis=0, keepdims=True)
        inverse = 1.0 / row_sum
        centre = centre * inverse
        for b in range(SLOTS):
            rows = slice(b * BLK, (b + 1) * BLK)
            p = s_ref[rows] * inverse
            probs_ref[0, rows, cols] = p.astype(BF16)
            ds_ref[0, rows, cols] = (p * (dp_ref[rows] - centre)).astype(BF16)
    for b, dest in ((4, mate_ref), (3, glob_ref), (5, random_ref)):
        for kind, term in enumerate(grads_of(b, queries, douts, probs_ref, ds_ref)):
            dest[kind, 0] = term.astype(dest.dtype)


def window_kernel(q_ref, do_ref, probs_ref, ds_ref, inner_ref, outer_ref):
    queries, douts = stacked(q_ref), stacked(do_ref)
    for b, dest in enumerate((inner_ref, outer_ref)):
        for kind, term in enumerate(grads_of(b, queries, douts, probs_ref, ds_ref)):
            dest[kind, 0] = term.astype(BF16)


def outputs_kernel(
    q_ref, do_ref, own_ref, inner_ref, outer_ref, far_ref, other_ref, probs_ref, ds_ref,
    from_inner_ref, from_outer_ref, out_ref, dq_ref, near_ref,
):
    near = (own_ref, inner_ref, outer_ref, far_ref, other_ref)
    keys_t, values_t = (
        jnp.concatenate([x.T for x in blocks_of(kind, *near)], axis=1)
        for kind in range(2)
    )
    for pair in range(WIDE // PAIR):
        cols = slice(pair * PAIR, (pair + 1) * PAIR)
        out_t = jnp.dot(values_t, probs_ref[0, :, cols], preferred_element_type=F32)
        dq_t = jnp.dot(keys_t, ds_ref[0, :, cols], preferred_element_type=F32) * SCALE
        for half in range(2):
            part = slice(half * HD, (half + 1) * HD)
            dest = slice(pair * PAIR + half * HD, pair * PAIR + (half + 1) * HD)
            out_ref[:, dest] = out_t[:, part].T.astype(BF16)
            dq_ref[:, dest] = dq_t[:, part].T.astype(BF16)
    queries, douts = stacked(q_ref), stacked(do_ref)
    for kind, term in enumerate(grads_of(2, queries, douts, probs_ref, ds_ref)):
        back = from_inner_ref[kind, 0].astype(F32) + from_outer_ref[kind, 0].astype(F32)
        near_ref[kind, 0] = term + back


def finish_kernel(near_ref, far_ref, dk_ref, dv_ref):
    for kind, dest in enumerate((dk_ref, dv_ref)):
        for g in range(KVH):
            total = near_ref[kind, g] + far_ref[kind, g].astype(F32)
            dest[:, g * HD : (g + 1) * HD] = total.astype(BF16)


def finish(near, far):
    shape = jax.ShapeDtypeStruct((BLK, KVH * HD), BF16)
    return pl.pallas_call(
        finish_kernel,
        out_shape=(shape, shape),
        compiler_params=params(8),
        name="finish",
    )(near, far)


def shards(queries, keys_in, values_in, cotangent, rand_blocks, glob_blocks):
    heads, ctx = lax.axis_size("heads"), lax.axis_size("ctx")
    count = heads * ctx
    mine = lax.axis_index("ctx") * heads + lax.axis_index("heads")
    edges = ((mine == 0) | (mine == count - 1)).astype(jnp.int32).reshape(1)
    wanted = jnp.concatenate([rand_blocks[:, 0], glob_blocks])
    rows = 2 * KVH * BLK // count
    share = BLK // rows if rows % 16 == 0 else 1
    packed = pack(keys_in, values_in)
    slices = all_to_all(packed.reshape(count, rows, HD))
    inner, outer = swap_inner(packed), swap_outer(packed)
    slices, inner = lax.optimization_barrier((slices, inner))
    far = all_to_all(select(wanted, slices, heads))
    far, outer = lax.optimization_barrier((far, outer))
    if share == 1:
        far = far.reshape(2, KVH, BLK // rows, 2, rows, HD)
        far = jnp.transpose(far, (0, 1, 3, 2, 4, 5))
    far = far.reshape(2, KVH * share, 2, BLK // share, HD)
    other = mate(far)

    token = pl.BlockSpec((BLK, WIDE), lambda g, *_: (0, g))
    block = pl.BlockSpec((2, 1, BLK, HD), lambda g, *_: (0, g, 0, 0))
    far_spec = pl.BlockSpec((2, share, 2, BLK // share, HD), lambda g, *_: (0, g, 0, 0, 0))
    square = pl.BlockSpec((1, SLOTS * BLK, WIDE), lambda g, *_: (g, 0, 0))
    two_rows = pl.BlockSpec((1, 2 * BLK, WIDE), lambda g, *_: (g, 0, 0))
    square_shape = jax.ShapeDtypeStruct((KVH, SLOTS * BLK, WIDE), BF16)
    token_shape = jax.ShapeDtypeStruct(queries.shape, BF16)
    low, wide = (jax.ShapeDtypeStruct((2, KVH, BLK, HD), dtype) for dtype in (BF16, F32))
    flops = 2 * H * BLK * SLOTS * BLK * HD
    blocks = (packed, inner, outer, far, other)
    block_specs = [block] * 3 + [far_spec] * 2

    def call(kernel, name, work, in_specs, outs, scalars=0, scratch=()):
        return pl.pallas_call(
            kernel,
            grid_spec=pltpu.PrefetchScalarGridSpec(
                num_scalar_prefetch=scalars,
                grid=(KVH,),
                in_specs=[token, token] + in_specs,
                out_specs=[spec for spec, _ in outs],
                scratch_shapes=scratch,
            ),
            out_shape=[shape for _, shape in outs],
            compiler_params=params(56, dimension_semantics=("arbitrary",)),
            cost_estimate=pl.CostEstimate(
                flops=work * flops, bytes_accessed=16 << 20, transcendentals=0
            ),
            name=name,
        )

    probs, ds, random, glob, for_mate = call(
        scores_kernel,
        "scores",
        3,
        block_specs,
        [(square, square_shape)] * 2 + [(block, low), (block, wide), (block, low)],
        1,
        [pltpu.VMEM((SLOTS * BLK, PAIR), F32)] * 2,
    )(edges, queries, cotangent, *blocks)
    flat = (count, rows, HD)
    terms = join(random.reshape(flat), glob.reshape(flat), mate(for_mate).reshape(flat))
    arrived = all_to_all(terms)
    back = call(
        window_kernel, "window", 1, [two_rows, two_rows], [(block, low)] * 2
    )(queries, cotangent, probs, ds)
    back = [swap_inner(back[0]), swap_outer(back[1])]
    arrived, *back = lax.optimization_barrier((arrived, *back))
    summed = combine(wanted, arrived, heads)
    returned = all_to_all(summed).reshape(2, KVH, BLK, HD)
    probs, summed = lax.optimization_barrier((probs, summed))
    attn_out, grad_query, near = call(
        outputs_kernel,
        "outputs",
        2,
        block_specs + [square, square, block, block],
        [(token, token_shape)] * 2 + [(block, wide)],
    )(queries, cotangent, *blocks, probs, ds, *back)
    grad_keys, grad_values = finish(near, returned)
    return attn_out, grad_query, grad_keys, grad_values


def solution(mesh):
    spec = P(AXES, None)
    return jax.shard_map(
        shards,
        mesh=mesh,
        in_specs=(spec, spec, spec, spec, P(), P()),
        out_specs=(spec, spec, spec, spec),
        check_vma=False,
    )
```

time: 138 us -> 113 us (0.82)
  blocking collectives: 26.5 us -> 0 us
  local copies, waits for them, and re-layouts: 19.3 us -> 2.53 us
  Pallas kernels: 24.3 us -> 35.2 us
  starting transfers between devices: 23.3 us -> 28.9 us
  waiting for transfers between devices: 43 us -> 44.7 us
    all_to_all x1 -> x0, blocking collectives: 26.5 us -> none  [all_to_all(): return lax.all_to_all(value, AXES, split_axis=0, concat_axis=0, tiled=True)]
    unnamed x33 -> x16, local copies, waits for them, and re-layouts: 19.3 us -> 2.53 us
    pallas_call x4 -> x6, Pallas kernels: 22.7 us -> 32.8 us  [the longest x1 14.4 us: shards(): call(scores_kernel, 'scores', 3, block_specs, [(square, square_shape)] *...]
    all_to_all x3 -> x4, starting transfers between devices: 12.6 us -> 21.3 us  [all_to_all(): return lax.all_to_all(value, AXES, split_axis=0, concat_axis=0, tiled=True)]
    all_to_all x3 -> x4, waiting for transfers between devices: 13.5 us -> 20.5 us  [all_to_all(): return lax.all_to_all(value, AXES, split_axis=0, concat_axis=0, tiled=True)]
    ppermute x4 -> x6, waiting for transfers between devices: 29.5 us -> 24.2 us  [the longest x2 21.3 us: swap_inner(): return lax.ppermute(value, 'heads', [(h, h ^ 1) for h in range(heads)])]
    ppermute x4 -> x6, starting transfers between devices: 10.7 us -> 7.55 us  [the longest x2 3.6 us: swap_inner(): return lax.ppermute(value, 'heads', [(h, h ^ 1) for h in range(heads)])]
  transfers between devices with their start and end apart: 7 -> 10, of which waited for: 6 -> 6; matrix products, arithmetic and copies ran while one was open for 1% -> 1% of each run, Pallas kernels for 4% -> 12%
where the time goes in v4:
time: 113 us
  waiting for transfers between devices  44.7 us (40%)
  Pallas kernels  35.2 us (31%)
  starting transfers between devices  28.9 us (26%)
  local copies, waits for them, and re-layouts  2.53 us (2%)
    all_to_all x4, starting transfers between devices, all_to_all(): return lax.all_to_all(value, AXES, split_axis=0, concat_axis=0, tiled=True)  21.3 us
    ppermute x2, waiting for transfers between devices, swap_inner(): return lax.ppermute(value, 'heads', [(h, h ^ 1) for h in range(heads)])  21.3 us
    all_to_all x4, waiting for transfers between devices, all_to_all(): return lax.all_to_all(value, AXES, split_axis=0, concat_axis=0, tiled=True)  20.5 us
    pallas_call x1, Pallas kernels, shards(): call(scores_kernel, 'scores', 3, block_specs, [(square, square_shape)] *...  14.4 us
    pallas_call x1, Pallas kernels, shards(): call(outputs_kernel, 'outputs', 2, block_specs + [square, square, block,...  8.56 us
    pallas_call x1, Pallas kernels, shards(): call(window_kernel, 'window', 1, [two_rows, two_rows], [(block, low)] * 2)  4.99 us
    ppermute x2, starting transfers between devices, swap_inner(): return lax.ppermute(value, 'heads', [(h, h ^ 1) for h in range(heads)])  3.6 us
    ppermute x2, waiting for transfers between devices, mate(): return lax.ppermute(value, 'ctx', [(i, i ^ 1) for i in range(count)])  2.91 us
  transfers between devices with their start and end apart: 10, of which 6 were waited for; matrix products, arithmetic and copies ran while one was open for 1% of the time, Pallas kernels for 12%

profile of v4, /device:TPU:0, one launch (start us, length us, event | category | flops | bytes accessed | tf_op | source)
XLA Modules:
  0.0 112.8 jit_solution(11960248436759983489)
XLA Ops:
  0.6 1.7 %pack.1.own_ref = bf16[2,4,128,128]{3,2,1,0:T(8,128)(2,1)} custom-call(bf16[128,512]{1,0:T(8,128)(2,1)} %k_ref.1, bf16[128,512]{1,0:T(8,128)(2,1)} %v_ref.1), custom_call_target="tpu_custom_call" | custom-call | tf_op jit(solution)/shard_map/pack/pallas_call | solution.py:64
  2.3 7.3 %all-to-all-start = ((bf16[32,32,128]{2,1,0:T(8,128)(2,1)}), bf16[32,32,128]{2,1,0:T(8,128)(2,1)S(1)}, u32[]{:S(2)}, u32[]{:S(2)}) async-start(bf16[32,32,128]{2,1,0:T(8,128)(2,1)} %bitcast.9), calls=%async_computation | async-start | bytes 524288 | tf_op jit(solution)/shard_map/all_to_all | solution.py:34
  9.6 1.8 %collective-permute-start = (bf16[2,4,128,128]{3,2,1,0:T(8,128)(2,1)}, bf16[2,4,128,128]{3,2,1,0:T(8,128)(2,1)S(1)}, u32[]{:S(2)}, u32[]{:S(2)}) collective-permute-start(bf16[2,4,128,128]{3,2,1,0:T(8,128)(2,1)} %pack.1.own_ref), channel_id=1, source_target_pairs={{0,4},{4,0},{8,12},{12,8},{16,20},{20,16},{24,28},{28,24},{1,5},{5... | collective-permute-start | bytes 786440 | tf_op jit(solution)/shard_map/ppermute | solution.py:44
  11.5 0.7 pad_add_fusion.refs_0_
  12.2 8.7 %collective-permute-done.inner_ref = bf16[2,4,128,128]{3,2,1,0:T(8,128)(2,1)S(1)} collective-permute-done((bf16[2,4,128,128]{3,2,1,0:T(8,128)(2,1)}, bf16[2,4,128,128]{3,2,1,0:T(8,128)(2,1)S(1)}, u32[]{:S(2)}, u32[]{:S(2)}) %collective-permute-start) | collective-permute-done | bytes 262176 | tf_op jit(solution)/shard_map/ppermute | solution.py:44
  20.9 0.0 copy-start.3
  20.9 0.0 all-to-all-done.refs_1_
  20.9 1.4 %select.1 = bf16[32,2,32,128]{3,2,1,0:T(8,128)(2,1)} custom-call(s32[34]{0:T(128)S(1)} %pad_add_fusion.refs_0_, bf16[32,32,128]{2,1,0:T(8,128)(2,1)S(1)} %all-to-all-done.refs_1_), custom_call_target="tpu_custom_call" | custom-call | tf_op jit(solution)/shard_map/select/pallas_call | solution.py:90
  22.3 4.6 %all-to-all-start.1 = ((bf16[32,2,32,128]{3,2,1,0:T(8,128)(2,1)}), bf16[32,2,32,128]{3,2,1,0:T(8,128)(2,1)S(1)}, u32[]{:S(2)}, u32[]{:S(2)}) async-start(bf16[32,2,32,128]{3,2,1,0:T(8,128)(2,1)} %select.1), calls=%async_computation.1 | async-start | bytes 1048576 | tf_op jit(solution)/shard_map/all_to_all | solution.py:34
  26.9 0.7 collective-permute-start.1
  27.6 0.0 collective-permute-done.1.outer_ref
  27.6 0.0 copy-start.4
  27.6 18.5 %all-to-all-done.1 = bf16[32,2,32,128]{3,2,1,0:T(8,128)(2,1)S(1)} async-done(((bf16[32,2,32,128]{3,2,1,0:T(8,128)(2,1)}), bf16[32,2,32,128]{3,2,1,0:T(8,128)(2,1)S(1)}, u32[]{:S(2)}, u32[]{:S(2)}) %all-to-all-start.1) | async-done | bytes 524320 | tf_op jit(solution)/shard_map/all_to_all | solution.py:34
  46.1 0.0 copy-start.1
  46.1 2.2 %collective-permute-start.2 = (bf16[2,16,2,32,128]{4,3,2,1,0:T(8,128)(2,1)S(1)}, bf16[2,16,2,32,128]{4,3,2,1,0:T(8,128)(2,1)S(1)}, u32[]{:S(2)}, u32[]{:S(2)}) collective-permute-start(bf16[2,16,2,32,128]{4,3,2,1,0:T(8,128)(2,1)S(1)} %bitcast.10), channel_id=1, source_target_pairs={{0,1},{1,0},{2,3},{3,2},{4,5},{5,4},{6,7},{7,6},{8,9},{9,8},{10,11... | collective-permute-start | bytes 1572872 | tf_op jit(solution)/shard_map/ppermute | solution.py:39
  48.3 1.5 %collective-permute-done.2.other_ref = bf16[2,16,2,32,128]{4,3,2,1,0:T(8,128)(2,1)S(1)} collective-permute-done((bf16[2,16,2,32,128]{4,3,2,1,0:T(8,128)(2,1)S(1)}, bf16[2,16,2,32,128]{4,3,2,1,0:T(8,128)(2,1)S(1)}, u32[]{:S(2)}, u32[]{:S(2)}) %collective-permute-start.2) | collective-permute-done | bytes 524320 | tf_op jit(solution)/shard_map/ppermute | solution.py:39
  49.8 0.0 copy-start.2
  49.8 0.0 copy-done.3
  49.8 0.0 copy-done.4
  49.8 0.0 copy-done.1
  49.8 0.8 copy-done.2
  50.6 14.4 %scores.1 = (bf16[4,768,1024]{2,1,0:T(8,128)(2,1)}, bf16[4,768,1024]{2,1,0:T(8,128)(2,1)}, bf16[2,4,128,128]{3,2,1,0:T(8,128)(2,1)}, f32[2,4,128,128]{3,2,1,0:T(8,128)}, bf16[2,4,128,128]{3,2,1,0:T(8,128)(2,1)}) custom-call(s32[1]{0:T(128)} %bitcast.3.edge_ref, bf16[128,4096]{1,0:T(8,128)(2,1)} %q_ref.5, bf16[128,4096]{1,0:T(8,128)(2,1)} %do_ref.5, ...), custom_call_target="tpu_custom_call" | custom-call | flops 2415919104 | bytes 16777216 | tf_op jit(solution)/shard_map/scores/pallas_call | solution.py:316
  65.0 0.4 collective-permute-start.3
  65.4 1.4 %collective-permute-done.3 = bf16[2,4,128,128]{3,2,1,0:T(8,128)(2,1)S(1)} collective-permute-done((bf16[2,4,128,128]{3,2,1,0:T(8,128)(2,1)}, bf16[2,4,128,128]{3,2,1,0:T(8,128)(2,1)S(1)}, u32[]{:S(2)}, u32[]{:S(2)}) %collective-permute-start.3) | collective-permute-done | bytes 262176 | tf_op jit(solution)/shard_map/ppermute | solution.py:39
  66.8 0.0 copy-start.7
  66.8 0.7 copy-done.7
  67.4 2.0 %join.1 = bf16[32,2,32,128]{3,2,1,0:T(8,128)(2,1)} custom-call(bf16[32,32,128]{2,1,0:T(8,128)(2,1)} %bitcast.14, f32[32,32,128]{2,1,0:T(8,128)} %bitcast.13, bf16[32,32,128]{2,1,0:T(8,128)(2,1)} %bitcast.15), custom_call_target="tpu_custom_call" | custom-call | tf_op jit(solution)/shard_map/join/pallas_call | solution.py:149
  69.5 3.1 %all-to-all-start.2 = ((bf16[32,2,32,128]{3,2,1,0:T(8,128)(2,1)}), bf16[32,2,32,128]{3,2,1,0:T(8,128)(2,1)S(1)}, u32[]{:S(2)}, u32[]{:S(2)}) async-start(bf16[32,2,32,128]{3,2,1,0:T(8,128)(2,1)} %join.1), calls=%async_computation.2 | async-start | bytes 1048576 | tf_op jit(solution)/shard_map/all_to_all | solution.py:34
  72.6 5.0 %window.1 = (bf16[2,4,128,128]{3,2,1,0:T(8,128)(2,1)}, bf16[2,4,128,128]{3,2,1,0:T(8,128)(2,1)}) custom-call(bf16[128,4096]{1,0:T(8,128)(2,1)} %q_ref.5, bf16[128,4096]{1,0:T(8,128)(2,1)} %do_ref.5, bf16[4,768,1024]{2,1,0:T(8,128)(2,1)} %get-tuple-element.36.probs_ref, bf16[4,768,1024]{2,1,0:T(8,128)(2,1)} %get-tuple-element.32.ds_ref), custom_call_target="tpu_custom_call" | custom-call | flops 805306368 | bytes 16777216 | tf_op jit(solution)/shard_map/window/pallas_call | solution.py:328
  77.6 1.8 %collective-permute-start.4 = (bf16[2,4,128,128]{3,2,1,0:T(8,128)(2,1)}, bf16[2,4,128,128]{3,2,1,0:T(8,128)(2,1)S(1)}, u32[]{:S(2)}, u32[]{:S(2)}) collective-permute-start(bf16[2,4,128,128]{3,2,1,0:T(8,128)(2,1)} %get-tuple-element.33), channel_id=1, source_target_pairs={{0,4},{4,0},{8,12},{12,8},{16,20},{20,16},{24,28},{28,24},{1,5},{5... | collective-permute-start | bytes 786440 | tf_op jit(solution)/shard_map/ppermute | solution.py:44
  79.4 0.7 collective-permute-start.5
  80.0 12.5 %collective-permute-done.4.from_inner_ref = bf16[2,4,128,128]{3,2,1,0:T(8,128)(2,1)S(1)} collective-permute-done((bf16[2,4,128,128]{3,2,1,0:T(8,128)(2,1)}, bf16[2,4,128,128]{3,2,1,0:T(8,128)(2,1)S(1)}, u32[]{:S(2)}, u32[]{:S(2)}) %collective-permute-start.4) | collective-permute-done | bytes 262176 | tf_op jit(solution)/shard_map/ppermute | solution.py:44
  92.6 0.0 copy-start.5
  92.6 0.0 collective-permute-done.5.from_outer_ref
  92.6 0.0 copy-start.6
  92.6 0.0 all-to-all-done.2.refs_1_
  92.6 1.4 %combine.1 = bf16[32,32,128]{2,1,0:T(8,128)(2,1)} custom-call(s32[34]{0:T(128)S(1)} %pad_add_fusion.refs_0_, bf16[32,2,32,128]{3,2,1,0:T(8,128)(2,1)S(1)} %all-to-all-done.2.refs_1_), custom_call_target="tpu_custom_call" | custom-call | tf_op jit(solution)/shard_map/combine/pallas_call | solution.py:125
  94.0 6.4 %all-to-all-start.3 = ((bf16[32,32,128]{2,1,0:T(8,128)(2,1)}), bf16[32,32,128]{2,1,0:T(8,128)(2,1)S(1)}, u32[]{:S(2)}, u32[]{:S(2)}) async-start(bf16[32,32,128]{2,1,0:T(8,128)(2,1)} %combine.1), calls=%async_computation.3 | async-start | bytes 524288 | tf_op jit(solution)/shard_map/all_to_all | solution.py:34
  100.4 0.0 copy-done.5
  100.4 0.0 copy-done.6
  100.4 8.6 %outputs.1 = (bf16[128,4096]{1,0:T(8,128)(2,1)}, bf16[128,4096]{1,0:T(8,128)(2,1)}, f32[2,4,128,128]{3,2,1,0:T(8,128)}) custom-call(bf16[128,4096]{1,0:T(8,128)(2,1)} %q_ref.5, bf16[128,4096]{1,0:T(8,128)(2,1)} %do_ref.5, bf16[2,4,128,128]{3,2,1,0:T(8,128)(2,1)} %pack.1.own_ref, bf16[2,4,128,128]{3,2,1,0:T(8,128)(2,1)} %copy-done.3, ...), custom_call_target="tpu_custom_call" | custom-call | flops 1610612736 | bytes 16777216 | tf_op jit(solution)/shard_map/outputs/pallas_call | solution.py:336
  109.0 2.1 %all-to-all-done.3 = bf16[32,32,128]{2,1,0:T(8,128)(2,1)S(1)} async-done(((bf16[32,32,128]{2,1,0:T(8,128)(2,1)}), bf16[32,32,128]{2,1,0:T(8,128)(2,1)S(1)}, u32[]{:S(2)}, u32[]{:S(2)}) %all-to-all-start.3) | async-done | bytes 262176 | tf_op jit(solution)/shard_map/all_to_all | solution.py:34
  111.0 0.0 copy-start
  111.0 1.0 copy-done
  112.1 0.7 finish.1
Async XLA Ops:
  2.3 18.6 %all-to-all-start = ((bf16[32,32,128]{2,1,0:T(8,128)(2,1)}), bf16[32,32,128]{2,1,0:T(8,128)(2,1)S(1)}, u32[]{:S(2)}, u32[]{:S(2)}) async-start(bf16[32,32,128]{2,1,0:T(8,128)(2,1)} %bitcast.9), calls=%async_computation | async-start | bytes 524288 | tf_op jit(solution)/shard_map/all_to_all | solution.py:34
  9.6 11.3 %collective-permute-start = (bf16[2,4,128,128]{3,2,1,0:T(8,128)(2,1)}, bf16[2,4,128,128]{3,2,1,0:T(8,128)(2,1)S(1)}, u32[]{:S(2)}, u32[]{:S(2)}) collective-permute-start(bf16[2,4,128,128]{3,2,1,0:T(8,128)(2,1)} %pack.1.own_ref), channel_id=1, source_target_pairs={{0,4},{4,0},{8,12},{12,8},{16,20},{20,16},{24,28},{28,24},{1,5},{5... | collective-permute-start | bytes 786440 | tf_op jit(solution)/shard_map/ppermute | solution.py:44
  20.9 28.9 %copy-start.3 = (bf16[2,4,128,128]{3,2,1,0:T(8,128)(2,1)}, bf16[2,4,128,128]{3,2,1,0:T(8,128)(2,1)S(1)}, u32[]{:S(2)}) copy-start(bf16[2,4,128,128]{3,2,1,0:T(8,128)(2,1)S(1)} %collective-permute-done.inner_ref) | copy-start | bytes 786436
  22.3 23.7 %all-to-all-start.1 = ((bf16[32,2,32,128]{3,2,1,0:T(8,128)(2,1)}), bf16[32,2,32,128]{3,2,1,0:T(8,128)(2,1)S(1)}, u32[]{:S(2)}, u32[]{:S(2)}) async-start(bf16[32,2,32,128]{3,2,1,0:T(8,128)(2,1)} %select.1), calls=%async_computation.1 | async-start | bytes 1048576 | tf_op jit(solution)/shard_map/all_to_all | solution.py:34
  26.9 0.7 collective-permute-start.1
  27.6 22.2 %copy-start.4 = (bf16[2,4,128,128]{3,2,1,0:T(8,128)(2,1)}, bf16[2,4,128,128]{3,2,1,0:T(8,128)(2,1)S(1)}, u32[]{:S(2)}) copy-start(bf16[2,4,128,128]{3,2,1,0:T(8,128)(2,1)S(1)} %collective-permute-done.1.outer_ref) | copy-start | bytes 786436
  46.1 3.7 %copy-start.1 = (bf16[32,2,32,128]{3,2,1,0:T(8,128)(2,1)}, bf16[32,2,32,128]{3,2,1,0:T(8,128)(2,1)S(1)}, u32[]{:S(2)}) copy-start(bf16[32,2,32,128]{3,2,1,0:T(8,128)(2,1)S(1)} %all-to-all-done.1) | copy-start | bytes 1572868
  46.1 3.7 %collective-permute-start.2 = (bf16[2,16,2,32,128]{4,3,2,1,0:T(8,128)(2,1)S(1)}, bf16[2,16,2,32,128]{4,3,2,1,0:T(8,128)(2,1)S(1)}, u32[]{:S(2)}, u32[]{:S(2)}) collective-permute-start(bf16[2,16,2,32,128]{4,3,2,1,0:T(8,128)(2,1)S(1)} %bitcast.10), channel_id=1, source_target_pairs={{0,1},{1,0},{2,3},{3,2},{4,5},{5,4},{6,7},{7,6},{8,9},{9,8},{10,11... | collective-permute-start | bytes 1572872 | tf_op jit(solution)/shard_map/ppermute | solution.py:39
  49.8 0.8 copy-start.2
  65.0 1.8 %collective-permute-start.3 = (bf16[2,4,128,128]{3,2,1,0:T(8,128)(2,1)}, bf16[2,4,128,128]{3,2,1,0:T(8,128)(2,1)S(1)}, u32[]{:S(2)}, u32[]{:S(2)}) collective-permute-start(bf16[2,4,128,128]{3,2,1,0:T(8,128)(2,1)} %get-tuple-element.31), channel_id=1, source_target_pairs={{0,1},{1,0},{2,3},{3,2},{4,5},{5,4},{6,7},{7,6},{8,9},{9,8},{10,11... | collective-permute-start | bytes 786440 | tf_op jit(solution)/shard_map/ppermute | solution.py:39
  66.8 0.7 copy-start.7
  69.5 23.1 %all-to-all-start.2 = ((bf16[32,2,32,128]{3,2,1,0:T(8,128)(2,1)}), bf16[32,2,32,128]{3,2,1,0:T(8,128)(2,1)S(1)}, u32[]{:S(2)}, u32[]{:S(2)}) async-start(bf16[32,2,32,128]{3,2,1,0:T(8,128)(2,1)} %join.1), calls=%async_computation.2 | async-start | bytes 1048576 | tf_op jit(solution)/shard_map/all_to_all | solution.py:34
  77.6 15.0 %collective-permute-start.4 = (bf16[2,4,128,128]{3,2,1,0:T(8,128)(2,1)}, bf16[2,4,128,128]{3,2,1,0:T(8,128)(2,1)S(1)}, u32[]{:S(2)}, u32[]{:S(2)}) collective-permute-start(bf16[2,4,128,128]{3,2,1,0:T(8,128)(2,1)} %get-tuple-element.33), channel_id=1, source_target_pairs={{0,4},{4,0},{8,12},{12,8},{16,20},{20,16},{24,28},{28,24},{1,5},{5... | collective-permute-start | bytes 786440 | tf_op jit(solution)/shard_map/ppermute | solution.py:44
  79.4 13.2 %collective-permute-start.5 = (bf16[2,4,128,128]{3,2,1,0:T(8,128)(2,1)}, bf16[2,4,128,128]{3,2,1,0:T(8,128)(2,1)S(1)}, u32[]{:S(2)}, u32[]{:S(2)}) collective-permute-start(bf16[2,4,128,128]{3,2,1,0:T(8,128)(2,1)} %get-tuple-element.34), channel_id=1, source_target_pairs={{4,8},{8,4},{12,16},{16,12},{20,24},{24,20},{28,1},{1,28},{5,9},{9... | collective-permute-start | bytes 786440 | tf_op jit(solution)/shard_map/ppermute | solution.py:53
  92.6 7.8 %copy-start.5 = (bf16[2,4,128,128]{3,2,1,0:T(8,128)(2,1)}, bf16[2,4,128,128]{3,2,1,0:T(8,128)(2,1)S(1)}, u32[]{:S(2)}) copy-start(bf16[2,4,128,128]{3,2,1,0:T(8,128)(2,1)S(1)} %collective-permute-done.4.from_inner_ref) | copy-start | bytes 786436
  92.6 7.8 %copy-start.6 = (bf16[2,4,128,128]{3,2,1,0:T(8,128)(2,1)}, bf16[2,4,128,128]{3,2,1,0:T(8,128)(2,1)S(1)}, u32[]{:S(2)}) copy-start(bf16[2,4,128,128]{3,2,1,0:T(8,128)(2,1)S(1)} %collective-permute-done.5.from_outer_ref) | copy-start | bytes 786436
  94.0 17.0 %all-to-all-start.3 = ((bf16[32,32,128]{2,1,0:T(8,128)(2,1)}), bf16[32,32,128]{2,1,0:T(8,128)(2,1)S(1)}, u32[]{:S(2)}, u32[]{:S(2)}) async-start(bf16[32,32,128]{2,1,0:T(8,128)(2,1)} %combine.1), calls=%async_computation.3 | async-start | bytes 524288 | tf_op jit(solution)/shard_map/all_to_all | solution.py:34
  111.0 1.0 copy-start

commit v5 on v4

v5 whole, which is shorter than its diff:
```python
import math

import jax
import jax.numpy as jnp
from jax import lax
from jax.experimental import pallas as pl
from jax.experimental.pallas import tpu as pltpu
from jax.sharding import PartitionSpec as P

HD = 128
H = 32
KVH = 4
BLK = 128
NG = 2
GROUP = H // KVH
SCALE = 1.0 / math.sqrt(HD)
NEG_FILL = -1e30
AXES = ("ctx", "heads")
MATES = 2
SLOTS = 3 + NG + 1
WIDE = GROUP * BLK
PART = WIDE
FACTOR = SCALE / math.log(2.0)
BF16 = jnp.bfloat16
F32 = jnp.float32

NT = (((1,), (1,)), ((), ()))


def params(mib, **kw):
    return pltpu.CompilerParams(vmem_limit_bytes=mib << 20, **kw)


def all_to_all(value):
    return lax.all_to_all(value, AXES, split_axis=0, concat_axis=0, tiled=True)


def mate(value):
    count = lax.axis_size("ctx")
    return lax.ppermute(value, "ctx", [(i, i ^ 1) for i in range(count)])


def swap_inner(value):
    heads = lax.axis_size("heads")
    return lax.ppermute(value, "heads", [(h, h ^ 1) for h in range(heads)])


def swap_outer(value):
    heads, ctx = lax.axis_size("heads"), lax.axis_size("ctx")
    pairs = []
    for i in range(1, heads * ctx - 1):
        j = i + 1 if i % 2 else i - 1
        pairs.append(tuple(b % heads * ctx + b // heads for b in (i, j)))
    return lax.ppermute(value, ("heads", "ctx"), pairs)


def pack_kernel(k_ref, v_ref, out_ref):
    for g in range(KVH):
        cols = slice(g * HD, (g + 1) * HD)
        out_ref[0, g] = k_ref[:, cols]
        out_ref[1, g] = v_ref[:, cols]


def pack(keys, values):
    return pl.pallas_call(
        pack_kernel,
        out_shape=jax.ShapeDtypeStruct((2, KVH, BLK, HD), BF16),
        compiler_params=params(58),
        name="pack",
    )(keys, values)


def side_of(i, heads):
    return i // heads % MATES


def select_kernel(heads, wanted_ref, in_ref, out_ref):
    count = in_ref.shape[0]
    globs = [in_ref[wanted_ref[count + slot]] for slot in range(NG)]
    for i in range(count):
        out_ref[i, 0] = in_ref[wanted_ref[i]]
        out_ref[i, 1] = globs[side_of(i, heads)]


def select(wanted, slices, heads):
    count, rows, _ = slices.shape
    if rows % 16:
        i = jnp.arange(count)
        glob = wanted[count + side_of(i, heads)]
        return slices[jnp.stack([wanted[i], glob], axis=1)]
    return pl.pallas_call(
        lambda *refs: select_kernel(heads, *refs),
        out_shape=jax.ShapeDtypeStruct((count, 2, rows, HD), BF16),
        in_specs=[
            pl.BlockSpec(memory_space=pltpu.SMEM),
            pl.BlockSpec(memory_space=pltpu.VMEM),
        ],
        out_specs=pl.BlockSpec(memory_space=pltpu.VMEM),
        compiler_params=params(8),
        name="select",
    )(wanted, slices)


def combine_kernel(heads, wanted_ref, in_ref, out_ref, acc_ref):
    count = in_ref.shape[0]
    acc_ref[...] = jnp.zeros_like(acc_ref)
    for side in range(MATES):
        total = None
        for i in range(count):
            if side_of(i, heads) == side:
                term = in_ref[i, 1].astype(F32)
                total = term if total is None else total + term
        acc_ref[wanted_ref[count + side]] += total
    for i in range(count):
        acc_ref[wanted_ref[i]] += in_ref[i, 0].astype(F32)
    out_ref[...] = acc_ref[...].astype(BF16)


def combine(wanted, terms, heads):
    count, _, rows, _ = terms.shape
    if rows % 16:
        i = jnp.arange(count)
        wide = terms.astype(F32)
        total = jnp.zeros((count, rows, HD), F32).at[wanted[i]].add(wide[:, 0])
        return total.at[wanted[count + side_of(i, heads)]].add(wide[:, 1]).astype(BF16)
    return pl.pallas_call(
        lambda *refs: combine_kernel(heads, *refs),
        out_shape=jax.ShapeDtypeStruct((count, rows, HD), BF16),
        in_specs=[
            pl.BlockSpec(memory_space=pltpu.SMEM),
            pl.BlockSpec(memory_space=pltpu.VMEM),
        ],
        out_specs=pl.BlockSpec(memory_space=pltpu.VMEM),
        scratch_shapes=[pltpu.VMEM((count, rows, HD), F32)],
        compiler_params=params(16),
        name="combine",
    )(wanted, terms)


def join_kernel(random_ref, glob_ref, other_ref, out_ref):
    out_ref[:, 0] = random_ref[...]
    out_ref[:, 1] = (glob_ref[...] + other_ref[...].astype(F32)).astype(BF16)


def join(random, glob, other):
    count, rows, _ = random.shape
    if rows % 16:
        total = (glob + other.astype(F32)).astype(BF16)
        return jnp.stack([random, total], axis=1)
    return pl.pallas_call(
        join_kernel,
        out_shape=jax.ShapeDtypeStruct((count, 2, rows, HD), BF16),
        compiler_params=params(8),
        name="join",
    )(random, glob, other)


def stacked(ref):
    return jnp.concatenate(
        [ref[:, h * HD : (h + 1) * HD] for h in range(GROUP)], axis=0
    )


def blocks_of(near, far_ref, other_ref):
    blocks = list(near)
    for ref, slot in ((far_ref, 1), (other_ref, 1), (far_ref, 0)):
        blocks.append(ref[:, slot].reshape(BLK, HD))
    return blocks


def dot_nt(a, b):
    return lax.dot_general(a, b, NT, preferred_element_type=F32)


def put_grads(rows, queries, douts, probs_ref, ds_ref, dests):
    dk = jnp.dot(ds_ref[rows], queries, preferred_element_type=F32) * SCALE
    dv = jnp.dot(probs_ref[rows], douts, preferred_element_type=F32)
    for i, dest in enumerate(dests):
        for kind, term in enumerate((dk, dv)):
            dest[kind] = term[i * BLK : (i + 1) * BLK].astype(dest.dtype)


def block_rows(b):
    return slice(b * BLK, (b + 1) * BLK)


def masked(edge_ref, b, scores):
    return jnp.where(edge_ref[0] == 0, scores, NEG_FILL) if b == 1 else scores


def scores_kernel(
    edge_ref, far_ref, other_ref, q_any, do_any, inner_any, outer_any, own_any,
    stats_ref, glob_ref, mate_ref, random_ref,
    s_ref, dp_ref, probs_ref, ds_ref, near_ref, tokens_ref, sem, token_sem,
):
    copies = [
        pltpu.make_async_copy(ref, near_ref.at[i], sem.at[i])
        for i, ref in enumerate((inner_any, outer_any, own_any))
    ]

    def token_copies(g):
        cols = pl.ds(pl.multiple_of(g * WIDE, WIDE), WIDE)
        return [
            pltpu.make_async_copy(
                ref.at[:, cols], tokens_ref.at[i, g], token_sem.at[i, g]
            )
            for i, ref in enumerate((q_any, do_any))
        ]

    for copy in copies:
        copy.start()
    for g in range(KVH):
        for copy in token_copies(g):
            copy.start()
    for copy in copies:
        copy.wait()
    share = far_ref.shape[1] // KVH

    def group(g, carry):
        for copy in token_copies(g):
            copy.wait()
        queries, douts = (stacked(tokens_ref.at[i, g]) for i in range(2))
        keys, values = (
            jnp.concatenate(
                blocks_of(
                    [near_ref[i, kind, g] for i in range(3)],
                    far_ref.at[kind, pl.ds(g * share, share)],
                    other_ref.at[kind, pl.ds(g * share, share)],
                ),
                axis=0,
            )
            for kind in range(2)
        )
        for part in range(WIDE // PART):
            cols = slice(part * PART, (part + 1) * PART)
            s = dot_nt(keys, queries[cols])
            dp_ref[...] = dot_nt(values, douts[cols])
            row_max = None
            for b in range(SLOTS):
                score = masked(edge_ref, b, s[block_rows(b)])
                s_ref[block_rows(b)] = score
                top = jnp.max(score, axis=0, keepdims=True)
                row_max = top if row_max is None else jnp.maximum(row_max, top)
            row_sum = jnp.zeros((1, PART), F32)
            centre = jnp.zeros((1, PART), F32)
            for b in range(SLOTS):
                w = jnp.exp2((s_ref[block_rows(b)] - row_max) * FACTOR)
                if b >= 3:
                    s_ref[block_rows(b)] = w
                row_sum = row_sum + jnp.sum(w, axis=0, keepdims=True)
                moved = w * dp_ref[block_rows(b)]
                centre = centre + jnp.sum(moved, axis=0, keepdims=True)
            inverse = 1.0 / row_sum
            centre = centre * inverse
            stats_ref[g, 0:1, cols] = row_max
            stats_ref[g, 1:2, cols] = inverse
            stats_ref[g, 2:3, cols] = centre
            for b in range(3, SLOTS):
                rows = block_rows(b)
                p = s_ref[rows] * inverse
                dest = block_rows(b - 3)
                probs_ref[dest, cols] = p.astype(BF16)
                ds_ref[dest, cols] = (p * (dp_ref[rows] - centre)).astype(BF16)
        dests = [ref.at[:, g] for ref in (glob_ref, mate_ref, random_ref)]
        put_grads(slice(None), queries, douts, probs_ref, ds_ref, dests)
        return carry

    lax.fori_loop(0, KVH, group, 0)


def again(edge_ref, first, keys, values, q, do, stats_ref, probs_ref, ds_ref, cols):
    row_max, inverse, centre = (stats_ref[0, i : i + 1, cols] for i in range(3))
    s, dp = dot_nt(keys, q), dot_nt(values, do)
    for b in range(keys.shape[0] // BLK):
        rows = block_rows(b)
        score = masked(edge_ref, first + b, s[rows])
        p = jnp.exp2((score - row_max) * FACTOR) * inverse
        probs_ref[rows, cols] = p.astype(BF16)
        ds_ref[rows, cols] = (p * (dp[rows] - centre)).astype(BF16)


def window_kernel(
    edge_ref, q_ref, do_ref, inner_ref, outer_ref, stats_ref,
    to_inner_ref, to_outer_ref, probs_ref, ds_ref,
):
    keys, values = (
        jnp.concatenate([inner_ref[kind, 0], outer_ref[kind, 0]], axis=0)
        for kind in range(2)
    )
    queries, douts = stacked(q_ref), stacked(do_ref)
    for part in range(WIDE // PART):
        cols = slice(part * PART, (part + 1) * PART)
        again(
            edge_ref, 0, keys, values, queries[cols], douts[cols],
            stats_ref, probs_ref, ds_ref, cols,
        )
    put_grads(
        slice(None), queries, douts, probs_ref, ds_ref,
        (to_inner_ref.at[:, 0], to_outer_ref.at[:, 0]),
    )


def outputs_kernel(
    edge_ref, q_ref, do_ref, own_ref, inner_ref, outer_ref, far_ref, other_ref,
    stats_ref, from_inner_ref, from_outer_ref, out_ref, dq_ref, near_ref, probs_ref, ds_ref,
):
    key_blocks, value_blocks = (
        blocks_of(
            [ref[kind, 0] for ref in (inner_ref, outer_ref, own_ref)],
            far_ref.at[kind],
            other_ref.at[kind],
        )
        for kind in range(2)
    )
    keys, values = (jnp.concatenate(x, axis=0) for x in (key_blocks, value_blocks))
    keys_t, values_t = (
        jnp.concatenate([x.T for x in blocks], axis=1)
        for blocks in (key_blocks, value_blocks)
    )
    queries, douts = stacked(q_ref), stacked(do_ref)
    for part in range(WIDE // PART):
        cols = slice(part * PART, (part + 1) * PART)
        again(
            edge_ref, 0, keys, values, queries[cols], douts[cols],
            stats_ref, probs_ref, ds_ref, cols,
        )
        out_t = jnp.dot(values_t, probs_ref[:, cols], preferred_element_type=F32)
        dq_t = jnp.dot(keys_t, ds_ref[:, cols], preferred_element_type=F32) * SCALE
        for i in range(PART // HD):
            place = slice(i * HD, (i + 1) * HD)
            dest = slice(part * PART + i * HD, part * PART + (i + 1) * HD)
            out_ref[:, dest] = out_t[:, place].T.astype(BF16)
            dq_ref[:, dest] = dq_t[:, place].T.astype(BF16)
    put_grads(block_rows(2), queries, douts, probs_ref, ds_ref, (near_ref.at[:, 0],))
    for kind in range(2):
        back = from_inner_ref[kind, 0].astype(F32) + from_outer_ref[kind, 0].astype(F32)
        near_ref[kind, 0] += back


def finish_kernel(near_ref, far_ref, dk_ref, dv_ref):
    for kind, dest in enumerate((dk_ref, dv_ref)):
        for g in range(KVH):
            total = near_ref[kind, g] + far_ref[kind, g].astype(F32)
            dest[:, g * HD : (g + 1) * HD] = total.astype(BF16)


def finish(near, far):
    shape = jax.ShapeDtypeStruct((BLK, KVH * HD), BF16)
    return pl.pallas_call(
        finish_kernel,
        out_shape=(shape, shape),
        compiler_params=params(8),
        name="finish",
    )(near, far)


def shards(queries, keys_in, values_in, cotangent, rand_blocks, glob_blocks):
    heads, ctx = lax.axis_size("heads"), lax.axis_size("ctx")
    count = heads * ctx
    mine = lax.axis_index("ctx") * heads + lax.axis_index("heads")
    edges = ((mine == 0) | (mine == count - 1)).astype(jnp.int32).reshape(1)
    wanted = jnp.concatenate([rand_blocks[:, 0], glob_blocks])
    rows = 2 * KVH * BLK // count
    share = BLK // rows if rows % 16 == 0 else 1
    token = pl.BlockSpec((BLK, WIDE), lambda g: (0, g))
    block = pl.BlockSpec((2, 1, BLK, HD), lambda g: (0, g, 0, 0))
    far_spec = pl.BlockSpec((2, share, 2, BLK // share, HD), lambda g: (0, g, 0, 0, 0))
    stat = pl.BlockSpec((1, 8, WIDE), lambda g: (g, 0, 0))
    vmem = pl.BlockSpec(memory_space=pltpu.VMEM)
    smem = pl.BlockSpec(memory_space=pltpu.SMEM)
    anywhere = pl.BlockSpec(memory_space=pl.ANY)
    low, wide = (jax.ShapeDtypeStruct((2, KVH, BLK, HD), dtype) for dtype in (BF16, F32))
    token_shape = jax.ShapeDtypeStruct(queries.shape, BF16)
    flops = 2 * H * BLK * SLOTS * BLK * HD

    def call(kernel, name, work, mib, ins, outs, scratch=(), **kw):
        return pl.pallas_call(
            kernel,
            in_specs=ins,
            out_specs=[spec for spec, _ in outs],
            out_shape=[shape for _, shape in outs],
            scratch_shapes=scratch,
            compiler_params=params(mib),
            cost_estimate=pl.CostEstimate(
                flops=int(work * flops), bytes_accessed=4 << 20, transcendentals=0
            ),
            name=name,
            **kw,
        )

    def low_pair(length):
        return [pltpu.VMEM((length * BLK, WIDE), BF16)] * 2

    grid = (KVH,)
    packed = pack(keys_in, values_in)
    slices = all_to_all(packed.reshape(count, rows, HD))
    inner, outer = swap_inner(packed), swap_outer(packed)
    slices, inner = lax.optimization_barrier((slices, inner))
    far = all_to_all(select(wanted, slices, heads))
    far, outer = lax.optimization_barrier((far, outer))
    if share == 1:
        far = far.reshape(2, KVH, BLK // rows, 2, rows, HD)
        far = jnp.transpose(far, (0, 1, 3, 2, 4, 5))
    far = far.reshape(2, KVH * share, 2, BLK // share, HD)
    other = mate(far)
    stats, glob, for_mate, random = call(
        scores_kernel,
        "scores",
        3,
        50,
        [smem, vmem, vmem] + [anywhere] * 5,
        [(vmem, jax.ShapeDtypeStruct((KVH, 8, WIDE), F32)), (vmem, wide)] + [(vmem, low)] * 2,
        [pltpu.VMEM((SLOTS * BLK, PART), F32)] * 2
        + low_pair(3)
        + [
            pltpu.VMEM((3, 2, KVH, BLK, HD), BF16),
            pltpu.VMEM((2, KVH, BLK, WIDE), BF16),
            pltpu.SemaphoreType.DMA((3,)),
            pltpu.SemaphoreType.DMA((2, KVH)),
        ],
    )(edges, far, other, queries, cotangent, inner, outer, packed)
    flat = (count, rows, HD)
    terms = join(random.reshape(flat), glob.reshape(flat), mate(for_mate).reshape(flat))
    arrived = all_to_all(terms)
    back = call(
        window_kernel, "window", 1, 56, [smem, token, token, block, block, stat],
        [(block, low)] * 2, low_pair(2), grid=grid,
    )(edges, queries, cotangent, inner, outer, stats)
    back = [swap_inner(back[0]), swap_outer(back[1])]
    arrived, *back = lax.optimization_barrier((arrived, *back))
    summed = combine(wanted, arrived, heads)
    returned = all_to_all(summed).reshape(2, KVH, BLK, HD)
    stats, summed = lax.optimization_barrier((stats, summed))
    attn_out, grad_query, near = call(
        outputs_kernel,
        "outputs",
        3,
        56,
        [smem, token, token] + [block] * 3 + [far_spec] * 2 + [stat, block, block],
        [(token, token_shape)] * 2 + [(block, wide)],
        low_pair(SLOTS),
        grid=grid,
    )(edges, queries, cotangent, packed, inner, outer, far, other, stats, *back)
    grad_keys, grad_values = finish(near, returned)
    return attn_out, grad_query, grad_keys, grad_values


def solution(mesh):
    spec = P(AXES, None)
    return jax.shard_map(
        shards,
        mesh=mesh,
        in_specs=(spec, spec, spec, spec, P(), P()),
        out_specs=(spec, spec, spec, spec),
        check_vma=False,
    )
```

time: 113 us -> 106 us (0.938)
  Pallas kernels: 35.2 us -> 30.6 us
    pallas_call x3, Pallas kernels: 27.9 us -> 24.4 us  [the longest x1 10.1 us: shards(): call(outputs_kernel, 'outputs', 3, 56, [smem, token, token] + [block] * 3...]
    all_to_all x4, waiting for transfers between devices: 20.5 us -> 19 us  [all_to_all(): return lax.all_to_all(value, AXES, split_axis=0, concat_axis=0, tiled=True)]
    pallas_call x1, Pallas kernels: 2.04 us -> 0.86 us  [join(): pl.pallas_call(join_kernel, out_shape=jax.ShapeDtypeStruct((count, 2, row...]
    unnamed x16 -> x24, local copies, waits for them, and re-layouts: 2.53 us -> 1.73 us
  transfers between devices with their start and end apart: 10 -> 10, of which waited for: 6 -> 6; matrix products, arithmetic and copies ran while one was open for 1% -> 0% of each run, Pallas kernels for 12% -> 14%
where the time goes in v5:
time: 106 us; the launch traced here: 105 us
  waiting for transfers between devices  43.6 us (41%)
  Pallas kernels  30.6 us (29%)
  starting transfers between devices  28.7 us (27%)
  local copies, waits for them, and re-layouts  1.73 us (2%)
    ppermute x2, waiting for transfers between devices, swap_inner(): return lax.ppermute(value, 'heads', [(h, h ^ 1) for h in range(heads)])  21.9 us
    all_to_all x4, starting transfers between devices, all_to_all(): return lax.all_to_all(value, AXES, split_axis=0, concat_axis=0, tiled=True)  21.2 us
    all_to_all x4, waiting for transfers between devices, all_to_all(): return lax.all_to_all(value, AXES, split_axis=0, concat_axis=0, tiled=True)  19 us
    pallas_call x1, Pallas kernels, shards(): call(outputs_kernel, 'outputs', 3, 56, [smem, token, token] + [block] * 3...  10.1 us
    pallas_call x1, Pallas kernels, shards(): call(scores_kernel, 'scores', 3, 50, [smem, vmem, vmem] + [anywhere] * 5,...  9.18 us
    pallas_call x1, Pallas kernels, shards(): call(window_kernel, 'window', 1, 56, [smem, token, token, block, block, s...  5.13 us
    ppermute x2, starting transfers between devices, swap_inner(): return lax.ppermute(value, 'heads', [(h, h ^ 1) for h in range(heads)])  3.6 us
    ppermute x2, waiting for transfers between devices, mate(): return lax.ppermute(value, 'ctx', [(i, i ^ 1) for i in range(count)])  2.7 us
  transfers between devices with their start and end apart: 10, of which 6 were waited for; matrix products, arithmetic and copies ran while one was open for 0% of the time, Pallas kernels for 14%

profile of v5, /device:TPU:0, one launch (start us, length us, event | category | flops | bytes accessed | tf_op | source)
XLA Modules:
  0.0 105.5 jit_solution(9959977095639508431)
XLA Ops:
  0.6 1.7 %pack.1.own_any.own_ref = bf16[2,4,128,128]{3,2,1,0:T(8,128)(2,1)} custom-call(bf16[128,512]{1,0:T(8,128)(2,1)} %k_ref.1, bf16[128,512]{1,0:T(8,128)(2,1)} %v_ref.1), custom_call_target="tpu_custom_call" | custom-call | tf_op jit(solution)/shard_map/pack/pallas_call | solution.py:65
  2.4 0.0 copy-start
  2.4 0.0 copy-start.10
  2.4 0.0 copy-start.11
  2.4 7.3 %all-to-all-start = ((bf16[32,32,128]{2,1,0:T(8,128)(2,1)}), bf16[32,32,128]{2,1,0:T(8,128)(2,1)S(1)}, u32[]{:S(2)}, u32[]{:S(2)}) async-start(bf16[32,32,128]{2,1,0:T(8,128)(2,1)} %bitcast.9), calls=%async_computation | async-start | bytes 524288 | tf_op jit(solution)/shard_map/all_to_all | solution.py:35
  9.7 0.0 copy-done
  9.7 0.0 copy-start.3
  9.7 1.8 %collective-permute-start = (bf16[2,4,128,128]{3,2,1,0:T(8,128)(2,1)S(1)}, bf16[2,4,128,128]{3,2,1,0:T(8,128)(2,1)S(1)}, u32[]{:S(2)}, u32[]{:S(2)}) collective-permute-start(bf16[2,4,128,128]{3,2,1,0:T(8,128)(2,1)S(1)} %copy-done), channel_id=1, source_target_pairs={{0,4},{4,0},{8,12},{12,8},{16,20},{20,16},{24,28},{28,24},{1,5},{5... | collective-permute-start | bytes 786440 | tf_op jit(solution)/shard_map/ppermute | solution.py:45
  11.5 0.0 copy-done.10
  11.5 0.0 copy-done.11
  11.5 0.1 pad_add_fusion.refs_0_
  11.6 9.4 %collective-permute-done.inner_any.inner_ref = bf16[2,4,128,128]{3,2,1,0:T(8,128)(2,1)S(1)} collective-permute-done((bf16[2,4,128,128]{3,2,1,0:T(8,128)(2,1)S(1)}, bf16[2,4,128,128]{3,2,1,0:T(8,128)(2,1)S(1)}, u32[]{:S(2)}, u32[]{:S(2)}) %collective-permute-start) | collective-permute-done | bytes 262176 | tf_op jit(solution)/shard_map/ppermute | solution.py:45
  21.0 0.0 copy-start.5
  21.0 0.0 all-to-all-done.refs_1_
  21.0 1.4 %select.1 = bf16[32,2,32,128]{3,2,1,0:T(8,128)(2,1)} custom-call(s32[34]{0:T(128)S(1)} %pad_add_fusion.refs_0_, bf16[32,32,128]{2,1,0:T(8,128)(2,1)S(1)} %all-to-all-done.refs_1_), custom_call_target="tpu_custom_call" | custom-call | tf_op jit(solution)/shard_map/select/pallas_call | solution.py:91
  22.4 4.5 %all-to-all-start.1 = ((bf16[32,2,32,128]{3,2,1,0:T(8,128)(2,1)}), bf16[32,2,32,128]{3,2,1,0:T(8,128)(2,1)S(1)}, u32[]{:S(2)}, u32[]{:S(2)}) async-start(bf16[32,2,32,128]{3,2,1,0:T(8,128)(2,1)} %select.1), calls=%async_computation.1 | async-start | bytes 1048576 | tf_op jit(solution)/shard_map/all_to_all | solution.py:35
  26.9 0.7 collective-permute-start.1
  27.6 0.0 collective-permute-done.1.outer_any.outer_ref
  27.6 0.0 copy-start.6
  27.6 18.5 %all-to-all-done.1 = bf16[32,2,32,128]{3,2,1,0:T(8,128)(2,1)S(1)} async-done(((bf16[32,2,32,128]{3,2,1,0:T(8,128)(2,1)}), bf16[32,2,32,128]{3,2,1,0:T(8,128)(2,1)S(1)}, u32[]{:S(2)}, u32[]{:S(2)}) %all-to-all-start.1) | async-done | bytes 524320 | tf_op jit(solution)/shard_map/all_to_all | solution.py:35
  46.1 0.0 copy-start.2
  46.1 2.2 %collective-permute-start.2 = (bf16[2,16,2,32,128]{4,3,2,1,0:T(8,128)(2,1)S(1)}, bf16[2,16,2,32,128]{4,3,2,1,0:T(8,128)(2,1)S(1)}, u32[]{:S(2)}, u32[]{:S(2)}) collective-permute-start(bf16[2,16,2,32,128]{4,3,2,1,0:T(8,128)(2,1)S(1)} %bitcast.11), channel_id=1, source_target_pairs={{0,1},{1,0},{2,3},{3,2},{4,5},{5,4},{6,7},{7,6},{8,9},{9,8},{10,11... | collective-permute-start | bytes 1572872 | tf_op jit(solution)/shard_map/ppermute | solution.py:40
  48.3 1.5 %collective-permute-done.2.other_ref = bf16[2,16,2,32,128]{4,3,2,1,0:T(8,128)(2,1)S(1)} collective-permute-done((bf16[2,16,2,32,128]{4,3,2,1,0:T(8,128)(2,1)S(1)}, bf16[2,16,2,32,128]{4,3,2,1,0:T(8,128)(2,1)S(1)}, u32[]{:S(2)}, u32[]{:S(2)}) %collective-permute-start.2) | collective-permute-done | bytes 524320 | tf_op jit(solution)/shard_map/ppermute | solution.py:40
  49.8 0.0 copy-start.4
  49.8 0.0 copy-done.5
  49.8 0.0 copy-done.3
  49.8 9.2 %scores.1 = (f32[4,8,1024]{2,1,0:T(8,128)S(1)}, f32[2,4,128,128]{3,2,1,0:T(8,128)S(1)}, bf16[2,4,128,128]{3,2,1,0:T(8,128)(2,1)S(1)}, bf16[2,4,128,128]{3,2,1,0:T(8,128)(2,1)S(1)}) custom-call(s32[1]{0:T(128)} %bitcast.edge_ref, bf16[2,16,2,32,128]{4,3,2,1,0:T(8,128)(2,1)S(1)} %bitcast.12, bf16[2,16,2,32,128]{4,3,2,1,0:T(8,128)(2,1)S(1)} %collective-permute-done.2.other_ref, ...), custom_call_target="tpu_custom_call" | custom-call | flops 2415919104 | bytes 4194304 | tf_op jit(solution)/shard_map/scores/pallas_call | solution.py:406
  59.0 0.0 copy-done.6
  59.0 0.0 copy-done.2
  59.0 0.0 copy-done.4
  59.0 0.0 copy-start.7
  59.0 0.6 copy-done.7
  59.7 0.4 collective-permute-start.3
  60.1 1.2 %collective-permute-done.3 = bf16[2,4,128,128]{3,2,1,0:T(8,128)(2,1)S(1)} collective-permute-done((bf16[2,4,128,128]{3,2,1,0:T(8,128)(2,1)S(1)}, bf16[2,4,128,128]{3,2,1,0:T(8,128)(2,1)S(1)}, u32[]{:S(2)}, u32[]{:S(2)}) %collective-permute-start.3) | collective-permute-done | bytes 262176 | tf_op jit(solution)/shard_map/ppermute | solution.py:40
  61.2 0.9 join.1
  62.1 3.1 %all-to-all-start.2 = ((bf16[32,2,32,128]{3,2,1,0:T(8,128)(2,1)}), bf16[32,2,32,128]{3,2,1,0:T(8,128)(2,1)S(1)}, u32[]{:S(2)}, u32[]{:S(2)}) async-start(bf16[32,2,32,128]{3,2,1,0:T(8,128)(2,1)} %join.1), calls=%async_computation.2 | async-start | bytes 1048576 | tf_op jit(solution)/shard_map/all_to_all | solution.py:35
  65.2 5.1 %window.1 = (bf16[2,4,128,128]{3,2,1,0:T(8,128)(2,1)}, bf16[2,4,128,128]{3,2,1,0:T(8,128)(2,1)}) custom-call(s32[1]{0:T(128)} %bitcast.edge_ref, bf16[128,4096]{1,0:T(8,128)(2,1)} %q_ref.3, bf16[128,4096]{1,0:T(8,128)(2,1)} %do_ref.3, bf16[2,4,128,128]{3,2,1,0:T(8,128)(2,1)} %copy-done.5, bf16[2,4,128,128]{3,2,1,0:T(8,128)(2,1)} %copy-done.6, ...), custom_call_target="tpu_custom_call" | custom-call | flops 805306368 | bytes 4194304 | tf_op jit(solution)/shard_map/window/pallas_call | solution.py:425
  70.3 1.8 %collective-permute-start.4 = (bf16[2,4,128,128]{3,2,1,0:T(8,128)(2,1)}, bf16[2,4,128,128]{3,2,1,0:T(8,128)(2,1)S(1)}, u32[]{:S(2)}, u32[]{:S(2)}) collective-permute-start(bf16[2,4,128,128]{3,2,1,0:T(8,128)(2,1)} %get-tuple-element.31), channel_id=1, source_target_pairs={{0,4},{4,0},{8,12},{12,8},{16,20},{20,16},{24,28},{28,24},{1,5},{5... | collective-permute-start | bytes 786440 | tf_op jit(solution)/shard_map/ppermute | solution.py:45
  72.1 0.7 collective-permute-start.5
  72.8 12.5 %collective-permute-done.4.from_inner_ref = bf16[2,4,128,128]{3,2,1,0:T(8,128)(2,1)S(1)} collective-permute-done((bf16[2,4,128,128]{3,2,1,0:T(8,128)(2,1)}, bf16[2,4,128,128]{3,2,1,0:T(8,128)(2,1)S(1)}, u32[]{:S(2)}, u32[]{:S(2)}) %collective-permute-start.4) | collective-permute-done | bytes 262176 | tf_op jit(solution)/shard_map/ppermute | solution.py:45
  85.3 0.0 copy-start.8
  85.3 0.0 collective-permute-done.5.from_outer_ref
  85.3 0.0 copy-start.9
  85.3 0.0 all-to-all-done.2.refs_1_
  85.3 1.4 %combine.1 = bf16[32,32,128]{2,1,0:T(8,128)(2,1)} custom-call(s32[34]{0:T(128)S(1)} %pad_add_fusion.refs_0_, bf16[32,2,32,128]{3,2,1,0:T(8,128)(2,1)S(1)} %all-to-all-done.2.refs_1_), custom_call_target="tpu_custom_call" | custom-call | tf_op jit(solution)/shard_map/combine/pallas_call | solution.py:126
  86.7 0.0 copy-done.8
  86.7 0.0 copy-done.9
  86.8 6.3 %all-to-all-start.3 = ((bf16[32,32,128]{2,1,0:T(8,128)(2,1)}), bf16[32,32,128]{2,1,0:T(8,128)(2,1)S(1)}, u32[]{:S(2)}, u32[]{:S(2)}) async-start(bf16[32,32,128]{2,1,0:T(8,128)(2,1)} %combine.1), calls=%async_computation.3 | async-start | bytes 524288 | tf_op jit(solution)/shard_map/all_to_all | solution.py:35
  93.0 10.1 %outputs.1 = (bf16[128,4096]{1,0:T(8,128)(2,1)}, bf16[128,4096]{1,0:T(8,128)(2,1)}, f32[2,4,128,128]{3,2,1,0:T(8,128)}) custom-call(s32[1]{0:T(128)} %bitcast.edge_ref, bf16[128,4096]{1,0:T(8,128)(2,1)} %q_ref.3, bf16[128,4096]{1,0:T(8,128)(2,1)} %do_ref.3, bf16[2,4,128,128]{3,2,1,0:T(8,128)(2,1)} %pack.1.own_any.own_ref, ...), custom_call_target="tpu_custom_call" | custom-call | flops 2415919104 | bytes 4194304 | tf_op jit(solution)/shard_map/outputs/pallas_call | solution.py:434
  103.1 0.6 all-to-all-done.3
  103.7 0.0 copy-start.1
  103.7 1.0 copy-done.1
  104.7 0.7 finish.1
Async XLA Ops:
  2.4 7.3 %copy-start = (bf16[2,4,128,128]{3,2,1,0:T(8,128)(2,1)S(1)}, bf16[2,4,128,128]{3,2,1,0:T(8,128)(2,1)}, u32[]{:S(2)}) copy-start(bf16[2,4,128,128]{3,2,1,0:T(8,128)(2,1)} %pack.1.own_any.own_ref) | copy-start | bytes 786436
  2.4 9.2 %copy-start.10 = (s32[2]{0:T(128)S(1)}, s32[2]{0:T(128)}, u32[]{:S(2)}) copy-start(s32[2]{0:T(128)} %param.11) | copy-start | bytes 28
  2.4 9.2 %copy-start.11 = (s32[32,1]{0,1:T(1,128)S(1)}, s32[32,1]{0,1:T(1,128)}, u32[]{:S(2)}) copy-start(s32[32,1]{0,1:T(1,128)} %param.10) | copy-start | bytes 388
  2.4 18.6 %all-to-all-start = ((bf16[32,32,128]{2,1,0:T(8,128)(2,1)}), bf16[32,32,128]{2,1,0:T(8,128)(2,1)S(1)}, u32[]{:S(2)}, u32[]{:S(2)}) async-start(bf16[32,32,128]{2,1,0:T(8,128)(2,1)} %bitcast.9), calls=%async_computation | async-start | bytes 524288 | tf_op jit(solution)/shard_map/all_to_all | solution.py:35
  9.7 40.1 %copy-start.3 = (bf16[128,4096]{1,0:T(8,128)(2,1)S(1)}, bf16[128,4096]{1,0:T(8,128)(2,1)}, u32[]{:S(2)}) copy-start(bf16[128,4096]{1,0:T(8,128)(2,1)} %q_ref.3) | copy-start | bytes 3145732
  9.7 11.3 %collective-permute-start = (bf16[2,4,128,128]{3,2,1,0:T(8,128)(2,1)S(1)}, bf16[2,4,128,128]{3,2,1,0:T(8,128)(2,1)S(1)}, u32[]{:S(2)}, u32[]{:S(2)}) collective-permute-start(bf16[2,4,128,128]{3,2,1,0:T(8,128)(2,1)S(1)} %copy-done), channel_id=1, source_target_pairs={{0,4},{4,0},{8,12},{12,8},{16,20},{20,16},{24,28},{28,24},{1,5},{5... | collective-permute-start | bytes 786440 | tf_op jit(solution)/shard_map/ppermute | solution.py:45
  21.0 28.8 %copy-start.5 = (bf16[2,4,128,128]{3,2,1,0:T(8,128)(2,1)}, bf16[2,4,128,128]{3,2,1,0:T(8,128)(2,1)S(1)}, u32[]{:S(2)}) copy-start(bf16[2,4,128,128]{3,2,1,0:T(8,128)(2,1)S(1)} %collective-permute-done.inner_any.inner_ref) | copy-start | bytes 786436
  22.4 23.7 %all-to-all-start.1 = ((bf16[32,2,32,128]{3,2,1,0:T(8,128)(2,1)}), bf16[32,2,32,128]{3,2,1,0:T(8,128)(2,1)S(1)}, u32[]{:S(2)}, u32[]{:S(2)}) async-start(bf16[32,2,32,128]{3,2,1,0:T(8,128)(2,1)} %select.1), calls=%async_computation.1 | async-start | bytes 1048576 | tf_op jit(solution)/shard_map/all_to_all | solution.py:35
  26.9 0.7 collective-permute-start.1
  27.6 31.4 %copy-start.6 = (bf16[2,4,128,128]{3,2,1,0:T(8,128)(2,1)}, bf16[2,4,128,128]{3,2,1,0:T(8,128)(2,1)S(1)}, u32[]{:S(2)}) copy-start(bf16[2,4,128,128]{3,2,1,0:T(8,128)(2,1)S(1)} %collective-permute-done.1.outer_any.outer_ref) | copy-start | bytes 786436
  46.1 12.9 %copy-start.2 = (bf16[32,2,32,128]{3,2,1,0:T(8,128)(2,1)}, bf16[32,2,32,128]{3,2,1,0:T(8,128)(2,1)S(1)}, u32[]{:S(2)}) copy-start(bf16[32,2,32,128]{3,2,1,0:T(8,128)(2,1)S(1)} %all-to-all-done.1) | copy-start | bytes 1572868
  46.1 3.7 %collective-permute-start.2 = (bf16[2,16,2,32,128]{4,3,2,1,0:T(8,128)(2,1)S(1)}, bf16[2,16,2,32,128]{4,3,2,1,0:T(8,128)(2,1)S(1)}, u32[]{:S(2)}, u32[]{:S(2)}) collective-permute-start(bf16[2,16,2,32,128]{4,3,2,1,0:T(8,128)(2,1)S(1)} %bitcast.11), channel_id=1, source_target_pairs={{0,1},{1,0},{2,3},{3,2},{4,5},{5,4},{6,7},{7,6},{8,9},{9,8},{10,11... | collective-permute-start | bytes 1572872 | tf_op jit(solution)/shard_map/ppermute | solution.py:40
  49.8 9.2 %copy-start.4 = (bf16[2,16,2,32,128]{4,3,2,1,0:T(8,128)(2,1)}, bf16[2,16,2,32,128]{4,3,2,1,0:T(8,128)(2,1)S(1)}, u32[]{:S(2)}) copy-start(bf16[2,16,2,32,128]{4,3,2,1,0:T(8,128)(2,1)S(1)} %collective-permute-done.2.other_ref) | copy-start | bytes 1572868
  59.0 0.7 copy-start.7
  59.7 1.5 %collective-permute-start.3 = (bf16[2,4,128,128]{3,2,1,0:T(8,128)(2,1)S(1)}, bf16[2,4,128,128]{3,2,1,0:T(8,128)(2,1)S(1)}, u32[]{:S(2)}, u32[]{:S(2)}) collective-permute-start(bf16[2,4,128,128]{3,2,1,0:T(8,128)(2,1)S(1)} %get-tuple-element.30), channel_id=1, source_target_pairs={{0,1},{1,0},{2,3},{3,2},{4,5},{5,4},{6,7},{7,6},{8,9},{9,8},{10,11... | collective-permute-start | bytes 786440 | tf_op jit(solution)/shard_map/ppermute | solution.py:40
  62.1 23.2 %all-to-all-start.2 = ((bf16[32,2,32,128]{3,2,1,0:T(8,128)(2,1)}), bf16[32,2,32,128]{3,2,1,0:T(8,128)(2,1)S(1)}, u32[]{:S(2)}, u32[]{:S(2)}) async-start(bf16[32,2,32,128]{3,2,1,0:T(8,128)(2,1)} %join.1), calls=%async_computation.2 | async-start | bytes 1048576 | tf_op jit(solution)/shard_map/all_to_all | solution.py:35
  70.3 15.0 %collective-permute-start.4 = (bf16[2,4,128,128]{3,2,1,0:T(8,128)(2,1)}, bf16[2,4,128,128]{3,2,1,0:T(8,128)(2,1)S(1)}, u32[]{:S(2)}, u32[]{:S(2)}) collective-permute-start(bf16[2,4,128,128]{3,2,1,0:T(8,128)(2,1)} %get-tuple-element.31), channel_id=1, source_target_pairs={{0,4},{4,0},{8,12},{12,8},{16,20},{20,16},{24,28},{28,24},{1,5},{5... | collective-permute-start | bytes 786440 | tf_op jit(solution)/shard_map/ppermute | solution.py:45
  72.1 13.2 %collective-permute-start.5 = (bf16[2,4,128,128]{3,2,1,0:T(8,128)(2,1)}, bf16[2,4,128,128]{3,2,1,0:T(8,128)(2,1)S(1)}, u32[]{:S(2)}, u32[]{:S(2)}) collective-permute-start(bf16[2,4,128,128]{3,2,1,0:T(8,128)(2,1)} %get-tuple-element.32), channel_id=1, source_target_pairs={{4,8},{8,4},{12,16},{16,12},{20,24},{24,20},{28,1},{1,28},{5,9},{9... | collective-permute-start | bytes 786440 | tf_op jit(solution)/shard_map/ppermute | solution.py:54
  85.3 1.4 %copy-start.8 = (bf16[2,4,128,128]{3,2,1,0:T(8,128)(2,1)}, bf16[2,4,128,128]{3,2,1,0:T(8,128)(2,1)S(1)}, u32[]{:S(2)}) copy-start(bf16[2,4,128,128]{3,2,1,0:T(8,128)(2,1)S(1)} %collective-permute-done.4.from_inner_ref) | copy-start | bytes 786436
  85.3 1.4 %copy-start.9 = (bf16[2,4,128,128]{3,2,1,0:T(8,128)(2,1)}, bf16[2,4,128,128]{3,2,1,0:T(8,128)(2,1)S(1)}, u32[]{:S(2)}) copy-start(bf16[2,4,128,128]{3,2,1,0:T(8,128)(2,1)S(1)} %collective-permute-done.5.from_outer_ref) | copy-start | bytes 786436
  86.8 16.9 %all-to-all-start.3 = ((bf16[32,32,128]{2,1,0:T(8,128)(2,1)}), bf16[32,32,128]{2,1,0:T(8,128)(2,1)S(1)}, u32[]{:S(2)}, u32[]{:S(2)}) async-start(bf16[32,32,128]{2,1,0:T(8,128)(2,1)} %combine.1), calls=%async_computation.3 | async-start | bytes 524288 | tf_op jit(solution)/shard_map/all_to_all | solution.py:35
  103.7 1.0 copy-start.1

commit v6 on v5

--- a/solution.py
+++ b/solution.py
@@ -20,6 +20,7 @@
 SLOTS = 3 + NG + 1
 WIDE = GROUP * BLK
 PART = WIDE
+PIECE = WIDE // 4
 FACTOR = SCALE / math.log(2.0)
 BF16 = jnp.bfloat16
 F32 = jnp.float32
@@ -188,15 +189,28 @@
     return jnp.where(edge_ref[0] == 0, scores, NEG_FILL) if b == 1 else scores
 
 
+def first_kernel(q_ref, do_ref, own_ref, inner_ref, stats_ref):
+    keys, values = (
+        jnp.concatenate([own_ref[kind, 0], inner_ref[kind, 0]], axis=0)
+        for kind in range(2)
+    )
+    queries, douts = stacked(q_ref), stacked(do_ref)
+    for part in range(WIDE // PART):
+        cols = slice(part * PART, (part + 1) * PART)
+        s, dp = dot_nt(keys, queries[cols]), dot_nt(values, douts[cols])
+        row_max = jnp.max(s, axis=0, keepdims=True)
+        w = jnp.exp2((s - row_max) * FACTOR)
+        stats_ref[0, 0:1, cols] = row_max
+        stats_ref[0, 1:2, cols] = jnp.sum(w, axis=0, keepdims=True)
+        stats_ref[0, 2:3, cols] = jnp.sum(w * dp, axis=0, keepdims=True)
+
+
 def scores_kernel(
-    edge_ref, far_ref, other_ref, q_any, do_any, inner_any, outer_any, own_any,
+    edge_ref, far_ref, other_ref, first_ref, q_any, do_any, outer_any,
     stats_ref, glob_ref, mate_ref, random_ref,
-    s_ref, dp_ref, probs_ref, ds_ref, near_ref, tokens_ref, sem, token_sem,
+    s_ref, dp_ref, probs_ref, ds_ref, outer_ref, tokens_ref, sem, token_sem,
 ):
-    copies = [
-        pltpu.make_async_copy(ref, near_ref.at[i], sem.at[i])
-        for i, ref in enumerate((inner_any, outer_any, own_any))
-    ]
+    outer_copy = pltpu.make_async_copy(outer_any, outer_ref, sem)
 
     def token_copies(g):
         cols = pl.ds(pl.multiple_of(g * WIDE, WIDE), WIDE)
@@ -207,58 +221,56 @@
             for i, ref in enumerate((q_any, do_any))
         ]
 
-    for copy in copies:
-        copy.start()
+    outer_copy.start()
     for g in range(KVH):
         for copy in token_copies(g):
             copy.start()
-    for copy in copies:
-        copy.wait()
+    outer_copy.wait()
     share = far_ref.shape[1] // KVH
+    count = SLOTS - 2
 
     def group(g, carry):
         for copy in token_copies(g):
             copy.wait()
         queries, douts = (stacked(tokens_ref.at[i, g]) for i in range(2))
         keys, values = (
-            jnp.concatenate(
-                blocks_of(
-                    [near_ref[i, kind, g] for i in range(3)],
-                    far_ref.at[kind, pl.ds(g * share, share)],
-                    other_ref.at[kind, pl.ds(g * share, share)],
-                ),
-                axis=0,
+            blocks_of(
+                [outer_ref[kind, g]],
+                far_ref.at[kind, pl.ds(g * share, share)],
+                other_ref.at[kind, pl.ds(g * share, share)],
             )
             for kind in range(2)
         )
-        for part in range(WIDE // PART):
-            cols = slice(part * PART, (part + 1) * PART)
-            s = dot_nt(keys, queries[cols])
-            dp_ref[...] = dot_nt(values, douts[cols])
-            row_max = None
-            for b in range(SLOTS):
-                score = masked(edge_ref, b, s[block_rows(b)])
+        for piece in range(WIDE // PIECE):
+            cols = slice(piece * PIECE, (piece + 1) * PIECE)
+            first_max = first_ref[g, 0:1, cols]
+            row_max = first_max
+            for b in range(count):
+                score = dot_nt(keys[b], queries[cols])
+                if b == 0:
+                    score = jnp.where(edge_ref[0] == 0, score, NEG_FILL)
                 s_ref[block_rows(b)] = score
-                top = jnp.max(score, axis=0, keepdims=True)
-                row_max = top if row_max is None else jnp.maximum(row_max, top)
-            row_sum = jnp.zeros((1, PART), F32)
-            centre = jnp.zeros((1, PART), F32)
-            for b in range(SLOTS):
+                row_max = jnp.maximum(row_max, jnp.max(score, axis=0, keepdims=True))
+            scale = jnp.exp2((first_max - row_max) * FACTOR)
+            row_sum = first_ref[g, 1:2, cols] * scale
+            centre = first_ref[g, 2:3, cols] * scale
+            for b in range(count):
                 w = jnp.exp2((s_ref[block_rows(b)] - row_max) * FACTOR)
-                if b >= 3:
+                if b >= 1:
                     s_ref[block_rows(b)] = w
+                dp = dot_nt(values[b], douts[cols])
+                dp_ref[block_rows(b)] = dp
                 row_sum = row_sum + jnp.sum(w, axis=0, keepdims=True)
-                moved = w * dp_ref[block_rows(b)]
-                centre = centre + jnp.sum(moved, axis=0, keepdims=True)
+                centre = centre + jnp.sum(w * dp, axis=0, keepdims=True)
             inverse = 1.0 / row_sum
             centre = centre * inverse
             stats_ref[g, 0:1, cols] = row_max
             stats_ref[g, 1:2, cols] = inverse
             stats_ref[g, 2:3, cols] = centre
-            for b in range(3, SLOTS):
+            for b in range(1, count):
                 rows = block_rows(b)
                 p = s_ref[rows] * inverse
-                dest = block_rows(b - 3)
+                dest = block_rows(b - 1)
                 probs_ref[dest, cols] = p.astype(BF16)
                 ds_ref[dest, cols] = (p * (dp_ref[rows] - centre)).astype(BF16)
         dests = [ref.at[:, g] for ref in (glob_ref, mate_ref, random_ref)]
@@ -370,6 +382,7 @@
     smem = pl.BlockSpec(memory_space=pltpu.SMEM)
     anywhere = pl.BlockSpec(memory_space=pl.ANY)
     low, wide = (jax.ShapeDtypeStruct((2, KVH, BLK, HD), dtype) for dtype in (BF16, F32))
+    stat_shape = jax.ShapeDtypeStruct((KVH, 8, WIDE), F32)
     token_shape = jax.ShapeDtypeStruct(queries.shape, BF16)
     flops = 2 * H * BLK * SLOTS * BLK * HD
 
@@ -397,7 +410,11 @@
     inner, outer = swap_inner(packed), swap_outer(packed)
     slices, inner = lax.optimization_barrier((slices, inner))
     far = all_to_all(select(wanted, slices, heads))
-    far, outer = lax.optimization_barrier((far, outer))
+    first = call(
+        first_kernel, "first", 1, 56, [token, token, block, block],
+        [(stat, stat_shape)], grid=grid,
+    )(queries, cotangent, packed, inner)[0]
+    far, outer, first = lax.optimization_barrier((far, outer, first))
     if share == 1:
         far = far.reshape(2, KVH, BLK // rows, 2, rows, HD)
         far = jnp.transpose(far, (0, 1, 3, 2, 4, 5))
@@ -408,22 +425,22 @@
         "scores",
         3,
         50,
-        [smem, vmem, vmem] + [anywhere] * 5,
-        [(vmem, jax.ShapeDtypeStruct((KVH, 8, WIDE), F32)), (vmem, wide)] + [(vmem, low)] * 2,
-        [pltpu.VMEM((SLOTS * BLK, PART), F32)] * 2
+        [smem, vmem, vmem, vmem] + [anywhere] * 3,
+        [(vmem, stat_shape), (vmem, wide)] + [(vmem, low)] * 2,
+        [pltpu.VMEM(((SLOTS - 2) * BLK, PIECE), F32)] * 2
         + low_pair(3)
         + [
-            pltpu.VMEM((3, 2, KVH, BLK, HD), BF16),
+            pltpu.VMEM((2, KVH, BLK, HD), BF16),
             pltpu.VMEM((2, KVH, BLK, WIDE), BF16),
-            pltpu.SemaphoreType.DMA((3,)),
+            pltpu.SemaphoreType.DMA,
             pltpu.SemaphoreType.DMA((2, KVH)),
         ],
-    )(edges, far, other, queries, cotangent, inner, outer, packed)
+    )(edges, far, other, first, queries, cotangent, outer)
     flat = (count, rows, HD)
     terms = join(random.reshape(flat), glob.reshape(flat), mate(for_mate).reshape(flat))
     arrived = all_to_all(terms)
     back = call(
-        window_kernel, "window", 1, 56, [smem, token, token, block, block, stat],
+        window_kernel, "window", 1, 53, [smem, token, token, block, block, stat],
         [(block, low)] * 2, low_pair(2), grid=grid,
     )(edges, queries, cotangent, inner, outer, stats)
     back = [swap_inner(back[0]), swap_outer(back[1])]
@@ -435,7 +452,7 @@
         outputs_kernel,
         "outputs",
         3,
-        56,
+        53,
         [smem, token, token] + [block] * 3 + [far_spec] * 2 + [stat, block, block],
         [(token, token_shape)] * 2 + [(block, wide)],
         low_pair(SLOTS),

time: 106 us -> 105 us (level)
  waiting for transfers between devices: 43.6 us -> 39.8 us
  Pallas kernels: 30.6 us -> 33 us
    all_to_all x4, waiting for transfers between devices: 19 us -> 14.4 us  [all_to_all(): return lax.all_to_all(value, AXES, split_axis=0, concat_axis=0, tiled=True)]
    pallas_call x3 -> x4, Pallas kernels: 24.4 us -> 26.9 us  [the longest x1 10 us: shards(): call(outputs_kernel, 'outputs', 3, 53, [smem, token, token] + [block] * 3...]
    unnamed x24 -> x30, local copies, waits for them, and re-layouts: 1.73 us -> 2.12 us
  transfers between devices with their start and end apart: 10 -> 10, of which waited for: 6 -> 6; matrix products, arithmetic and copies ran while one was open for 0% -> 0% of each run, Pallas kernels for 14% -> 18%
where the time goes in v6:
time: 105 us; the launch traced here: 104 us
  waiting for transfers between devices  39.8 us (38%)
  Pallas kernels  33 us (31%)
  starting transfers between devices  28.3 us (27%)
  local copies, waits for them, and re-layouts  2.12 us (2%)
    ppermute x2, waiting for transfers between devices, swap_inner(): return lax.ppermute(value, 'heads', [(h, h ^ 1) for h in range(heads)])  22.6 us
    all_to_all x4, starting transfers between devices, all_to_all(): return lax.all_to_all(value, AXES, split_axis=0, concat_axis=0, tiled=True)  20.6 us
    all_to_all x4, waiting for transfers between devices, all_to_all(): return lax.all_to_all(value, AXES, split_axis=0, concat_axis=0, tiled=True)  14.4 us
    pallas_call x1, Pallas kernels, shards(): call(outputs_kernel, 'outputs', 3, 53, [smem, token, token] + [block] * 3...  10 us
    pallas_call x1, Pallas kernels, shards(): call(scores_kernel, 'scores', 3, 50, [smem, vmem, vmem, vmem] + [anywhere...  7.89 us
    pallas_call x1, Pallas kernels, shards(): call(first_kernel, 'first', 1, 56, [token, token, block, block], [(stat,...  4.49 us
    pallas_call x1, Pallas kernels, shards(): call(window_kernel, 'window', 1, 53, [smem, token, token, block, block, s...  4.44 us
    ppermute x2, starting transfers between devices, swap_inner(): return lax.ppermute(value, 'heads', [(h, h ^ 1) for h in range(heads)])  3.66 us
  transfers between devices with their start and end apart: 10, of which 6 were waited for; matrix products, arithmetic and copies ran while one was open for 0% of the time, Pallas kernels for 18%

profile of v6, /device:TPU:0, one launch (start us, length us, event | category | flops | bytes accessed | tf_op | source)
XLA Modules:
  0.0 104.1 jit_solution(1432131399681281997)
XLA Ops:
  0.6 1.7 %pack.1.own_ref = bf16[2,4,128,128]{3,2,1,0:T(8,128)(2,1)} custom-call(bf16[128,512]{1,0:T(8,128)(2,1)} %k_ref.1, bf16[128,512]{1,0:T(8,128)(2,1)} %v_ref.1), custom_call_target="tpu_custom_call" | custom-call | tf_op jit(solution)/shard_map/pack/pallas_call | solution.py:66
  2.3 0.0 copy-start
  2.3 7.3 %all-to-all-start = ((bf16[32,32,128]{2,1,0:T(8,128)(2,1)}), bf16[32,32,128]{2,1,0:T(8,128)(2,1)S(1)}, u32[]{:S(2)}, u32[]{:S(2)}) async-start(bf16[32,32,128]{2,1,0:T(8,128)(2,1)} %bitcast.9), calls=%async_computation | async-start | bytes 524288 | tf_op jit(solution)/shard_map/all_to_all | solution.py:36
  9.7 0.0 copy-done
  9.7 0.0 copy-start.13
  9.7 0.0 copy-start.14
  9.7 1.8 %collective-permute-start = (bf16[2,4,128,128]{3,2,1,0:T(8,128)(2,1)S(1)}, bf16[2,4,128,128]{3,2,1,0:T(8,128)(2,1)S(1)}, u32[]{:S(2)}, u32[]{:S(2)}) collective-permute-start(bf16[2,4,128,128]{3,2,1,0:T(8,128)(2,1)S(1)} %copy-done), channel_id=1, source_target_pairs={{0,4},{4,0},{8,12},{12,8},{16,20},{20,16},{24,28},{28,24},{1,5},{5... | collective-permute-start | bytes 786440 | tf_op jit(solution)/shard_map/ppermute | solution.py:46
  11.5 0.0 copy-done.13
  11.5 0.0 copy-done.14
  11.5 0.1 pad_add_fusion.refs_0_
  11.6 9.3 %collective-permute-done.inner_ref = bf16[2,4,128,128]{3,2,1,0:T(8,128)(2,1)S(1)} collective-permute-done((bf16[2,4,128,128]{3,2,1,0:T(8,128)(2,1)S(1)}, bf16[2,4,128,128]{3,2,1,0:T(8,128)(2,1)S(1)}, u32[]{:S(2)}, u32[]{:S(2)}) %collective-permute-start) | collective-permute-done | bytes 262176 | tf_op jit(solution)/shard_map/ppermute | solution.py:46
  20.9 0.0 copy-start.6
  21.0 0.0 all-to-all-done.refs_1_
  21.0 1.4 %select.1 = bf16[32,2,32,128]{3,2,1,0:T(8,128)(2,1)} custom-call(s32[34]{0:T(128)S(1)} %pad_add_fusion.refs_0_, bf16[32,32,128]{2,1,0:T(8,128)(2,1)S(1)} %all-to-all-done.refs_1_), custom_call_target="tpu_custom_call" | custom-call | tf_op jit(solution)/shard_map/select/pallas_call | solution.py:92
  22.4 0.0 copy-done.6
  22.4 4.5 %all-to-all-start.1 = ((bf16[32,2,32,128]{3,2,1,0:T(8,128)(2,1)}), bf16[32,2,32,128]{3,2,1,0:T(8,128)(2,1)S(1)}, u32[]{:S(2)}, u32[]{:S(2)}) async-start(bf16[32,2,32,128]{3,2,1,0:T(8,128)(2,1)} %select.1), calls=%async_computation.1 | async-start | bytes 1048576 | tf_op jit(solution)/shard_map/all_to_all | solution.py:36
  26.9 0.0 copy-start.4
  26.9 0.8 collective-permute-start.1
  27.7 4.5 %first.1.first_ref = f32[4,8,1024]{2,1,0:T(8,128)} custom-call(bf16[128,4096]{1,0:T(8,128)(2,1)} %q_ref.5, bf16[128,4096]{1,0:T(8,128)(2,1)} %do_ref.5, bf16[2,4,128,128]{3,2,1,0:T(8,128)(2,1)} %pack.1.own_ref, bf16[2,4,128,128]{3,2,1,0:T(8,128)(2,1)} %copy-done.6), custom_call_target="tpu_custom_call" | custom-call | flops 805306368 | bytes 4194304 | tf_op jit(solution)/shard_map/first/pallas_call | solution.py:413
  32.2 0.0 collective-permute-done.1.outer_any.outer_ref
  32.2 0.0 copy-start.8
  32.2 13.8 %all-to-all-done.1 = bf16[32,2,32,128]{3,2,1,0:T(8,128)(2,1)S(1)} async-done(((bf16[32,2,32,128]{3,2,1,0:T(8,128)(2,1)}), bf16[32,2,32,128]{3,2,1,0:T(8,128)(2,1)S(1)}, u32[]{:S(2)}, u32[]{:S(2)}) %all-to-all-start.1) | async-done | bytes 524320 | tf_op jit(solution)/shard_map/all_to_all | solution.py:36
  46.1 0.0 copy-start.3
  46.1 2.2 %collective-permute-start.2 = (bf16[2,16,2,32,128]{4,3,2,1,0:T(8,128)(2,1)S(1)}, bf16[2,16,2,32,128]{4,3,2,1,0:T(8,128)(2,1)S(1)}, u32[]{:S(2)}, u32[]{:S(2)}) collective-permute-start(bf16[2,16,2,32,128]{4,3,2,1,0:T(8,128)(2,1)S(1)} %bitcast.11), channel_id=1, source_target_pairs={{0,1},{1,0},{2,3},{3,2},{4,5},{5,4},{6,7},{7,6},{8,9},{9,8},{10,11... | collective-permute-start | bytes 1572872 | tf_op jit(solution)/shard_map/ppermute | solution.py:41
  48.3 1.5 %collective-permute-done.2.other_ref = bf16[2,16,2,32,128]{4,3,2,1,0:T(8,128)(2,1)S(1)} collective-permute-done((bf16[2,16,2,32,128]{4,3,2,1,0:T(8,128)(2,1)S(1)}, bf16[2,16,2,32,128]{4,3,2,1,0:T(8,128)(2,1)S(1)}, u32[]{:S(2)}, u32[]{:S(2)}) %collective-permute-start.2) | collective-permute-done | bytes 524320 | tf_op jit(solution)/shard_map/ppermute | solution.py:41
  49.8 0.0 copy-start.5
  49.8 0.0 copy-done.4
  49.8 0.0 copy-start.10
  49.8 1.0 copy-done.10
  50.8 7.9 %scores.1 = (f32[4,8,1024]{2,1,0:T(8,128)S(1)}, f32[2,4,128,128]{3,2,1,0:T(8,128)S(1)}, bf16[2,4,128,128]{3,2,1,0:T(8,128)(2,1)S(1)}, bf16[2,4,128,128]{3,2,1,0:T(8,128)(2,1)S(1)}) custom-call(s32[1]{0:T(128)} %bitcast.edge_ref, bf16[2,16,2,32,128]{4,3,2,1,0:T(8,128)(2,1)S(1)} %bitcast.12, bf16[2,16,2,32,128]{4,3,2,1,0:T(8,128)(2,1)S(1)} %collective-permute-done.2.other_ref, ...), custom_call_target="tpu_custom_call" | custom-call | flops 2415919104 | bytes 4194304 | tf_op jit(solution)/shard_map/scores/pallas_call | solution.py:423
  58.7 0.0 copy-done.8
  58.7 0.0 copy-done.3
  58.7 0.0 copy-done.5
  58.7 0.4 collective-permute-start.3
  59.2 1.2 %collective-permute-done.3 = bf16[2,4,128,128]{3,2,1,0:T(8,128)(2,1)S(1)} collective-permute-done((bf16[2,4,128,128]{3,2,1,0:T(8,128)(2,1)S(1)}, bf16[2,4,128,128]{3,2,1,0:T(8,128)(2,1)S(1)}, u32[]{:S(2)}, u32[]{:S(2)}) %collective-permute-start.3) | collective-permute-done | bytes 262176 | tf_op jit(solution)/shard_map/ppermute | solution.py:41
  60.4 0.9 join.1
  61.2 0.0 copy-start.7
  61.2 3.1 %all-to-all-start.2 = ((bf16[32,2,32,128]{3,2,1,0:T(8,128)(2,1)}), bf16[32,2,32,128]{3,2,1,0:T(8,128)(2,1)S(1)}, u32[]{:S(2)}, u32[]{:S(2)}) async-start(bf16[32,2,32,128]{3,2,1,0:T(8,128)(2,1)} %join.1), calls=%async_computation.2 | async-start | bytes 1048576 | tf_op jit(solution)/shard_map/all_to_all | solution.py:36
  64.3 0.0 copy-done.7
  64.3 4.4 %window.1 = (bf16[2,4,128,128]{3,2,1,0:T(8,128)(2,1)S(1)}, bf16[2,4,128,128]{3,2,1,0:T(8,128)(2,1)S(1)}) custom-call(s32[1]{0:T(128)} %bitcast.edge_ref, bf16[128,4096]{1,0:T(8,128)(2,1)} %q_ref.5, bf16[128,4096]{1,0:T(8,128)(2,1)} %do_ref.5, bf16[2,4,128,128]{3,2,1,0:T(8,128)(2,1)S(1)} %copy-done.7, bf16[2,4,128,128]{3,2,1,0:T(8,128)(2,1)} %copy-done.8, ...), custom_call_target="tpu_custom_call" | custom-call | flops 805306368 | bytes 4194304 | tf_op jit(solution)/shard_map/window/pallas_call | solution.py:442
  68.8 1.8 %collective-permute-start.4 = (bf16[2,4,128,128]{3,2,1,0:T(8,128)(2,1)S(1)}, bf16[2,4,128,128]{3,2,1,0:T(8,128)(2,1)S(1)}, u32[]{:S(2)}, u32[]{:S(2)}) collective-permute-start(bf16[2,4,128,128]{3,2,1,0:T(8,128)(2,1)S(1)} %get-tuple-element.33), channel_id=1, source_target_pairs={{0,4},{4,0},{8,12},{12,8},{16,20},{20,16},{24,28},{28,24},{1,5},{5... | collective-permute-start | bytes 786440 | tf_op jit(solution)/shard_map/ppermute | solution.py:46
  70.6 0.7 collective-permute-start.5
  71.3 13.3 %collective-permute-done.4.from_inner_ref = bf16[2,4,128,128]{3,2,1,0:T(8,128)(2,1)S(1)} collective-permute-done((bf16[2,4,128,128]{3,2,1,0:T(8,128)(2,1)S(1)}, bf16[2,4,128,128]{3,2,1,0:T(8,128)(2,1)S(1)}, u32[]{:S(2)}, u32[]{:S(2)}) %collective-permute-start.4) | collective-permute-done | bytes 262176 | tf_op jit(solution)/shard_map/ppermute | solution.py:46
  84.6 0.0 copy-start.11
  84.6 0.0 collective-permute-done.5.from_outer_ref
  84.6 0.0 copy-start.12
  84.6 0.0 all-to-all-done.2.refs_1_
  84.6 1.4 %combine.1 = bf16[32,32,128]{2,1,0:T(8,128)(2,1)} custom-call(s32[34]{0:T(128)S(1)} %pad_add_fusion.refs_0_, bf16[32,2,32,128]{3,2,1,0:T(8,128)(2,1)S(1)} %all-to-all-done.2.refs_1_), custom_call_target="tpu_custom_call" | custom-call | tf_op jit(solution)/shard_map/combine/pallas_call | solution.py:127
  86.0 0.0 copy-done.11
  86.0 0.0 copy-done.12
  86.0 0.0 copy-start.1
  86.0 0.0 copy-start.9
  86.0 5.7 %all-to-all-start.3 = ((bf16[32,32,128]{2,1,0:T(8,128)(2,1)}), bf16[32,32,128]{2,1,0:T(8,128)(2,1)S(1)}, u32[]{:S(2)}, u32[]{:S(2)}) async-start(bf16[32,32,128]{2,1,0:T(8,128)(2,1)} %combine.1), calls=%async_computation.3 | async-start | bytes 524288 | tf_op jit(solution)/shard_map/all_to_all | solution.py:36
  91.7 0.0 copy-done.1
  91.7 0.0 copy-done.9
  91.7 10.0 %outputs.1 = (bf16[128,4096]{1,0:T(8,128)(2,1)}, bf16[128,4096]{1,0:T(8,128)(2,1)}, f32[2,4,128,128]{3,2,1,0:T(8,128)}) custom-call(s32[1]{0:T(128)} %bitcast.edge_ref, bf16[128,4096]{1,0:T(8,128)(2,1)} %q_ref.5, bf16[128,4096]{1,0:T(8,128)(2,1)} %do_ref.5, bf16[2,4,128,128]{3,2,1,0:T(8,128)(2,1)S(1)} %copy-done.1, bf16[2,4,128,128]{3,2,1,0:T(8,128)(2,1)S(1)} %copy-done.7, ...), custom_call_target="tpu_custom_call" | custom-call | flops 2415919104 | bytes 4194304 | tf_op jit(solution)/shard_map/outputs/pallas_call | solution.py:451
  101.8 0.6 all-to-all-done.3
  102.4 0.0 copy-start.2
  102.4 1.0 copy-done.2
  103.4 0.7 finish.1
Async XLA Ops:
  2.3 7.3 %copy-start = (bf16[2,4,128,128]{3,2,1,0:T(8,128)(2,1)S(1)}, bf16[2,4,128,128]{3,2,1,0:T(8,128)(2,1)}, u32[]{:S(2)}) copy-start(bf16[2,4,128,128]{3,2,1,0:T(8,128)(2,1)} %pack.1.own_ref) | copy-start | bytes 786436
  2.3 18.6 %all-to-all-start = ((bf16[32,32,128]{2,1,0:T(8,128)(2,1)}), bf16[32,32,128]{2,1,0:T(8,128)(2,1)S(1)}, u32[]{:S(2)}, u32[]{:S(2)}) async-start(bf16[32,32,128]{2,1,0:T(8,128)(2,1)} %bitcast.9), calls=%async_computation | async-start | bytes 524288 | tf_op jit(solution)/shard_map/all_to_all | solution.py:36
  9.7 1.9 %copy-start.13 = (s32[2]{0:T(128)S(1)}, s32[2]{0:T(128)}, u32[]{:S(2)}) copy-start(s32[2]{0:T(128)} %param.11) | copy-start | bytes 28
  9.7 1.9 %copy-start.14 = (s32[32,1]{0,1:T(1,128)S(1)}, s32[32,1]{0,1:T(1,128)}, u32[]{:S(2)}) copy-start(s32[32,1]{0,1:T(1,128)} %param.10) | copy-start | bytes 388
  9.7 11.3 %collective-permute-start = (bf16[2,4,128,128]{3,2,1,0:T(8,128)(2,1)S(1)}, bf16[2,4,128,128]{3,2,1,0:T(8,128)(2,1)S(1)}, u32[]{:S(2)}, u32[]{:S(2)}) collective-permute-start(bf16[2,4,128,128]{3,2,1,0:T(8,128)(2,1)S(1)} %copy-done), channel_id=1, source_target_pairs={{0,4},{4,0},{8,12},{12,8},{16,20},{20,16},{24,28},{28,24},{1,5},{5... | collective-permute-start | bytes 786440 | tf_op jit(solution)/shard_map/ppermute | solution.py:46
  20.9 1.4 %copy-start.6 = (bf16[2,4,128,128]{3,2,1,0:T(8,128)(2,1)}, bf16[2,4,128,128]{3,2,1,0:T(8,128)(2,1)S(1)}, u32[]{:S(2)}) copy-start(bf16[2,4,128,128]{3,2,1,0:T(8,128)(2,1)S(1)} %collective-permute-done.inner_ref) | copy-start | bytes 786436
  22.4 23.7 %all-to-all-start.1 = ((bf16[32,2,32,128]{3,2,1,0:T(8,128)(2,1)}), bf16[32,2,32,128]{3,2,1,0:T(8,128)(2,1)S(1)}, u32[]{:S(2)}, u32[]{:S(2)}) async-start(bf16[32,2,32,128]{3,2,1,0:T(8,128)(2,1)} %select.1), calls=%async_computation.1 | async-start | bytes 1048576 | tf_op jit(solution)/shard_map/all_to_all | solution.py:36
  26.9 22.9 %copy-start.4 = (bf16[128,4096]{1,0:T(8,128)(2,1)S(1)}, bf16[128,4096]{1,0:T(8,128)(2,1)}, u32[]{:S(2)}) copy-start(bf16[128,4096]{1,0:T(8,128)(2,1)} %q_ref.5) | copy-start | bytes 3145732
  26.9 5.3 %collective-permute-start.1 = (bf16[2,4,128,128]{3,2,1,0:T(8,128)(2,1)S(1)}, bf16[2,4,128,128]{3,2,1,0:T(8,128)(2,1)S(1)}, u32[]{:S(2)}, u32[]{:S(2)}) collective-permute-start(bf16[2,4,128,128]{3,2,1,0:T(8,128)(2,1)S(1)} %copy-done), channel_id=1, source_target_pairs={{4,8},{8,4},{12,16},{16,12},{20,24},{24,20},{28,1},{1,28},{5,9},{9... | collective-permute-start | bytes 786440 | tf_op jit(solution)/shard_map/ppermute | solution.py:55
  32.2 26.5 %copy-start.8 = (bf16[2,4,128,128]{3,2,1,0:T(8,128)(2,1)}, bf16[2,4,128,128]{3,2,1,0:T(8,128)(2,1)S(1)}, u32[]{:S(2)}) copy-start(bf16[2,4,128,128]{3,2,1,0:T(8,128)(2,1)S(1)} %collective-permute-done.1.outer_any.outer_ref) | copy-start | bytes 786436
  46.1 12.7 %copy-start.3 = (bf16[32,2,32,128]{3,2,1,0:T(8,128)(2,1)}, bf16[32,2,32,128]{3,2,1,0:T(8,128)(2,1)S(1)}, u32[]{:S(2)}) copy-start(bf16[32,2,32,128]{3,2,1,0:T(8,128)(2,1)S(1)} %all-to-all-done.1) | copy-start | bytes 1572868
  46.1 3.7 %collective-permute-start.2 = (bf16[2,16,2,32,128]{4,3,2,1,0:T(8,128)(2,1)S(1)}, bf16[2,16,2,32,128]{4,3,2,1,0:T(8,128)(2,1)S(1)}, u32[]{:S(2)}, u32[]{:S(2)}) collective-permute-start(bf16[2,16,2,32,128]{4,3,2,1,0:T(8,128)(2,1)S(1)} %bitcast.11), channel_id=1, source_target_pairs={{0,1},{1,0},{2,3},{3,2},{4,5},{5,4},{6,7},{7,6},{8,9},{9,8},{10,11... | collective-permute-start | bytes 1572872 | tf_op jit(solution)/shard_map/ppermute | solution.py:41
  49.8 8.9 %copy-start.5 = (bf16[2,16,2,32,128]{4,3,2,1,0:T(8,128)(2,1)}, bf16[2,16,2,32,128]{4,3,2,1,0:T(8,128)(2,1)S(1)}, u32[]{:S(2)}) copy-start(bf16[2,16,2,32,128]{4,3,2,1,0:T(8,128)(2,1)S(1)} %collective-permute-done.2.other_ref) | copy-start | bytes 1572868
  49.8 1.0 copy-start.10
  58.7 1.6 %collective-permute-start.3 = (bf16[2,4,128,128]{3,2,1,0:T(8,128)(2,1)S(1)}, bf16[2,4,128,128]{3,2,1,0:T(8,128)(2,1)S(1)}, u32[]{:S(2)}, u32[]{:S(2)}) collective-permute-start(bf16[2,4,128,128]{3,2,1,0:T(8,128)(2,1)S(1)} %get-tuple-element.32), channel_id=1, source_target_pairs={{0,1},{1,0},{2,3},{3,2},{4,5},{5,4},{6,7},{7,6},{8,9},{9,8},{10,11... | collective-permute-start | bytes 786440 | tf_op jit(solution)/shard_map/ppermute | solution.py:41
  61.2 3.1 %copy-start.7 = (bf16[2,4,128,128]{3,2,1,0:T(8,128)(2,1)S(1)}, bf16[2,4,128,128]{3,2,1,0:T(8,128)(2,1)}, u32[]{:S(2)}) copy-start(bf16[2,4,128,128]{3,2,1,0:T(8,128)(2,1)} %copy-done.6) | copy-start | bytes 786436
  61.2 23.4 %all-to-all-start.2 = ((bf16[32,2,32,128]{3,2,1,0:T(8,128)(2,1)}), bf16[32,2,32,128]{3,2,1,0:T(8,128)(2,1)S(1)}, u32[]{:S(2)}, u32[]{:S(2)}) async-start(bf16[32,2,32,128]{3,2,1,0:T(8,128)(2,1)} %join.1), calls=%async_computation.2 | async-start | bytes 1048576 | tf_op jit(solution)/shard_map/all_to_all | solution.py:36
  68.8 15.8 %collective-permute-start.4 = (bf16[2,4,128,128]{3,2,1,0:T(8,128)(2,1)S(1)}, bf16[2,4,128,128]{3,2,1,0:T(8,128)(2,1)S(1)}, u32[]{:S(2)}, u32[]{:S(2)}) collective-permute-start(bf16[2,4,128,128]{3,2,1,0:T(8,128)(2,1)S(1)} %get-tuple-element.33), channel_id=1, source_target_pairs={{0,4},{4,0},{8,12},{12,8},{16,20},{20,16},{24,28},{28,24},{1,5},{5... | collective-permute-start | bytes 786440 | tf_op jit(solution)/shard_map/ppermute | solution.py:46
  70.6 14.0 %collective-permute-start.5 = (bf16[2,4,128,128]{3,2,1,0:T(8,128)(2,1)S(1)}, bf16[2,4,128,128]{3,2,1,0:T(8,128)(2,1)S(1)}, u32[]{:S(2)}, u32[]{:S(2)}) collective-permute-start(bf16[2,4,128,128]{3,2,1,0:T(8,128)(2,1)S(1)} %get-tuple-element.34), channel_id=1, source_target_pairs={{4,8},{8,4},{12,16},{16,12},{20,24},{24,20},{28,1},{1,28},{5,9},{9... | collective-permute-start | bytes 786440 | tf_op jit(solution)/shard_map/ppermute | solution.py:55
  84.6 1.5 %copy-start.11 = (bf16[2,4,128,128]{3,2,1,0:T(8,128)(2,1)}, bf16[2,4,128,128]{3,2,1,0:T(8,128)(2,1)S(1)}, u32[]{:S(2)}) copy-start(bf16[2,4,128,128]{3,2,1,0:T(8,128)(2,1)S(1)} %collective-permute-done.4.from_inner_ref) | copy-start | bytes 786436
  84.6 1.5 %copy-start.12 = (bf16[2,4,128,128]{3,2,1,0:T(8,128)(2,1)}, bf16[2,4,128,128]{3,2,1,0:T(8,128)(2,1)S(1)}, u32[]{:S(2)}) copy-start(bf16[2,4,128,128]{3,2,1,0:T(8,128)(2,1)S(1)} %collective-permute-done.5.from_outer_ref) | copy-start | bytes 786436
  86.0 5.7 %copy-start.1 = (bf16[2,4,128,128]{3,2,1,0:T(8,128)(2,1)S(1)}, bf16[2,4,128,128]{3,2,1,0:T(8,128)(2,1)}, u32[]{:S(2)}) copy-start(bf16[2,4,128,128]{3,2,1,0:T(8,128)(2,1)} %pack.1.own_ref) | copy-start | bytes 786436
  86.0 5.7 %copy-start.9 = (bf16[2,4,128,128]{3,2,1,0:T(8,128)(2,1)S(1)}, bf16[2,4,128,128]{3,2,1,0:T(8,128)(2,1)}, u32[]{:S(2)}) copy-start(bf16[2,4,128,128]{3,2,1,0:T(8,128)(2,1)} %copy-done.8) | copy-start | bytes 786436
  86.0 16.3 %all-to-all-start.3 = ((bf16[32,32,128]{2,1,0:T(8,128)(2,1)}), bf16[32,32,128]{2,1,0:T(8,128)(2,1)S(1)}, u32[]{:S(2)}, u32[]{:S(2)}) async-start(bf16[32,32,128]{2,1,0:T(8,128)(2,1)} %combine.1), calls=%async_computation.3 | async-start | bytes 524288 | tf_op jit(solution)/shard_map/all_to_all | solution.py:36
  102.4 1.0 %copy-start.2 = (f32[2,4,128,128]{3,2,1,0:T(8,128)S(1)}, f32[2,4,128,128]{3,2,1,0:T(8,128)}, u32[]{:S(2)}) copy-start(f32[2,4,128,128]{3,2,1,0:T(8,128)} %get-tuple-element.41.near_ref) | copy-start | bytes 1572868

commit v7 on v6

--- a/solution.py
+++ b/solution.py
@@ -52,6 +52,19 @@
     for i in range(1, heads * ctx - 1):
         j = i + 1 if i % 2 else i - 1
         pairs.append(tuple(b % heads * ctx + b // heads for b in (i, j)))
+    return lax.ppermute(value, ("heads", "ctx"), pairs)
+
+
+def fetch_outer(own, inner):
+    heads, ctx = lax.axis_size("heads"), lax.axis_size("ctx")
+    count = heads * ctx
+    pairs = []
+    for i in range(count):
+        step = 1 if i % 2 else -1
+        j = i - 2 * step if i // heads % MATES else i + step
+        if 0 <= j < count:
+            pairs.append(tuple(b % heads * ctx + b // heads for b in (i, j)))
+    value = jnp.where(lax.axis_index("ctx") % MATES == 0, own, inner)
     return lax.ppermute(value, ("heads", "ctx"), pairs)
 
 
@@ -407,11 +420,12 @@
     grid = (KVH,)
     packed = pack(keys_in, values_in)
     slices = all_to_all(packed.reshape(count, rows, HD))
-    inner, outer = swap_inner(packed), swap_outer(packed)
+    inner = swap_inner(packed)
     slices, inner = lax.optimization_barrier((slices, inner))
+    outer = fetch_outer(packed, inner)
     far = all_to_all(select(wanted, slices, heads))
     first = call(
-        first_kernel, "first", 1, 56, [token, token, block, block],
+        first_kernel, "first", 1, 53, [token, token, block, block],
         [(stat, stat_shape)], grid=grid,
     )(queries, cotangent, packed, inner)[0]
     far, outer, first = lax.optimization_barrier((far, outer, first))

time: 105 us -> 103 us (0.981)
  starting transfers between devices: 28.3 us -> 29.6 us
  waiting for transfers between devices: 39.8 us -> 38.7 us
    all_to_all x4, waiting for transfers between devices: 14.4 us -> 13.3 us  [all_to_all(): return lax.all_to_all(value, AXES, split_axis=0, concat_axis=0, tiled=True)]
    unnamed x30 -> x22, local copies, waits for them, and re-layouts: 2.12 us -> 1.09 us
where the time goes in v7:
time: 103 us
  waiting for transfers between devices  38.7 us (38%)
  Pallas kernels  32.3 us (31%)
  starting transfers between devices  29.6 us (29%)
  local copies, waits for them, and re-layouts  1.09 us (1%)
    ppermute x2, waiting for transfers between devices, swap_inner(): return lax.ppermute(value, 'heads', [(h, h ^ 1) for h in range(heads)])  22.7 us
    all_to_all x4, starting transfers between devices, all_to_all(): return lax.all_to_all(value, AXES, split_axis=0, concat_axis=0, tiled=True)  21.6 us
    all_to_all x4, waiting for transfers between devices, all_to_all(): return lax.all_to_all(value, AXES, split_axis=0, concat_axis=0, tiled=True)  13.3 us
    pallas_call x1, Pallas kernels, shards(): call(outputs_kernel, 'outputs', 3, 53, [smem, token, token] + [block] * 3...  10 us
    pallas_call x1, Pallas kernels, shards(): call(scores_kernel, 'scores', 3, 50, [smem, vmem, vmem, vmem] + [anywhere...  8.09 us
    pallas_call x1, Pallas kernels, shards(): call(window_kernel, 'window', 1, 53, [smem, token, token, block, block, s...  4.44 us
    ppermute x2, starting transfers between devices, swap_inner(): return lax.ppermute(value, 'heads', [(h, h ^ 1) for h in range(heads)])  3.66 us
    pallas_call x1, Pallas kernels, shards(): call(first_kernel, 'first', 1, 53, [token, token, block, block], [(stat,...  3.64 us
  transfers between devices with their start and end apart: 10, of which 6 were waited for; matrix products, arithmetic and copies ran while one was open for 0% of the time, Pallas kernels for 18%

profile of v7, /device:TPU:0, one launch (start us, length us, event | category | flops | bytes accessed | tf_op | source)
XLA Modules:
  0.0 102.6 jit_solution(8838015840991477811)
XLA Ops:
  0.6 1.7 %pack.1.own_ref = bf16[2,4,128,128]{3,2,1,0:T(8,128)(2,1)} custom-call(bf16[128,512]{1,0:T(8,128)(2,1)} %k_ref.1, bf16[128,512]{1,0:T(8,128)(2,1)} %v_ref.1), custom_call_target="tpu_custom_call" | custom-call | tf_op jit(solution)/shard_map/pack/pallas_call | solution.py:79
  2.3 0.0 copy-start
  2.3 7.3 %all-to-all-start = ((bf16[32,32,128]{2,1,0:T(8,128)(2,1)}), bf16[32,32,128]{2,1,0:T(8,128)(2,1)S(1)}, u32[]{:S(2)}, u32[]{:S(2)}) async-start(bf16[32,32,128]{2,1,0:T(8,128)(2,1)} %bitcast.8), calls=%async_computation | async-start | bytes 524288 | tf_op jit(solution)/shard_map/all_to_all | solution.py:36
  9.7 0.0 copy-done
  9.7 0.0 copy-start.9
  9.7 0.0 copy-start.10
  9.7 1.8 %collective-permute-start = (bf16[2,4,128,128]{3,2,1,0:T(8,128)(2,1)S(1)}, bf16[2,4,128,128]{3,2,1,0:T(8,128)(2,1)S(1)}, u32[]{:S(2)}, u32[]{:S(2)}) collective-permute-start(bf16[2,4,128,128]{3,2,1,0:T(8,128)(2,1)S(1)} %copy-done), channel_id=1, source_target_pairs={{0,4},{4,0},{8,12},{12,8},{16,20},{20,16},{24,28},{28,24},{1,5},{5... | collective-permute-start | bytes 786440 | tf_op jit(solution)/shard_map/ppermute | solution.py:46
  11.5 0.0 copy-done.9
  11.5 0.0 copy-done.10
  11.5 0.1 pad_add_fusion.refs_0_
  11.6 9.3 %collective-permute-done.inner_ref = bf16[2,4,128,128]{3,2,1,0:T(8,128)(2,1)S(1)} collective-permute-done((bf16[2,4,128,128]{3,2,1,0:T(8,128)(2,1)S(1)}, bf16[2,4,128,128]{3,2,1,0:T(8,128)(2,1)S(1)}, u32[]{:S(2)}, u32[]{:S(2)}) %collective-permute-start) | collective-permute-done | bytes 262176 | tf_op jit(solution)/shard_map/ppermute | solution.py:46
  20.9 0.0 all-to-all-done.refs_1_
  21.0 1.4 %select.3 = bf16[32,2,32,128]{3,2,1,0:T(8,128)(2,1)} custom-call(s32[34]{0:T(128)S(1)} %pad_add_fusion.refs_0_, bf16[32,32,128]{2,1,0:T(8,128)(2,1)S(1)} %all-to-all-done.refs_1_), custom_call_target="tpu_custom_call" | custom-call | tf_op jit(solution)/shard_map/select/pallas_call | solution.py:105
  22.4 4.5 %all-to-all-start.1 = ((bf16[32,2,32,128]{3,2,1,0:T(8,128)(2,1)}), bf16[32,2,32,128]{3,2,1,0:T(8,128)(2,1)S(1)}, u32[]{:S(2)}, u32[]{:S(2)}) async-start(bf16[32,2,32,128]{3,2,1,0:T(8,128)(2,1)} %select.3), calls=%async_computation.1 | async-start | bytes 1048576 | tf_op jit(solution)/shard_map/all_to_all | solution.py:36
  27.0 0.0 copy-start.3
  27.0 0.8 collective-permute-start.1
  27.8 3.6 %first.1.first_ref = f32[4,8,1024]{2,1,0:T(8,128)S(1)} custom-call(bf16[128,4096]{1,0:T(8,128)(2,1)} %q_ref.5, bf16[128,4096]{1,0:T(8,128)(2,1)} %do_ref.5, bf16[2,4,128,128]{3,2,1,0:T(8,128)(2,1)S(1)} %copy-done, bf16[2,4,128,128]{3,2,1,0:T(8,128)(2,1)S(1)} %collective-permute-done.inner_ref), custom_call_target="tpu_custom_call" | custom-call | flops 805306368 | bytes 4194304 | tf_op jit(solution)/shard_map/first/pallas_call | solution.py:427
  31.4 0.0 collective-permute-done.1.outer_any.outer_ref
  31.4 0.0 copy-start.5
  31.5 12.7 %all-to-all-done.1 = bf16[32,2,32,128]{3,2,1,0:T(8,128)(2,1)S(1)} async-done(((bf16[32,2,32,128]{3,2,1,0:T(8,128)(2,1)}), bf16[32,2,32,128]{3,2,1,0:T(8,128)(2,1)S(1)}, u32[]{:S(2)}, u32[]{:S(2)}) %all-to-all-start.1) | async-done | bytes 524320 | tf_op jit(solution)/shard_map/all_to_all | solution.py:36
  44.1 0.0 copy-start.2
  44.1 2.4 %collective-permute-start.2 = (bf16[2,16,2,32,128]{4,3,2,1,0:T(8,128)(2,1)S(1)}, bf16[2,16,2,32,128]{4,3,2,1,0:T(8,128)(2,1)S(1)}, u32[]{:S(2)}, u32[]{:S(2)}) collective-permute-start(bf16[2,16,2,32,128]{4,3,2,1,0:T(8,128)(2,1)S(1)} %bitcast.11), channel_id=1, source_target_pairs={{0,1},{1,0},{2,3},{3,2},{4,5},{5,4},{6,7},{7,6},{8,9},{9,8},{10,11... | collective-permute-start | bytes 1572872 | tf_op jit(solution)/shard_map/ppermute | solution.py:41
  46.5 1.5 %collective-permute-done.2.other_ref = bf16[2,16,2,32,128]{4,3,2,1,0:T(8,128)(2,1)S(1)} collective-permute-done((bf16[2,16,2,32,128]{4,3,2,1,0:T(8,128)(2,1)S(1)}, bf16[2,16,2,32,128]{4,3,2,1,0:T(8,128)(2,1)S(1)}, u32[]{:S(2)}, u32[]{:S(2)}) %collective-permute-start.2) | collective-permute-done | bytes 524320 | tf_op jit(solution)/shard_map/ppermute | solution.py:41
  48.1 0.0 copy-start.4
  48.1 0.0 copy-done.3
  48.1 8.1 %scores.1 = (f32[4,8,1024]{2,1,0:T(8,128)S(1)}, f32[2,4,128,128]{3,2,1,0:T(8,128)S(1)}, bf16[2,4,128,128]{3,2,1,0:T(8,128)(2,1)S(1)}, bf16[2,4,128,128]{3,2,1,0:T(8,128)(2,1)S(1)}) custom-call(s32[1]{0:T(128)} %bitcast.edge_ref, bf16[2,16,2,32,128]{4,3,2,1,0:T(8,128)(2,1)S(1)} %bitcast.12, bf16[2,16,2,32,128]{4,3,2,1,0:T(8,128)(2,1)S(1)} %collective-permute-done.2.other_ref, ...), custom_call_target="tpu_custom_call" | custom-call | flops 2415919104 | bytes 4194304 | tf_op jit(solution)/shard_map/scores/pallas_call | solution.py:437
  56.2 0.0 copy-done.5
  56.2 0.0 copy-done.2
  56.2 0.0 copy-done.4
  56.2 0.4 collective-permute-start.3
  56.6 1.2 %collective-permute-done.3 = bf16[2,4,128,128]{3,2,1,0:T(8,128)(2,1)S(1)} collective-permute-done((bf16[2,4,128,128]{3,2,1,0:T(8,128)(2,1)S(1)}, bf16[2,4,128,128]{3,2,1,0:T(8,128)(2,1)S(1)}, u32[]{:S(2)}, u32[]{:S(2)}) %collective-permute-start.3) | collective-permute-done | bytes 262176 | tf_op jit(solution)/shard_map/ppermute | solution.py:41
  57.8 0.9 join.1
  58.6 4.2 %all-to-all-start.2 = ((bf16[32,2,32,128]{3,2,1,0:T(8,128)(2,1)}), bf16[32,2,32,128]{3,2,1,0:T(8,128)(2,1)S(1)}, u32[]{:S(2)}, u32[]{:S(2)}) async-start(bf16[32,2,32,128]{3,2,1,0:T(8,128)(2,1)} %join.1), calls=%async_computation.2 | async-start | bytes 1048576 | tf_op jit(solution)/shard_map/all_to_all | solution.py:36
  62.8 4.4 %window.1 = (bf16[2,4,128,128]{3,2,1,0:T(8,128)(2,1)S(1)}, bf16[2,4,128,128]{3,2,1,0:T(8,128)(2,1)S(1)}) custom-call(s32[1]{0:T(128)} %bitcast.edge_ref, bf16[128,4096]{1,0:T(8,128)(2,1)} %q_ref.5, bf16[128,4096]{1,0:T(8,128)(2,1)} %do_ref.5, bf16[2,4,128,128]{3,2,1,0:T(8,128)(2,1)S(1)} %collective-permute-done.inner_ref, ...), custom_call_target="tpu_custom_call" | custom-call | flops 805306368 | bytes 4194304 | tf_op jit(solution)/shard_map/window/pallas_call | solution.py:456
  67.3 1.8 %collective-permute-start.4 = (bf16[2,4,128,128]{3,2,1,0:T(8,128)(2,1)S(1)}, bf16[2,4,128,128]{3,2,1,0:T(8,128)(2,1)S(1)}, u32[]{:S(2)}, u32[]{:S(2)}) collective-permute-start(bf16[2,4,128,128]{3,2,1,0:T(8,128)(2,1)S(1)} %get-tuple-element.33), channel_id=1, source_target_pairs={{0,4},{4,0},{8,12},{12,8},{16,20},{20,16},{24,28},{28,24},{1,5},{5... | collective-permute-start | bytes 786440 | tf_op jit(solution)/shard_map/ppermute | solution.py:46
  69.1 0.7 collective-permute-start.5
  69.8 13.3 %collective-permute-done.4.from_inner_ref = bf16[2,4,128,128]{3,2,1,0:T(8,128)(2,1)S(1)} collective-permute-done((bf16[2,4,128,128]{3,2,1,0:T(8,128)(2,1)S(1)}, bf16[2,4,128,128]{3,2,1,0:T(8,128)(2,1)S(1)}, u32[]{:S(2)}, u32[]{:S(2)}) %collective-permute-start.4) | collective-permute-done | bytes 262176 | tf_op jit(solution)/shard_map/ppermute | solution.py:46
  83.1 0.0 copy-start.7
  83.1 0.0 collective-permute-done.5.from_outer_ref
  83.1 0.0 copy-start.8
  83.1 0.0 all-to-all-done.2.refs_1_
  83.1 1.4 %combine.1 = bf16[32,32,128]{2,1,0:T(8,128)(2,1)} custom-call(s32[34]{0:T(128)S(1)} %pad_add_fusion.refs_0_, bf16[32,2,32,128]{3,2,1,0:T(8,128)(2,1)S(1)} %all-to-all-done.2.refs_1_), custom_call_target="tpu_custom_call" | custom-call | tf_op jit(solution)/shard_map/combine/pallas_call | solution.py:140
  84.5 0.0 copy-done.7
  84.5 0.0 copy-done.8
  84.5 0.0 copy-start.6
  84.5 5.6 %all-to-all-start.3 = ((bf16[32,32,128]{2,1,0:T(8,128)(2,1)}), bf16[32,32,128]{2,1,0:T(8,128)(2,1)S(1)}, u32[]{:S(2)}, u32[]{:S(2)}) async-start(bf16[32,32,128]{2,1,0:T(8,128)(2,1)} %combine.1), calls=%async_computation.3 | async-start | bytes 524288 | tf_op jit(solution)/shard_map/all_to_all | solution.py:36
  90.2 0.0 copy-done.6
  90.2 10.0 %outputs.1 = (bf16[128,4096]{1,0:T(8,128)(2,1)}, bf16[128,4096]{1,0:T(8,128)(2,1)}, f32[2,4,128,128]{3,2,1,0:T(8,128)}) custom-call(s32[1]{0:T(128)} %bitcast.edge_ref, bf16[128,4096]{1,0:T(8,128)(2,1)} %q_ref.5, bf16[128,4096]{1,0:T(8,128)(2,1)} %do_ref.5, bf16[2,4,128,128]{3,2,1,0:T(8,128)(2,1)S(1)} %copy-done, ...), custom_call_target="tpu_custom_call" | custom-call | flops 2415919104 | bytes 4194304 | tf_op jit(solution)/shard_map/outputs/pallas_call | solution.py:465
  100.2 0.6 all-to-all-done.3
  100.8 0.0 copy-start.1
  100.8 1.0 %copy-done.1 = f32[2,4,128,128]{3,2,1,0:T(8,128)S(1)} copy-done((f32[2,4,128,128]{3,2,1,0:T(8,128)S(1)}, f32[2,4,128,128]{3,2,1,0:T(8,128)}, u32[]{:S(2)}) %copy-start.1) | copy-done | bytes 524312
  101.9 0.7 finish.1
  (1 shorter events, 0.0 us)
Async XLA Ops:
  2.3 7.3 %copy-start = (bf16[2,4,128,128]{3,2,1,0:T(8,128)(2,1)S(1)}, bf16[2,4,128,128]{3,2,1,0:T(8,128)(2,1)}, u32[]{:S(2)}) copy-start(bf16[2,4,128,128]{3,2,1,0:T(8,128)(2,1)} %pack.1.own_ref) | copy-start | bytes 786436
  2.3 18.6 %all-to-all-start = ((bf16[32,32,128]{2,1,0:T(8,128)(2,1)}), bf16[32,32,128]{2,1,0:T(8,128)(2,1)S(1)}, u32[]{:S(2)}, u32[]{:S(2)}) async-start(bf16[32,32,128]{2,1,0:T(8,128)(2,1)} %bitcast.8), calls=%async_computation | async-start | bytes 524288 | tf_op jit(solution)/shard_map/all_to_all | solution.py:36
  9.7 1.9 %copy-start.9 = (s32[2]{0:T(128)S(1)}, s32[2]{0:T(128)}, u32[]{:S(2)}) copy-start(s32[2]{0:T(128)} %param.11) | copy-start | bytes 28
  9.7 1.9 %copy-start.10 = (s32[32,1]{0,1:T(1,128)S(1)}, s32[32,1]{0,1:T(1,128)}, u32[]{:S(2)}) copy-start(s32[32,1]{0,1:T(1,128)} %param.10) | copy-start | bytes 388
  9.7 11.3 %collective-permute-start = (bf16[2,4,128,128]{3,2,1,0:T(8,128)(2,1)S(1)}, bf16[2,4,128,128]{3,2,1,0:T(8,128)(2,1)S(1)}, u32[]{:S(2)}, u32[]{:S(2)}) collective-permute-start(bf16[2,4,128,128]{3,2,1,0:T(8,128)(2,1)S(1)} %copy-done), channel_id=1, source_target_pairs={{0,4},{4,0},{8,12},{12,8},{16,20},{20,16},{24,28},{28,24},{1,5},{5... | collective-permute-start | bytes 786440 | tf_op jit(solution)/shard_map/ppermute | solution.py:46
  22.4 21.8 %all-to-all-start.1 = ((bf16[32,2,32,128]{3,2,1,0:T(8,128)(2,1)}), bf16[32,2,32,128]{3,2,1,0:T(8,128)(2,1)S(1)}, u32[]{:S(2)}, u32[]{:S(2)}) async-start(bf16[32,2,32,128]{3,2,1,0:T(8,128)(2,1)} %select.3), calls=%async_computation.1 | async-start | bytes 1048576 | tf_op jit(solution)/shard_map/all_to_all | solution.py:36
  27.0 21.1 %copy-start.3 = (bf16[128,4096]{1,0:T(8,128)(2,1)S(1)}, bf16[128,4096]{1,0:T(8,128)(2,1)}, u32[]{:S(2)}) copy-start(bf16[128,4096]{1,0:T(8,128)(2,1)} %q_ref.5) | copy-start | bytes 3145732
  27.0 4.5 %collective-permute-start.1 = (bf16[2,4,128,128]{3,2,1,0:T(8,128)(2,1)S(1)}, bf16[2,4,128,128]{3,2,1,0:T(8,128)(2,1)S(1)}, u32[]{:S(2)}, u32[]{:S(2)}) collective-permute-start(bf16[2,4,128,128]{3,2,1,0:T(8,128)(2,1)S(1)} %broadcast_select_fusion), channel_id=1, source_target_pairs={{4,8},{8,4},{12,16},{16,12},{20,24},{24,20},{28,1},{1,9},{5,28},{9... | collective-permute-start | bytes 786440 | tf_op jit(solution)/shard_map/ppermute | solution.py:68
  31.4 24.7 %copy-start.5 = (bf16[2,4,128,128]{3,2,1,0:T(8,128)(2,1)}, bf16[2,4,128,128]{3,2,1,0:T(8,128)(2,1)S(1)}, u32[]{:S(2)}) copy-start(bf16[2,4,128,128]{3,2,1,0:T(8,128)(2,1)S(1)} %collective-permute-done.1.outer_any.outer_ref) | copy-start | bytes 786436
  44.1 12.0 %copy-start.2 = (bf16[32,2,32,128]{3,2,1,0:T(8,128)(2,1)}, bf16[32,2,32,128]{3,2,1,0:T(8,128)(2,1)S(1)}, u32[]{:S(2)}) copy-start(bf16[32,2,32,128]{3,2,1,0:T(8,128)(2,1)S(1)} %all-to-all-done.1) | copy-start | bytes 1572868
  44.1 3.9 %collective-permute-start.2 = (bf16[2,16,2,32,128]{4,3,2,1,0:T(8,128)(2,1)S(1)}, bf16[2,16,2,32,128]{4,3,2,1,0:T(8,128)(2,1)S(1)}, u32[]{:S(2)}, u32[]{:S(2)}) collective-permute-start(bf16[2,16,2,32,128]{4,3,2,1,0:T(8,128)(2,1)S(1)} %bitcast.11), channel_id=1, source_target_pairs={{0,1},{1,0},{2,3},{3,2},{4,5},{5,4},{6,7},{7,6},{8,9},{9,8},{10,11... | collective-permute-start | bytes 1572872 | tf_op jit(solution)/shard_map/ppermute | solution.py:41
  48.1 8.1 %copy-start.4 = (bf16[2,16,2,32,128]{4,3,2,1,0:T(8,128)(2,1)}, bf16[2,16,2,32,128]{4,3,2,1,0:T(8,128)(2,1)S(1)}, u32[]{:S(2)}) copy-start(bf16[2,16,2,32,128]{4,3,2,1,0:T(8,128)(2,1)S(1)} %collective-permute-done.2.other_ref) | copy-start | bytes 1572868
  56.2 1.6 %collective-permute-start.3 = (bf16[2,4,128,128]{3,2,1,0:T(8,128)(2,1)S(1)}, bf16[2,4,128,128]{3,2,1,0:T(8,128)(2,1)S(1)}, u32[]{:S(2)}, u32[]{:S(2)}) collective-permute-start(bf16[2,4,128,128]{3,2,1,0:T(8,128)(2,1)S(1)} %get-tuple-element.32), channel_id=1, source_target_pairs={{0,1},{1,0},{2,3},{3,2},{4,5},{5,4},{6,7},{7,6},{8,9},{9,8},{10,11... | collective-permute-start | bytes 786440 | tf_op jit(solution)/shard_map/ppermute | solution.py:41
  58.6 24.4 %all-to-all-start.2 = ((bf16[32,2,32,128]{3,2,1,0:T(8,128)(2,1)}), bf16[32,2,32,128]{3,2,1,0:T(8,128)(2,1)S(1)}, u32[]{:S(2)}, u32[]{:S(2)}) async-start(bf16[32,2,32,128]{3,2,1,0:T(8,128)(2,1)} %join.1), calls=%async_computation.2 | async-start | bytes 1048576 | tf_op jit(solution)/shard_map/all_to_all | solution.py:36
  67.3 15.8 %collective-permute-start.4 = (bf16[2,4,128,128]{3,2,1,0:T(8,128)(2,1)S(1)}, bf16[2,4,128,128]{3,2,1,0:T(8,128)(2,1)S(1)}, u32[]{:S(2)}, u32[]{:S(2)}) collective-permute-start(bf16[2,4,128,128]{3,2,1,0:T(8,128)(2,1)S(1)} %get-tuple-element.33), channel_id=1, source_target_pairs={{0,4},{4,0},{8,12},{12,8},{16,20},{20,16},{24,28},{28,24},{1,5},{5... | collective-permute-start | bytes 786440 | tf_op jit(solution)/shard_map/ppermute | solution.py:46
  69.1 14.0 %collective-permute-start.5 = (bf16[2,4,128,128]{3,2,1,0:T(8,128)(2,1)S(1)}, bf16[2,4,128,128]{3,2,1,0:T(8,128)(2,1)S(1)}, u32[]{:S(2)}, u32[]{:S(2)}) collective-permute-start(bf16[2,4,128,128]{3,2,1,0:T(8,128)(2,1)S(1)} %get-tuple-element.34), channel_id=1, source_target_pairs={{4,8},{8,4},{12,16},{16,12},{20,24},{24,20},{28,1},{1,28},{5,9},{9... | collective-permute-start | bytes 786440 | tf_op jit(solution)/shard_map/ppermute | solution.py:55
  83.1 1.4 %copy-start.7 = (bf16[2,4,128,128]{3,2,1,0:T(8,128)(2,1)}, bf16[2,4,128,128]{3,2,1,0:T(8,128)(2,1)S(1)}, u32[]{:S(2)}) copy-start(bf16[2,4,128,128]{3,2,1,0:T(8,128)(2,1)S(1)} %collective-permute-done.4.from_inner_ref) | copy-start | bytes 786436
  83.1 1.4 %copy-start.8 = (bf16[2,4,128,128]{3,2,1,0:T(8,128)(2,1)}, bf16[2,4,128,128]{3,2,1,0:T(8,128)(2,1)S(1)}, u32[]{:S(2)}) copy-start(bf16[2,4,128,128]{3,2,1,0:T(8,128)(2,1)S(1)} %collective-permute-done.5.from_outer_ref) | copy-start | bytes 786436
  84.5 5.7 %copy-start.6 = (bf16[2,4,128,128]{3,2,1,0:T(8,128)(2,1)S(1)}, bf16[2,4,128,128]{3,2,1,0:T(8,128)(2,1)}, u32[]{:S(2)}) copy-start(bf16[2,4,128,128]{3,2,1,0:T(8,128)(2,1)} %copy-done.5) | copy-start | bytes 786436
  84.5 16.3 %all-to-all-start.3 = ((bf16[32,32,128]{2,1,0:T(8,128)(2,1)}), bf16[32,32,128]{2,1,0:T(8,128)(2,1)S(1)}, u32[]{:S(2)}, u32[]{:S(2)}) async-start(bf16[32,32,128]{2,1,0:T(8,128)(2,1)} %combine.1), calls=%async_computation.3 | async-start | bytes 524288 | tf_op jit(solution)/shard_map/all_to_all | solution.py:36
  100.8 1.0 %copy-start.1 = (f32[2,4,128,128]{3,2,1,0:T(8,128)S(1)}, f32[2,4,128,128]{3,2,1,0:T(8,128)}, u32[]{:S(2)}) copy-start(f32[2,4,128,128]{3,2,1,0:T(8,128)} %get-tuple-element.41.near_ref) | copy-start | bytes 1572868

commit v8 on v7

--- a/solution.py
+++ b/solution.py
@@ -466,7 +466,7 @@
         outputs_kernel,
         "outputs",
         3,
-        53,
+        52,
         [smem, token, token] + [block] * 3 + [far_spec] * 2 + [stat, block, block],
         [(token, token_shape)] * 2 + [(block, wide)],
         low_pair(SLOTS),

time: 103 us -> 102 us (level)
  local copies, waits for them, and re-layouts: 1.09 us -> 0.04 us
    unnamed x22 -> x16, local copies, waits for them, and re-layouts: 1.09 us -> 0.04 us
where the time goes in v8:
time: 102 us
  waiting for transfers between devices  38.7 us (38%)
  Pallas kernels  32.2 us (32%)
  starting transfers between devices  29.6 us (29%)
    ppermute x2, waiting for transfers between devices, swap_inner(): return lax.ppermute(value, 'heads', [(h, h ^ 1) for h in range(heads)])  22.7 us
    all_to_all x4, starting transfers between devices, all_to_all(): return lax.all_to_all(value, AXES, split_axis=0, concat_axis=0, tiled=True)  21.6 us
    all_to_all x4, waiting for transfers between devices, all_to_all(): return lax.all_to_all(value, AXES, split_axis=0, concat_axis=0, tiled=True)  13.4 us
    pallas_call x1, Pallas kernels, shards(): call(outputs_kernel, 'outputs', 3, 52, [smem, token, token] + [block] * 3...  9.97 us
    pallas_call x1, Pallas kernels, shards(): call(scores_kernel, 'scores', 3, 50, [smem, vmem, vmem, vmem] + [anywhere...  8.04 us
    pallas_call x1, Pallas kernels, shards(): call(window_kernel, 'window', 1, 53, [smem, token, token, block, block, s...  4.44 us
    ppermute x2, starting transfers between devices, swap_inner(): return lax.ppermute(value, 'heads', [(h, h ^ 1) for h in range(heads)])  3.66 us
    pallas_call x1, Pallas kernels, shards(): call(first_kernel, 'first', 1, 53, [token, token, block, block], [(stat,...  3.64 us
  transfers between devices with their start and end apart: 10, of which 6 were waited for; matrix products, arithmetic and copies ran while one was open for 0% of the time, Pallas kernels for 18%

profile of v8, /device:TPU:0, one launch (start us, length us, event | category | flops | bytes accessed | tf_op | source)
XLA Modules:
  0.0 101.5 jit_solution(16414924134761102826)
XLA Ops:
  0.6 1.7 %pack.1.own_ref = bf16[2,4,128,128]{3,2,1,0:T(8,128)(2,1)} custom-call(bf16[128,512]{1,0:T(8,128)(2,1)} %k_ref.1, bf16[128,512]{1,0:T(8,128)(2,1)} %v_ref.1), custom_call_target="tpu_custom_call" | custom-call | tf_op jit(solution)/shard_map/pack/pallas_call | solution.py:79
  2.3 0.0 copy-start
  2.3 7.3 %all-to-all-start = ((bf16[32,32,128]{2,1,0:T(8,128)(2,1)}), bf16[32,32,128]{2,1,0:T(8,128)(2,1)S(1)}, u32[]{:S(2)}, u32[]{:S(2)}) async-start(bf16[32,32,128]{2,1,0:T(8,128)(2,1)} %bitcast.8), calls=%async_computation | async-start | bytes 524288 | tf_op jit(solution)/shard_map/all_to_all | solution.py:36
  9.7 0.0 copy-done
  9.7 0.0 copy-start.6
  9.7 0.0 copy-start.7
  9.7 1.8 %collective-permute-start = (bf16[2,4,128,128]{3,2,1,0:T(8,128)(2,1)S(1)}, bf16[2,4,128,128]{3,2,1,0:T(8,128)(2,1)S(1)}, u32[]{:S(2)}, u32[]{:S(2)}) collective-permute-start(bf16[2,4,128,128]{3,2,1,0:T(8,128)(2,1)S(1)} %copy-done), channel_id=1, source_target_pairs={{0,4},{4,0},{8,12},{12,8},{16,20},{20,16},{24,28},{28,24},{1,5},{5... | collective-permute-start | bytes 786440 | tf_op jit(solution)/shard_map/ppermute | solution.py:46
  11.5 0.0 copy-done.6
  11.5 0.0 copy-done.7
  11.5 0.1 pad_add_fusion.refs_0_
  11.6 9.3 %collective-permute-done.inner_ref = bf16[2,4,128,128]{3,2,1,0:T(8,128)(2,1)S(1)} collective-permute-done((bf16[2,4,128,128]{3,2,1,0:T(8,128)(2,1)S(1)}, bf16[2,4,128,128]{3,2,1,0:T(8,128)(2,1)S(1)}, u32[]{:S(2)}, u32[]{:S(2)}) %collective-permute-start) | collective-permute-done | bytes 262176 | tf_op jit(solution)/shard_map/ppermute | solution.py:46
  20.9 0.0 all-to-all-done.refs_1_
  21.0 1.4 %select.3 = bf16[32,2,32,128]{3,2,1,0:T(8,128)(2,1)} custom-call(s32[34]{0:T(128)S(1)} %pad_add_fusion.refs_0_, bf16[32,32,128]{2,1,0:T(8,128)(2,1)S(1)} %all-to-all-done.refs_1_), custom_call_target="tpu_custom_call" | custom-call | tf_op jit(solution)/shard_map/select/pallas_call | solution.py:105
  22.4 4.5 %all-to-all-start.1 = ((bf16[32,2,32,128]{3,2,1,0:T(8,128)(2,1)}), bf16[32,2,32,128]{3,2,1,0:T(8,128)(2,1)S(1)}, u32[]{:S(2)}, u32[]{:S(2)}) async-start(bf16[32,2,32,128]{3,2,1,0:T(8,128)(2,1)} %select.3), calls=%async_computation.1 | async-start | bytes 1048576 | tf_op jit(solution)/shard_map/all_to_all | solution.py:36
  27.0 0.0 copy-start.2
  27.0 0.8 collective-permute-start.1
  27.8 3.6 %first.1.first_ref = f32[4,8,1024]{2,1,0:T(8,128)S(1)} custom-call(bf16[128,4096]{1,0:T(8,128)(2,1)} %q_ref.5, bf16[128,4096]{1,0:T(8,128)(2,1)} %do_ref.5, bf16[2,4,128,128]{3,2,1,0:T(8,128)(2,1)S(1)} %copy-done, bf16[2,4,128,128]{3,2,1,0:T(8,128)(2,1)S(1)} %collective-permute-done.inner_ref), custom_call_target="tpu_custom_call" | custom-call | flops 805306368 | bytes 4194304 | tf_op jit(solution)/shard_map/first/pallas_call | solution.py:427
  31.4 0.0 collective-permute-done.1.outer_any.outer_ref
  31.4 0.0 copy-start.4
  31.5 12.7 %all-to-all-done.1 = bf16[32,2,32,128]{3,2,1,0:T(8,128)(2,1)S(1)} async-done(((bf16[32,2,32,128]{3,2,1,0:T(8,128)(2,1)}), bf16[32,2,32,128]{3,2,1,0:T(8,128)(2,1)S(1)}, u32[]{:S(2)}, u32[]{:S(2)}) %all-to-all-start.1) | async-done | bytes 524320 | tf_op jit(solution)/shard_map/all_to_all | solution.py:36
  44.1 0.0 copy-start.1
  44.1 2.4 %collective-permute-start.2 = (bf16[2,16,2,32,128]{4,3,2,1,0:T(8,128)(2,1)S(1)}, bf16[2,16,2,32,128]{4,3,2,1,0:T(8,128)(2,1)S(1)}, u32[]{:S(2)}, u32[]{:S(2)}) collective-permute-start(bf16[2,16,2,32,128]{4,3,2,1,0:T(8,128)(2,1)S(1)} %bitcast.11), channel_id=1, source_target_pairs={{0,1},{1,0},{2,3},{3,2},{4,5},{5,4},{6,7},{7,6},{8,9},{9,8},{10,11... | collective-permute-start | bytes 1572872 | tf_op jit(solution)/shard_map/ppermute | solution.py:41
  46.5 1.5 %collective-permute-done.2.other_ref = bf16[2,16,2,32,128]{4,3,2,1,0:T(8,128)(2,1)S(1)} collective-permute-done((bf16[2,16,2,32,128]{4,3,2,1,0:T(8,128)(2,1)S(1)}, bf16[2,16,2,32,128]{4,3,2,1,0:T(8,128)(2,1)S(1)}, u32[]{:S(2)}, u32[]{:S(2)}) %collective-permute-start.2) | collective-permute-done | bytes 524320 | tf_op jit(solution)/shard_map/ppermute | solution.py:41
  48.1 0.0 copy-start.3
  48.1 0.0 copy-done.2
  48.1 8.0 %scores.1 = (f32[4,8,1024]{2,1,0:T(8,128)S(1)}, f32[2,4,128,128]{3,2,1,0:T(8,128)S(1)}, bf16[2,4,128,128]{3,2,1,0:T(8,128)(2,1)S(1)}, bf16[2,4,128,128]{3,2,1,0:T(8,128)(2,1)S(1)}) custom-call(s32[1]{0:T(128)} %bitcast.edge_ref, bf16[2,16,2,32,128]{4,3,2,1,0:T(8,128)(2,1)S(1)} %bitcast.12, bf16[2,16,2,32,128]{4,3,2,1,0:T(8,128)(2,1)S(1)} %collective-permute-done.2.other_ref, ...), custom_call_target="tpu_custom_call" | custom-call | flops 2415919104 | bytes 4194304 | tf_op jit(solution)/shard_map/scores/pallas_call | solution.py:437
  56.1 0.0 copy-done.4
  56.1 0.0 copy-done.1
  56.1 0.0 copy-done.3
  56.1 0.4 collective-permute-start.3
  56.6 1.2 %collective-permute-done.3 = bf16[2,4,128,128]{3,2,1,0:T(8,128)(2,1)S(1)} collective-permute-done((bf16[2,4,128,128]{3,2,1,0:T(8,128)(2,1)S(1)}, bf16[2,4,128,128]{3,2,1,0:T(8,128)(2,1)S(1)}, u32[]{:S(2)}, u32[]{:S(2)}) %collective-permute-start.3) | collective-permute-done | bytes 262176 | tf_op jit(solution)/shard_map/ppermute | solution.py:41
  57.7 0.9 join.1
  58.6 4.2 %all-to-all-start.2 = ((bf16[32,2,32,128]{3,2,1,0:T(8,128)(2,1)}), bf16[32,2,32,128]{3,2,1,0:T(8,128)(2,1)S(1)}, u32[]{:S(2)}, u32[]{:S(2)}) async-start(bf16[32,2,32,128]{3,2,1,0:T(8,128)(2,1)} %join.1), calls=%async_computation.2 | async-start | bytes 1048576 | tf_op jit(solution)/shard_map/all_to_all | solution.py:36
  62.8 4.4 %window.1 = (bf16[2,4,128,128]{3,2,1,0:T(8,128)(2,1)S(1)}, bf16[2,4,128,128]{3,2,1,0:T(8,128)(2,1)S(1)}) custom-call(s32[1]{0:T(128)} %bitcast.edge_ref, bf16[128,4096]{1,0:T(8,128)(2,1)} %q_ref.5, bf16[128,4096]{1,0:T(8,128)(2,1)} %do_ref.5, bf16[2,4,128,128]{3,2,1,0:T(8,128)(2,1)S(1)} %collective-permute-done.inner_ref, ...), custom_call_target="tpu_custom_call" | custom-call | flops 805306368 | bytes 4194304 | tf_op jit(solution)/shard_map/window/pallas_call | solution.py:456
  67.2 1.8 %collective-permute-start.4 = (bf16[2,4,128,128]{3,2,1,0:T(8,128)(2,1)S(1)}, bf16[2,4,128,128]{3,2,1,0:T(8,128)(2,1)S(1)}, u32[]{:S(2)}, u32[]{:S(2)}) collective-permute-start(bf16[2,4,128,128]{3,2,1,0:T(8,128)(2,1)S(1)} %get-tuple-element.33), channel_id=1, source_target_pairs={{0,4},{4,0},{8,12},{12,8},{16,20},{20,16},{24,28},{28,24},{1,5},{5... | collective-permute-start | bytes 786440 | tf_op jit(solution)/shard_map/ppermute | solution.py:46
  69.1 0.7 collective-permute-start.5
  69.7 13.3 %collective-permute-done.4.from_inner_ref = bf16[2,4,128,128]{3,2,1,0:T(8,128)(2,1)S(1)} collective-permute-done((bf16[2,4,128,128]{3,2,1,0:T(8,128)(2,1)S(1)}, bf16[2,4,128,128]{3,2,1,0:T(8,128)(2,1)S(1)}, u32[]{:S(2)}, u32[]{:S(2)}) %collective-permute-start.4) | collective-permute-done | bytes 262176 | tf_op jit(solution)/shard_map/ppermute | solution.py:46
  83.0 0.0 collective-permute-done.5.from_outer_ref
  83.1 0.0 all-to-all-done.2.refs_1_
  83.1 1.4 %combine.1 = bf16[32,32,128]{2,1,0:T(8,128)(2,1)} custom-call(s32[34]{0:T(128)S(1)} %pad_add_fusion.refs_0_, bf16[32,2,32,128]{3,2,1,0:T(8,128)(2,1)S(1)} %all-to-all-done.2.refs_1_), custom_call_target="tpu_custom_call" | custom-call | tf_op jit(solution)/shard_map/combine/pallas_call | solution.py:140
  84.5 0.0 copy-start.5
  84.5 5.6 %all-to-all-start.3 = ((bf16[32,32,128]{2,1,0:T(8,128)(2,1)}), bf16[32,32,128]{2,1,0:T(8,128)(2,1)S(1)}, u32[]{:S(2)}, u32[]{:S(2)}) async-start(bf16[32,32,128]{2,1,0:T(8,128)(2,1)} %combine.1), calls=%async_computation.3 | async-start | bytes 524288 | tf_op jit(solution)/shard_map/all_to_all | solution.py:36
  90.1 0.0 copy-done.5
  90.1 10.0 %outputs.1 = (bf16[128,4096]{1,0:T(8,128)(2,1)}, bf16[128,4096]{1,0:T(8,128)(2,1)}, f32[2,4,128,128]{3,2,1,0:T(8,128)S(1)}) custom-call(s32[1]{0:T(128)} %bitcast.edge_ref, bf16[128,4096]{1,0:T(8,128)(2,1)} %q_ref.5, bf16[128,4096]{1,0:T(8,128)(2,1)} %do_ref.5, bf16[2,4,128,128]{3,2,1,0:T(8,128)(2,1)S(1)} %copy-done, ...), custom_call_target="tpu_custom_call" | custom-call | flops 2415919104 | bytes 4194304 | tf_op jit(solution)/shard_map/outputs/pallas_call | solution.py:465
  100.1 0.7 all-to-all-done.3
  100.8 0.7 finish.1
  (1 shorter events, 0.0 us)
Async XLA Ops:
  2.3 7.3 %copy-start = (bf16[2,4,128,128]{3,2,1,0:T(8,128)(2,1)S(1)}, bf16[2,4,128,128]{3,2,1,0:T(8,128)(2,1)}, u32[]{:S(2)}) copy-start(bf16[2,4,128,128]{3,2,1,0:T(8,128)(2,1)} %pack.1.own_ref) | copy-start | bytes 786436
  2.3 18.6 %all-to-all-start = ((bf16[32,32,128]{2,1,0:T(8,128)(2,1)}), bf16[32,32,128]{2,1,0:T(8,128)(2,1)S(1)}, u32[]{:S(2)}, u32[]{:S(2)}) async-start(bf16[32,32,128]{2,1,0:T(8,128)(2,1)} %bitcast.8), calls=%async_computation | async-start | bytes 524288 | tf_op jit(solution)/shard_map/all_to_all | solution.py:36
  9.7 1.9 %copy-start.6 = (s32[2]{0:T(128)S(1)}, s32[2]{0:T(128)}, u32[]{:S(2)}) copy-start(s32[2]{0:T(128)} %param.11) | copy-start | bytes 28
  9.7 1.9 %copy-start.7 = (s32[32,1]{0,1:T(1,128)S(1)}, s32[32,1]{0,1:T(1,128)}, u32[]{:S(2)}) copy-start(s32[32,1]{0,1:T(1,128)} %param.10) | copy-start | bytes 388
  9.7 11.3 %collective-permute-start = (bf16[2,4,128,128]{3,2,1,0:T(8,128)(2,1)S(1)}, bf16[2,4,128,128]{3,2,1,0:T(8,128)(2,1)S(1)}, u32[]{:S(2)}, u32[]{:S(2)}) collective-permute-start(bf16[2,4,128,128]{3,2,1,0:T(8,128)(2,1)S(1)} %copy-done), channel_id=1, source_target_pairs={{0,4},{4,0},{8,12},{12,8},{16,20},{20,16},{24,28},{28,24},{1,5},{5... | collective-permute-start | bytes 786440 | tf_op jit(solution)/shard_map/ppermute | solution.py:46
  22.4 21.8 %all-to-all-start.1 = ((bf16[32,2,32,128]{3,2,1,0:T(8,128)(2,1)}), bf16[32,2,32,128]{3,2,1,0:T(8,128)(2,1)S(1)}, u32[]{:S(2)}, u32[]{:S(2)}) async-start(bf16[32,2,32,128]{3,2,1,0:T(8,128)(2,1)} %select.3), calls=%async_computation.1 | async-start | bytes 1048576 | tf_op jit(solution)/shard_map/all_to_all | solution.py:36
  27.0 21.1 %copy-start.2 = (bf16[128,4096]{1,0:T(8,128)(2,1)S(1)}, bf16[128,4096]{1,0:T(8,128)(2,1)}, u32[]{:S(2)}) copy-start(bf16[128,4096]{1,0:T(8,128)(2,1)} %q_ref.5) | copy-start | bytes 3145732
  27.0 4.5 %collective-permute-start.1 = (bf16[2,4,128,128]{3,2,1,0:T(8,128)(2,1)S(1)}, bf16[2,4,128,128]{3,2,1,0:T(8,128)(2,1)S(1)}, u32[]{:S(2)}, u32[]{:S(2)}) collective-permute-start(bf16[2,4,128,128]{3,2,1,0:T(8,128)(2,1)S(1)} %broadcast_select_fusion), channel_id=1, source_target_pairs={{4,8},{8,4},{12,16},{16,12},{20,24},{24,20},{28,1},{1,9},{5,28},{9... | collective-permute-start | bytes 786440 | tf_op jit(solution)/shard_map/ppermute | solution.py:68
  31.4 24.7 %copy-start.4 = (bf16[2,4,128,128]{3,2,1,0:T(8,128)(2,1)}, bf16[2,4,128,128]{3,2,1,0:T(8,128)(2,1)S(1)}, u32[]{:S(2)}) copy-start(bf16[2,4,128,128]{3,2,1,0:T(8,128)(2,1)S(1)} %collective-permute-done.1.outer_any.outer_ref) | copy-start | bytes 786436
  44.1 12.0 %copy-start.1 = (bf16[32,2,32,128]{3,2,1,0:T(8,128)(2,1)}, bf16[32,2,32,128]{3,2,1,0:T(8,128)(2,1)S(1)}, u32[]{:S(2)}) copy-start(bf16[32,2,32,128]{3,2,1,0:T(8,128)(2,1)S(1)} %all-to-all-done.1) | copy-start | bytes 1572868
  44.1 3.9 %collective-permute-start.2 = (bf16[2,16,2,32,128]{4,3,2,1,0:T(8,128)(2,1)S(1)}, bf16[2,16,2,32,128]{4,3,2,1,0:T(8,128)(2,1)S(1)}, u32[]{:S(2)}, u32[]{:S(2)}) collective-permute-start(bf16[2,16,2,32,128]{4,3,2,1,0:T(8,128)(2,1)S(1)} %bitcast.11), channel_id=1, source_target_pairs={{0,1},{1,0},{2,3},{3,2},{4,5},{5,4},{6,7},{7,6},{8,9},{9,8},{10,11... | collective-permute-start | bytes 1572872 | tf_op jit(solution)/shard_map/ppermute | solution.py:41
  48.1 8.1 %copy-start.3 = (bf16[2,16,2,32,128]{4,3,2,1,0:T(8,128)(2,1)}, bf16[2,16,2,32,128]{4,3,2,1,0:T(8,128)(2,1)S(1)}, u32[]{:S(2)}) copy-start(bf16[2,16,2,32,128]{4,3,2,1,0:T(8,128)(2,1)S(1)} %collective-permute-done.2.other_ref) | copy-start | bytes 1572868
  56.1 1.6 %collective-permute-start.3 = (bf16[2,4,128,128]{3,2,1,0:T(8,128)(2,1)S(1)}, bf16[2,4,128,128]{3,2,1,0:T(8,128)(2,1)S(1)}, u32[]{:S(2)}, u32[]{:S(2)}) collective-permute-start(bf16[2,4,128,128]{3,2,1,0:T(8,128)(2,1)S(1)} %get-tuple-element.32), channel_id=1, source_target_pairs={{0,1},{1,0},{2,3},{3,2},{4,5},{5,4},{6,7},{7,6},{8,9},{9,8},{10,11... | collective-permute-start | bytes 786440 | tf_op jit(solution)/shard_map/ppermute | solution.py:41
  58.6 24.5 %all-to-all-start.2 = ((bf16[32,2,32,128]{3,2,1,0:T(8,128)(2,1)}), bf16[32,2,32,128]{3,2,1,0:T(8,128)(2,1)S(1)}, u32[]{:S(2)}, u32[]{:S(2)}) async-start(bf16[32,2,32,128]{3,2,1,0:T(8,128)(2,1)} %join.1), calls=%async_computation.2 | async-start | bytes 1048576 | tf_op jit(solution)/shard_map/all_to_all | solution.py:36
  67.2 15.8 %collective-permute-start.4 = (bf16[2,4,128,128]{3,2,1,0:T(8,128)(2,1)S(1)}, bf16[2,4,128,128]{3,2,1,0:T(8,128)(2,1)S(1)}, u32[]{:S(2)}, u32[]{:S(2)}) collective-permute-start(bf16[2,4,128,128]{3,2,1,0:T(8,128)(2,1)S(1)} %get-tuple-element.33), channel_id=1, source_target_pairs={{0,4},{4,0},{8,12},{12,8},{16,20},{20,16},{24,28},{28,24},{1,5},{5... | collective-permute-start | bytes 786440 | tf_op jit(solution)/shard_map/ppermute | solution.py:46
  69.1 14.0 %collective-permute-start.5 = (bf16[2,4,128,128]{3,2,1,0:T(8,128)(2,1)S(1)}, bf16[2,4,128,128]{3,2,1,0:T(8,128)(2,1)S(1)}, u32[]{:S(2)}, u32[]{:S(2)}) collective-permute-start(bf16[2,4,128,128]{3,2,1,0:T(8,128)(2,1)S(1)} %get-tuple-element.34), channel_id=1, source_target_pairs={{4,8},{8,4},{12,16},{16,12},{20,24},{24,20},{28,1},{1,28},{5,9},{9... | collective-permute-start | bytes 786440 | tf_op jit(solution)/shard_map/ppermute | solution.py:55
  84.5 5.7 %copy-start.5 = (bf16[2,4,128,128]{3,2,1,0:T(8,128)(2,1)S(1)}, bf16[2,4,128,128]{3,2,1,0:T(8,128)(2,1)}, u32[]{:S(2)}) copy-start(bf16[2,4,128,128]{3,2,1,0:T(8,128)(2,1)} %copy-done.4) | copy-start | bytes 786436
  84.5 16.3 %all-to-all-start.3 = ((bf16[32,32,128]{2,1,0:T(8,128)(2,1)}), bf16[32,32,128]{2,1,0:T(8,128)(2,1)S(1)}, u32[]{:S(2)}, u32[]{:S(2)}) async-start(bf16[32,32,128]{2,1,0:T(8,128)(2,1)} %combine.1), calls=%async_computation.3 | async-start | bytes 524288 | tf_op jit(solution)/shard_map/all_to_all | solution.py:36

commit v9 on v8

--- a/solution.py
+++ b/solution.py
@@ -19,7 +19,7 @@
 MATES = 2
 SLOTS = 3 + NG + 1
 WIDE = GROUP * BLK
-PART = WIDE
+PART = WIDE // 2
 PIECE = WIDE // 4
 FACTOR = SCALE / math.log(2.0)
 BF16 = jnp.bfloat16

time: 102 us -> 102 us (level)
  transfers between devices with their start and end apart: 10 -> 10, of which waited for: 6 -> 6; matrix products, arithmetic and copies ran while one was open for 0% -> 0% of each run, Pallas kernels for 18% -> 17%
where the time goes in v9:
time: 102 us; the launch traced here: 101 us
  waiting for transfers between devices  39.6 us (39%)
  Pallas kernels  31.3 us (31%)
  starting transfers between devices  29.6 us (29%)
    ppermute x2, waiting for transfers between devices, swap_inner(): return lax.ppermute(value, 'heads', [(h, h ^ 1) for h in range(heads)])  22.7 us
    all_to_all x4, starting transfers between devices, all_to_all(): return lax.all_to_all(value, AXES, split_axis=0, concat_axis=0, tiled=True)  21.6 us
    all_to_all x4, waiting for transfers between devices, all_to_all(): return lax.all_to_all(value, AXES, split_axis=0, concat_axis=0, tiled=True)  14.3 us
    pallas_call x1, Pallas kernels, shards(): call(outputs_kernel, 'outputs', 3, 52, [smem, token, token] + [block] * 3...  9.07 us
    pallas_call x1, Pallas kernels, shards(): call(scores_kernel, 'scores', 3, 50, [smem, vmem, vmem, vmem] + [anywhere...  8.05 us
    pallas_call x1, Pallas kernels, shards(): call(window_kernel, 'window', 1, 53, [smem, token, token, block, block, s...  4.42 us
    ppermute x2, starting transfers between devices, swap_inner(): return lax.ppermute(value, 'heads', [(h, h ^ 1) for h in range(heads)])  3.66 us
    pallas_call x1, Pallas kernels, shards(): call(first_kernel, 'first', 1, 53, [token, token, block, block], [(stat,...  3.65 us
  transfers between devices with their start and end apart: 10, of which 6 were waited for; matrix products, arithmetic and copies ran while one was open for 0% of the time, Pallas kernels for 17%

profile of v9, /device:TPU:0, one launch (start us, length us, event | category | flops | bytes accessed | tf_op | source)
XLA Modules:
  0.0 101.5 jit_solution(16564724179292828724)
XLA Ops:
  0.6 1.7 %pack.1.own_ref = bf16[2,4,128,128]{3,2,1,0:T(8,128)(2,1)} custom-call(bf16[128,512]{1,0:T(8,128)(2,1)} %k_ref.1, bf16[128,512]{1,0:T(8,128)(2,1)} %v_ref.1), custom_call_target="tpu_custom_call" | custom-call | tf_op jit(solution)/shard_map/pack/pallas_call | solution.py:79
  2.3 0.0 copy-start
  2.3 7.3 %all-to-all-start = ((bf16[32,32,128]{2,1,0:T(8,128)(2,1)}), bf16[32,32,128]{2,1,0:T(8,128)(2,1)S(1)}, u32[]{:S(2)}, u32[]{:S(2)}) async-start(bf16[32,32,128]{2,1,0:T(8,128)(2,1)} %bitcast.8), calls=%async_computation | async-start | bytes 524288 | tf_op jit(solution)/shard_map/all_to_all | solution.py:36
  9.7 0.0 copy-done
  9.7 0.0 copy-start.6
  9.7 0.0 copy-start.7
  9.7 1.8 %collective-permute-start = (bf16[2,4,128,128]{3,2,1,0:T(8,128)(2,1)S(1)}, bf16[2,4,128,128]{3,2,1,0:T(8,128)(2,1)S(1)}, u32[]{:S(2)}, u32[]{:S(2)}) collective-permute-start(bf16[2,4,128,128]{3,2,1,0:T(8,128)(2,1)S(1)} %copy-done), channel_id=1, source_target_pairs={{0,4},{4,0},{8,12},{12,8},{16,20},{20,16},{24,28},{28,24},{1,5},{5... | collective-permute-start | bytes 786440 | tf_op jit(solution)/shard_map/ppermute | solution.py:46
  11.5 0.0 copy-done.6
  11.5 0.0 copy-done.7
  11.5 0.1 pad_add_fusion.refs_0_
  11.6 9.3 %collective-permute-done.inner_ref = bf16[2,4,128,128]{3,2,1,0:T(8,128)(2,1)S(1)} collective-permute-done((bf16[2,4,128,128]{3,2,1,0:T(8,128)(2,1)S(1)}, bf16[2,4,128,128]{3,2,1,0:T(8,128)(2,1)S(1)}, u32[]{:S(2)}, u32[]{:S(2)}) %collective-permute-start) | collective-permute-done | bytes 262176 | tf_op jit(solution)/shard_map/ppermute | solution.py:46
  20.9 0.0 all-to-all-done.refs_1_
  21.0 1.4 %select.3 = bf16[32,2,32,128]{3,2,1,0:T(8,128)(2,1)} custom-call(s32[34]{0:T(128)S(1)} %pad_add_fusion.refs_0_, bf16[32,32,128]{2,1,0:T(8,128)(2,1)S(1)} %all-to-all-done.refs_1_), custom_call_target="tpu_custom_call" | custom-call | tf_op jit(solution)/shard_map/select/pallas_call | solution.py:105
  22.4 4.5 %all-to-all-start.1 = ((bf16[32,2,32,128]{3,2,1,0:T(8,128)(2,1)}), bf16[32,2,32,128]{3,2,1,0:T(8,128)(2,1)S(1)}, u32[]{:S(2)}, u32[]{:S(2)}) async-start(bf16[32,2,32,128]{3,2,1,0:T(8,128)(2,1)} %select.3), calls=%async_computation.1 | async-start | bytes 1048576 | tf_op jit(solution)/shard_map/all_to_all | solution.py:36
  27.0 0.0 copy-start.2
  27.0 0.8 collective-permute-start.1
  27.8 3.6 %first.1.first_ref = f32[4,8,1024]{2,1,0:T(8,128)S(1)} custom-call(bf16[128,4096]{1,0:T(8,128)(2,1)} %q_ref.5, bf16[128,4096]{1,0:T(8,128)(2,1)} %do_ref.5, bf16[2,4,128,128]{3,2,1,0:T(8,128)(2,1)S(1)} %copy-done, bf16[2,4,128,128]{3,2,1,0:T(8,128)(2,1)S(1)} %collective-permute-done.inner_ref), custom_call_target="tpu_custom_call" | custom-call | flops 805306368 | bytes 4194304 | tf_op jit(solution)/shard_map/first/pallas_call | solution.py:427
  31.4 0.0 collective-permute-done.1.outer_any.outer_ref
  31.4 0.0 copy-start.4
  31.5 12.7 %all-to-all-done.1 = bf16[32,2,32,128]{3,2,1,0:T(8,128)(2,1)S(1)} async-done(((bf16[32,2,32,128]{3,2,1,0:T(8,128)(2,1)}), bf16[32,2,32,128]{3,2,1,0:T(8,128)(2,1)S(1)}, u32[]{:S(2)}, u32[]{:S(2)}) %all-to-all-start.1) | async-done | bytes 524320 | tf_op jit(solution)/shard_map/all_to_all | solution.py:36
  44.1 0.0 copy-start.1
  44.1 2.4 %collective-permute-start.2 = (bf16[2,16,2,32,128]{4,3,2,1,0:T(8,128)(2,1)S(1)}, bf16[2,16,2,32,128]{4,3,2,1,0:T(8,128)(2,1)S(1)}, u32[]{:S(2)}, u32[]{:S(2)}) collective-permute-start(bf16[2,16,2,32,128]{4,3,2,1,0:T(8,128)(2,1)S(1)} %bitcast.11), channel_id=1, source_target_pairs={{0,1},{1,0},{2,3},{3,2},{4,5},{5,4},{6,7},{7,6},{8,9},{9,8},{10,11... | collective-permute-start | bytes 1572872 | tf_op jit(solution)/shard_map/ppermute | solution.py:41
  46.5 1.5 %collective-permute-done.2.other_ref = bf16[2,16,2,32,128]{4,3,2,1,0:T(8,128)(2,1)S(1)} collective-permute-done((bf16[2,16,2,32,128]{4,3,2,1,0:T(8,128)(2,1)S(1)}, bf16[2,16,2,32,128]{4,3,2,1,0:T(8,128)(2,1)S(1)}, u32[]{:S(2)}, u32[]{:S(2)}) %collective-permute-start.2) | collective-permute-done | bytes 524320 | tf_op jit(solution)/shard_map/ppermute | solution.py:41
  48.1 0.0 copy-start.3
  48.1 0.0 copy-done.2
  48.1 8.0 %scores.1 = (f32[4,8,1024]{2,1,0:T(8,128)S(1)}, f32[2,4,128,128]{3,2,1,0:T(8,128)S(1)}, bf16[2,4,128,128]{3,2,1,0:T(8,128)(2,1)S(1)}, bf16[2,4,128,128]{3,2,1,0:T(8,128)(2,1)S(1)}) custom-call(s32[1]{0:T(128)} %bitcast.edge_ref, bf16[2,16,2,32,128]{4,3,2,1,0:T(8,128)(2,1)S(1)} %bitcast.12, bf16[2,16,2,32,128]{4,3,2,1,0:T(8,128)(2,1)S(1)} %collective-permute-done.2.other_ref, ...), custom_call_target="tpu_custom_call" | custom-call | flops 2415919104 | bytes 4194304 | tf_op jit(solution)/shard_map/scores/pallas_call | solution.py:437
  56.1 0.0 copy-done.4
  56.1 0.0 copy-done.1
  56.1 0.0 copy-done.3
  56.1 0.4 collective-permute-start.3
  56.6 1.2 %collective-permute-done.3 = bf16[2,4,128,128]{3,2,1,0:T(8,128)(2,1)S(1)} collective-permute-done((bf16[2,4,128,128]{3,2,1,0:T(8,128)(2,1)S(1)}, bf16[2,4,128,128]{3,2,1,0:T(8,128)(2,1)S(1)}, u32[]{:S(2)}, u32[]{:S(2)}) %collective-permute-start.3) | collective-permute-done | bytes 262176 | tf_op jit(solution)/shard_map/ppermute | solution.py:41
  57.7 0.9 join.1
  58.6 4.2 %all-to-all-start.2 = ((bf16[32,2,32,128]{3,2,1,0:T(8,128)(2,1)}), bf16[32,2,32,128]{3,2,1,0:T(8,128)(2,1)S(1)}, u32[]{:S(2)}, u32[]{:S(2)}) async-start(bf16[32,2,32,128]{3,2,1,0:T(8,128)(2,1)} %join.1), calls=%async_computation.2 | async-start | bytes 1048576 | tf_op jit(solution)/shard_map/all_to_all | solution.py:36
  62.8 4.4 %window.1 = (bf16[2,4,128,128]{3,2,1,0:T(8,128)(2,1)S(1)}, bf16[2,4,128,128]{3,2,1,0:T(8,128)(2,1)S(1)}) custom-call(s32[1]{0:T(128)} %bitcast.edge_ref, bf16[128,4096]{1,0:T(8,128)(2,1)} %q_ref.5, bf16[128,4096]{1,0:T(8,128)(2,1)} %do_ref.5, bf16[2,4,128,128]{3,2,1,0:T(8,128)(2,1)S(1)} %collective-permute-done.inner_ref, ...), custom_call_target="tpu_custom_call" | custom-call | flops 805306368 | bytes 4194304 | tf_op jit(solution)/shard_map/window/pallas_call | solution.py:456
  67.2 1.8 %collective-permute-start.4 = (bf16[2,4,128,128]{3,2,1,0:T(8,128)(2,1)S(1)}, bf16[2,4,128,128]{3,2,1,0:T(8,128)(2,1)S(1)}, u32[]{:S(2)}, u32[]{:S(2)}) collective-permute-start(bf16[2,4,128,128]{3,2,1,0:T(8,128)(2,1)S(1)} %get-tuple-element.33), channel_id=1, source_target_pairs={{0,4},{4,0},{8,12},{12,8},{16,20},{20,16},{24,28},{28,24},{1,5},{5... | collective-permute-start | bytes 786440 | tf_op jit(solution)/shard_map/ppermute | solution.py:46
  69.0 0.7 collective-permute-start.5
  69.7 13.3 %collective-permute-done.4.from_inner_ref = bf16[2,4,128,128]{3,2,1,0:T(8,128)(2,1)S(1)} collective-permute-done((bf16[2,4,128,128]{3,2,1,0:T(8,128)(2,1)S(1)}, bf16[2,4,128,128]{3,2,1,0:T(8,128)(2,1)S(1)}, u32[]{:S(2)}, u32[]{:S(2)}) %collective-permute-start.4) | collective-permute-done | bytes 262176 | tf_op jit(solution)/shard_map/ppermute | solution.py:46
  83.0 0.0 collective-permute-done.5.from_outer_ref
  83.1 0.0 all-to-all-done.2.refs_1_
  83.1 1.4 %combine.1 = bf16[32,32,128]{2,1,0:T(8,128)(2,1)} custom-call(s32[34]{0:T(128)S(1)} %pad_add_fusion.refs_0_, bf16[32,2,32,128]{3,2,1,0:T(8,128)(2,1)S(1)} %all-to-all-done.2.refs_1_), custom_call_target="tpu_custom_call" | custom-call | tf_op jit(solution)/shard_map/combine/pallas_call | solution.py:140
  84.5 0.0 copy-start.5
  84.5 5.6 %all-to-all-start.3 = ((bf16[32,32,128]{2,1,0:T(8,128)(2,1)}), bf16[32,32,128]{2,1,0:T(8,128)(2,1)S(1)}, u32[]{:S(2)}, u32[]{:S(2)}) async-start(bf16[32,32,128]{2,1,0:T(8,128)(2,1)} %combine.1), calls=%async_computation.3 | async-start | bytes 524288 | tf_op jit(solution)/shard_map/all_to_all | solution.py:36
  90.1 0.0 copy-done.5
  90.1 9.1 %outputs.1 = (bf16[128,4096]{1,0:T(8,128)(2,1)}, bf16[128,4096]{1,0:T(8,128)(2,1)}, f32[2,4,128,128]{3,2,1,0:T(8,128)S(1)}) custom-call(s32[1]{0:T(128)} %bitcast.edge_ref, bf16[128,4096]{1,0:T(8,128)(2,1)} %q_ref.5, bf16[128,4096]{1,0:T(8,128)(2,1)} %do_ref.5, bf16[2,4,128,128]{3,2,1,0:T(8,128)(2,1)S(1)} %copy-done, ...), custom_call_target="tpu_custom_call" | custom-call | flops 2415919104 | bytes 4194304 | tf_op jit(solution)/shard_map/outputs/pallas_call | solution.py:465
  99.2 1.6 %all-to-all-done.3 = bf16[32,32,128]{2,1,0:T(8,128)(2,1)S(1)} async-done(((bf16[32,32,128]{2,1,0:T(8,128)(2,1)}), bf16[32,32,128]{2,1,0:T(8,128)(2,1)S(1)}, u32[]{:S(2)}, u32[]{:S(2)}) %all-to-all-start.3) | async-done | bytes 262176 | tf_op jit(solution)/shard_map/all_to_all | solution.py:36
  100.7 0.7 finish.1
  (1 shorter events, 0.0 us)
Async XLA Ops:
  2.3 7.3 %copy-start = (bf16[2,4,128,128]{3,2,1,0:T(8,128)(2,1)S(1)}, bf16[2,4,128,128]{3,2,1,0:T(8,128)(2,1)}, u32[]{:S(2)}) copy-start(bf16[2,4,128,128]{3,2,1,0:T(8,128)(2,1)} %pack.1.own_ref) | copy-start | bytes 786436
  2.3 18.6 %all-to-all-start = ((bf16[32,32,128]{2,1,0:T(8,128)(2,1)}), bf16[32,32,128]{2,1,0:T(8,128)(2,1)S(1)}, u32[]{:S(2)}, u32[]{:S(2)}) async-start(bf16[32,32,128]{2,1,0:T(8,128)(2,1)} %bitcast.8), calls=%async_computation | async-start | bytes 524288 | tf_op jit(solution)/shard_map/all_to_all | solution.py:36
  9.7 1.9 %copy-start.6 = (s32[2]{0:T(128)S(1)}, s32[2]{0:T(128)}, u32[]{:S(2)}) copy-start(s32[2]{0:T(128)} %param.11) | copy-start | bytes 28
  9.7 1.9 %copy-start.7 = (s32[32,1]{0,1:T(1,128)S(1)}, s32[32,1]{0,1:T(1,128)}, u32[]{:S(2)}) copy-start(s32[32,1]{0,1:T(1,128)} %param.10) | copy-start | bytes 388
  9.7 11.3 %collective-permute-start = (bf16[2,4,128,128]{3,2,1,0:T(8,128)(2,1)S(1)}, bf16[2,4,128,128]{3,2,1,0:T(8,128)(2,1)S(1)}, u32[]{:S(2)}, u32[]{:S(2)}) collective-permute-start(bf16[2,4,128,128]{3,2,1,0:T(8,128)(2,1)S(1)} %copy-done), channel_id=1, source_target_pairs={{0,4},{4,0},{8,12},{12,8},{16,20},{20,16},{24,28},{28,24},{1,5},{5... | collective-permute-start | bytes 786440 | tf_op jit(solution)/shard_map/ppermute | solution.py:46
  22.4 21.8 %all-to-all-start.1 = ((bf16[32,2,32,128]{3,2,1,0:T(8,128)(2,1)}), bf16[32,2,32,128]{3,2,1,0:T(8,128)(2,1)S(1)}, u32[]{:S(2)}, u32[]{:S(2)}) async-start(bf16[32,2,32,128]{3,2,1,0:T(8,128)(2,1)} %select.3), calls=%async_computation.1 | async-start | bytes 1048576 | tf_op jit(solution)/shard_map/all_to_all | solution.py:36
  27.0 21.1 %copy-start.2 = (bf16[128,4096]{1,0:T(8,128)(2,1)S(1)}, bf16[128,4096]{1,0:T(8,128)(2,1)}, u32[]{:S(2)}) copy-start(bf16[128,4096]{1,0:T(8,128)(2,1)} %q_ref.5) | copy-start | bytes 3145732
  27.0 4.5 %collective-permute-start.1 = (bf16[2,4,128,128]{3,2,1,0:T(8,128)(2,1)S(1)}, bf16[2,4,128,128]{3,2,1,0:T(8,128)(2,1)S(1)}, u32[]{:S(2)}, u32[]{:S(2)}) collective-permute-start(bf16[2,4,128,128]{3,2,1,0:T(8,128)(2,1)S(1)} %broadcast_select_fusion), channel_id=1, source_target_pairs={{4,8},{8,4},{12,16},{16,12},{20,24},{24,20},{28,1},{1,9},{5,28},{9... | collective-permute-start | bytes 786440 | tf_op jit(solution)/shard_map/ppermute | solution.py:68
  31.4 24.7 %copy-start.4 = (bf16[2,4,128,128]{3,2,1,0:T(8,128)(2,1)}, bf16[2,4,128,128]{3,2,1,0:T(8,128)(2,1)S(1)}, u32[]{:S(2)}) copy-start(bf16[2,4,128,128]{3,2,1,0:T(8,128)(2,1)S(1)} %collective-permute-done.1.outer_any.outer_ref) | copy-start | bytes 786436
  44.1 12.0 %copy-start.1 = (bf16[32,2,32,128]{3,2,1,0:T(8,128)(2,1)}, bf16[32,2,32,128]{3,2,1,0:T(8,128)(2,1)S(1)}, u32[]{:S(2)}) copy-start(bf16[32,2,32,128]{3,2,1,0:T(8,128)(2,1)S(1)} %all-to-all-done.1) | copy-start | bytes 1572868
  44.1 3.9 %collective-permute-start.2 = (bf16[2,16,2,32,128]{4,3,2,1,0:T(8,128)(2,1)S(1)}, bf16[2,16,2,32,128]{4,3,2,1,0:T(8,128)(2,1)S(1)}, u32[]{:S(2)}, u32[]{:S(2)}) collective-permute-start(bf16[2,16,2,32,128]{4,3,2,1,0:T(8,128)(2,1)S(1)} %bitcast.11), channel_id=1, source_target_pairs={{0,1},{1,0},{2,3},{3,2},{4,5},{5,4},{6,7},{7,6},{8,9},{9,8},{10,11... | collective-permute-start | bytes 1572872 | tf_op jit(solution)/shard_map/ppermute | solution.py:41
  48.1 8.1 %copy-start.3 = (bf16[2,16,2,32,128]{4,3,2,1,0:T(8,128)(2,1)}, bf16[2,16,2,32,128]{4,3,2,1,0:T(8,128)(2,1)S(1)}, u32[]{:S(2)}) copy-start(bf16[2,16,2,32,128]{4,3,2,1,0:T(8,128)(2,1)S(1)} %collective-permute-done.2.other_ref) | copy-start | bytes 1572868
  56.1 1.6 %collective-permute-start.3 = (bf16[2,4,128,128]{3,2,1,0:T(8,128)(2,1)S(1)}, bf16[2,4,128,128]{3,2,1,0:T(8,128)(2,1)S(1)}, u32[]{:S(2)}, u32[]{:S(2)}) collective-permute-start(bf16[2,4,128,128]{3,2,1,0:T(8,128)(2,1)S(1)} %get-tuple-element.32), channel_id=1, source_target_pairs={{0,1},{1,0},{2,3},{3,2},{4,5},{5,4},{6,7},{7,6},{8,9},{9,8},{10,11... | collective-permute-start | bytes 786440 | tf_op jit(solution)/shard_map/ppermute | solution.py:41
  58.6 24.4 %all-to-all-start.2 = ((bf16[32,2,32,128]{3,2,1,0:T(8,128)(2,1)}), bf16[32,2,32,128]{3,2,1,0:T(8,128)(2,1)S(1)}, u32[]{:S(2)}, u32[]{:S(2)}) async-start(bf16[32,2,32,128]{3,2,1,0:T(8,128)(2,1)} %join.1), calls=%async_computation.2 | async-start | bytes 1048576 | tf_op jit(solution)/shard_map/all_to_all | solution.py:36
  67.2 15.8 %collective-permute-start.4 = (bf16[2,4,128,128]{3,2,1,0:T(8,128)(2,1)S(1)}, bf16[2,4,128,128]{3,2,1,0:T(8,128)(2,1)S(1)}, u32[]{:S(2)}, u32[]{:S(2)}) collective-permute-start(bf16[2,4,128,128]{3,2,1,0:T(8,128)(2,1)S(1)} %get-tuple-element.33), channel_id=1, source_target_pairs={{0,4},{4,0},{8,12},{12,8},{16,20},{20,16},{24,28},{28,24},{1,5},{5... | collective-permute-start | bytes 786440 | tf_op jit(solution)/shard_map/ppermute | solution.py:46
  69.0 14.0 %collective-permute-start.5 = (bf16[2,4,128,128]{3,2,1,0:T(8,128)(2,1)S(1)}, bf16[2,4,128,128]{3,2,1,0:T(8,128)(2,1)S(1)}, u32[]{:S(2)}, u32[]{:S(2)}) collective-permute-start(bf16[2,4,128,128]{3,2,1,0:T(8,128)(2,1)S(1)} %get-tuple-element.34), channel_id=1, source_target_pairs={{4,8},{8,4},{12,16},{16,12},{20,24},{24,20},{28,1},{1,28},{5,9},{9... | collective-permute-start | bytes 786440 | tf_op jit(solution)/shard_map/ppermute | solution.py:55
  84.5 5.6 %copy-start.5 = (bf16[2,4,128,128]{3,2,1,0:T(8,128)(2,1)S(1)}, bf16[2,4,128,128]{3,2,1,0:T(8,128)(2,1)}, u32[]{:S(2)}) copy-start(bf16[2,4,128,128]{3,2,1,0:T(8,128)(2,1)} %copy-done.4) | copy-start | bytes 786436
  84.5 16.3 %all-to-all-start.3 = ((bf16[32,32,128]{2,1,0:T(8,128)(2,1)}), bf16[32,32,128]{2,1,0:T(8,128)(2,1)S(1)}, u32[]{:S(2)}, u32[]{:S(2)}) async-start(bf16[32,32,128]{2,1,0:T(8,128)(2,1)} %combine.1), calls=%async_computation.3 | async-start | bytes 524288 | tf_op jit(solution)/shard_map/all_to_all | solution.py:36
